TPU v7x, 256 devices: a whole 4x4x8 slice. The times are simulated.
256 devices in a mesh: frame: 16 (over z, core), tok: 16 (over x, y).
Axes of the slice: x: 4, y: 4, z: 8, core: 2. Of those that a mesh axis runs over, the one named last changes fastest.
Arguments:
- stream: bfloat16 [16, 4096, 1152], P('frame', 'tok'), may hold values from -20 to 20
- queries: bfloat16 [16, 4096, 1152], P('frame', 'tok'), may hold values from -200 to 200
- key_vectors: bfloat16 [16, 4096, 1152], P('frame', 'tok'), may hold values from -6 to 6
- value_vectors: bfloat16 [16, 4096, 1152], P('frame', 'tok'), may hold values from -6 to 6
- modulation: float32 [16, 4, 1152], P('frame'), may hold values from -4 to 4
- output_weight: bfloat16 [1152, 1152], replicated, may hold values from -0.1875 to 0.1875
- output_bias: float32 [1152], replicated, may hold values from -3 to 3
- router_weight: bfloat16 [1152, 16], replicated, may hold values from -0.1875 to 0.1875
- expand_weight: bfloat16 [16, 1152, 4608], P('frame', None, 'tok'), may hold values from -0.1875 to 0.1875
- expand_bias: float32 [16, 4608], P('frame', 'tok'), may hold values from -3 to 3
- reduce_weight: bfloat16 [16, 4608, 1152], P('frame', 'tok'), may hold values from -0.09375 to 0.09375
- reduce_bias: float32 [16, 1152], P('frame'), may hold values from -3 to 3
- counts: int32 [16, 16], P(None, 'frame'), may hold values from 1 to 48, 256 in all within a row
- picked_rows: int32 [16, 16, 48], P(None, 'frame'), may hold values from 0 to 4095, as said below
Outputs:
- layer_out: bfloat16 [16, 4096, 1152], P('frame', 'tok')
Inputs may be any that keep to these rules, and one draw needn't show every extreme that they name: counts[e, g] slots of block (e, g) are used; the counts of one expert sum to 256. The entries of one block picked_rows[e, g, :] are distinct positions among the 4096 tokens of frame g; slots at or beyond counts[e, g] are unused.
All inputs are finite; a program needn't handle non-finite values.
Results may differ from a plain program's by a relative error of at most 0.0055.
Values may be sent and summed in bfloat16 or wider, within the bound.
No kernel may reach another device: no remote copies, remote signals or barrier semaphores. Data moves between devices by JAX's collectives and lax.ppermute only.
A program may use at most 64 MiB of HBM per device.

v0:
```python
import math

import jax
import jax.numpy as jnp
from jax import lax
from jax.sharding import PartitionSpec as P

H = 16
HD = 72


def layer_norm(values):
    mean_val = jnp.mean(values, axis=-1, keepdims=True)
    centred = values - mean_val
    variance = jnp.mean(centred * centred, axis=-1, keepdims=True)
    return centred * lax.rsqrt(variance + 1e-06)


def head_attention(operands):
    head_queries, head_keys, head_values = operands
    length = head_queries.shape[1]
    block_rows = min(512, length)
    score_scale = 1.0 / math.sqrt(HD)

    def one_block(first_row):
        query_block = lax.dynamic_slice_in_dim(head_queries, first_row, block_rows, 1)
        scores = (
            lax.dot_general(
                query_block, head_keys, (((0,), (0,)), ((), ())), preferred_element_type=jnp.float32
            )
            * score_scale
        )
        scores = scores - jnp.max(scores, axis=1, keepdims=True)
        exponent = jnp.exp(scores)
        weights = (exponent / jnp.sum(exponent, axis=1, keepdims=True)).astype(jnp.bfloat16)
        return lax.dot_general(
            head_values, weights, (((1,), (1,)), ((), ())), preferred_element_type=jnp.float32
        ).astype(jnp.bfloat16)

    starts = jnp.arange(length // block_rows, dtype=jnp.int32) * block_rows
    blocks = lax.map(one_block, starts)
    return blocks.transpose(1, 0, 2).reshape(head_queries.shape[0], length)


def attend_items(pieces):
    outputs = lax.map(head_attention, (pieces[0][0], pieces[1][0], pieces[2][0]))
    return outputs[None]


def per_device(
    stream,
    queries,
    key_vectors,
    value_vectors,
    modulation,
    output_weight,
    output_bias,
    router_weight,
    expand_weight,
    expand_bias,
    reduce_weight,
    reduce_bias,
    counts,
    picked_rows,
):
    tok_groups = lax.axis_size("tok")
    tok_local = stream.shape[1]
    model_width = stream.shape[2]
    heads_local = H // tok_groups

    def to_heads(tensor):
        return tensor[0].reshape(tok_local, tok_groups, heads_local, HD).transpose(1, 2, 3, 0)

    attended = attend_items(
        (
            lax.all_to_all(to_heads(queries), "tok", split_axis=0, concat_axis=3, tiled=True),
            lax.all_to_all(to_heads(key_vectors), "tok", split_axis=0, concat_axis=3, tiled=True),
            lax.all_to_all(to_heads(value_vectors), "tok", split_axis=0, concat_axis=3, tiled=True),
        )
    )
    returned = lax.all_to_all(attended, "tok", split_axis=3, concat_axis=0, tiled=True)
    attended_rows = returned.transpose(3, 0, 1, 2).reshape(tok_local, model_width)
    projected = (
        jnp.dot(attended_rows, output_weight, preferred_element_type=jnp.float32) + output_bias
    )
    shares = modulation[0]
    residual = (stream[0].astype(jnp.float32) + shares[0] * projected).astype(jnp.bfloat16)
    normed = (layer_norm(residual.astype(jnp.float32)) * (1.0 + shares[2]) + shares[1]).astype(
        jnp.bfloat16
    )
    gate_values = jax.nn.sigmoid(jnp.dot(normed, router_weight, preferred_element_type=jnp.float32))
    slot_count = picked_rows.shape[2]
    local_pos = picked_rows[:, 0, :] - lax.axis_index("tok") * tok_local
    in_use = jnp.arange(slot_count, dtype=jnp.int32)[None, :] < counts
    on_shard = in_use & (local_pos >= 0) & (local_pos < tok_local)
    safe_pos = jnp.clip(local_pos, 0, tok_local - 1)
    chosen = jnp.take(normed, safe_pos, axis=0)
    chosen = jnp.where(on_shard[:, :, None], chosen, jnp.zeros_like(chosen))
    moved = lax.all_to_all(chosen, "frame", split_axis=0, concat_axis=1, tiled=True)
    expert_rows = lax.psum(moved.astype(jnp.float32).astype(jnp.bfloat16), "tok")
    hidden = jax.nn.gelu(
        jnp.einsum("erd,edf->erf", expert_rows, expand_weight, preferred_element_type=jnp.float32)
        + expand_bias[:, None, :],
        approximate=True,
    ).astype(jnp.bfloat16)
    partial_out = jnp.einsum(
        "erf,efd->erd", hidden, reduce_weight, preferred_element_type=jnp.float32
    )
    summed = lax.psum(partial_out.astype(jnp.bfloat16), "tok").astype(jnp.float32)
    expert_out = (summed + reduce_bias[:, None, :]).astype(jnp.bfloat16)
    returned_rows = lax.all_to_all(expert_out, "frame", split_axis=1, concat_axis=0, tiled=True)
    mix_weight = jnp.take_along_axis(gate_values.T, safe_pos, axis=1)
    mix_weight = jnp.where(on_shard, mix_weight, jnp.zeros_like(mix_weight)).astype(jnp.bfloat16)
    targets = jnp.arange(tok_local, dtype=jnp.int32)
    matches = (safe_pos.reshape(-1)[None, :] == targets[:, None]) & on_shard.reshape(-1)[None, :]
    scatter_table = jnp.where(matches, mix_weight.reshape(-1)[None, :], jnp.zeros((), jnp.bfloat16))
    expert_mix = jnp.dot(
        scatter_table, returned_rows.reshape(-1, model_width), preferred_element_type=jnp.float32
    )
    layer_out = (residual.astype(jnp.float32) + shares[3] * expert_mix).astype(jnp.bfloat16)
    return layer_out[None]


def solution(mesh):
    return jax.shard_map(
        per_device,
        mesh=mesh,
        in_specs=(
            P("frame", "tok", None),
            P("frame", "tok", None),
            P("frame", "tok", None),
            P("frame", "tok", None),
            P("frame", None, None),
            P(),
            P(),
            P(),
            P("frame", None, "tok"),
            P("frame", "tok"),
            P("frame", "tok", None),
            P("frame", None),
            P(None, "frame"),
            P(None, "frame", None),
        ),
        out_specs=P("frame", "tok", None),
        check_vma=False,
    )
```

profile of v0, /device:TPU:1, one launch (start us, length us, event | category | flops | bytes accessed | tf_op | source)
XLA Modules:
  0.0 551.0 jit_solution(5295147345059921114)
XLA Ops:
  6.5 2.3 copy.62
  8.8 7.6 %all-to-all-start = ((bf16[16,1,72,256]{3,2,1,0:T(8,128)(2,1)}), bf16[16,1,72,256]{3,2,1,0:T(8,128)(2,1)S(1)}, u32[]{:S(2)}, u32[]{:S(2)}) async-start(bf16[16,1,72,256]{3,2,1,0:T(8,128)(2,1)} %bitcast.139), calls=%async_computation | async-start | bytes 1179648 | tf_op jit(solution)/shard_map/all_to_all | solution.py:76
  16.4 2.1 copy.65
  18.5 8.9 %all-to-all-done = bf16[16,1,72,256]{3,2,1,0:T(8,128)(2,1)S(1)} async-done(((bf16[16,1,72,256]{3,2,1,0:T(8,128)(2,1)}), bf16[16,1,72,256]{3,2,1,0:T(8,128)(2,1)S(1)}, u32[]{:S(2)}, u32[]{:S(2)}) %all-to-all-start) | async-done | bytes 589856 | tf_op jit(solution)/shard_map/all_to_all | solution.py:76
  27.4 4.4 all-to-all-start.1
  31.8 2.1 copy.68
  33.9 7.3 %all-to-all-done.1 = bf16[16,1,72,256]{3,2,1,0:T(8,128)(2,1)} async-done(((bf16[16,1,72,256]{3,2,1,0:T(8,128)(2,1)}), bf16[16,1,72,256]{3,2,1,0:T(8,128)(2,1)}, u32[]{:S(2)}, u32[]{:S(2)}) %all-to-all-start.1) | async-done | bytes 589856 | tf_op jit(solution)/shard_map/all_to_all | solution.py:77
  41.2 4.7 all-to-all-start.2
  48.1 7.2 %all-to-all-done.2 = bf16[16,1,72,256]{3,2,1,0:T(8,128)(2,1)} async-done(((bf16[16,1,72,256]{3,2,1,0:T(8,128)(2,1)}), bf16[16,1,72,256]{3,2,1,0:T(8,128)(2,1)}, u32[]{:S(2)}, u32[]{:S(2)}) %all-to-all-start.2) | async-done | bytes 589856 | tf_op jit(solution)/shard_map/all_to_all | solution.py:78
  55.4 1.9 copy.84
  57.3 74.4 %while.17 = (s32[]{:T(128)}, bf16[8,72,512]{2,1,0:T(8,128)(2,1)}, s32[8]{0:T(128)S(1)}, bf16[72,4096]{1,0:T(8,128)(2,1)}, bf16[72,4096]{1,0:T(8,128)(2,1)S(1)}, ...) while((s32[]{:T(128)}, bf16[8,72,512]{2,1,0:T(8,128)(2,1)}, s32[8]{0:T(128)S(1)}, ...), condition=%wide.region_3.0_spmd, body=%wide.region_0.3_spmd.sunk | while | flops 622889984 | bytes 28862648 | solution.py:41
  59.8 2.4 multiply_reduce_fusion.3
  63.7 2.9 fusion.68
  69.1 2.3 multiply_reduce_fusion.3
  73.0 2.9 fusion.68
  78.4 2.3 multiply_reduce_fusion.3
  82.3 2.9 fusion.68
  87.7 2.4 multiply_reduce_fusion.3
  91.6 2.9 fusion.68
  97.0 2.3 multiply_reduce_fusion.3
  100.9 2.9 fusion.68
  106.3 2.3 multiply_reduce_fusion.3
  110.2 2.9 fusion.68
  115.6 2.3 multiply_reduce_fusion.3
  119.5 2.9 fusion.68
  124.9 2.3 multiply_reduce_fusion.3
  128.8 2.9 fusion.68
  131.7 2.2 copy.78
  133.9 6.9 %reshape.245 = bf16[1,1,72,4096]{2,1,0,3:T(2,128)(2,1)} reshape(bf16[72,8,512]{0,2,1:T(8,128)(2,1)} %copy.78) | data formatting | bytes 1179648 | tf_op jit(solution)/shard_map/broadcast_in_dim | solution.py:47
  141.3 24.4 %reduce.12 = bf16[4096,72]{1,0:T(8,128)(2,1)} reduce(bf16[4096,1,1,72]{3,2,1,0:T(2,128)(2,1)} %bitcast.131, bf16[]{:T(256)} %broadcast.275), dimensions={1,2}, to_apply=%bitcast.108.reduce_sub_computation | reduce | bytes 1179650
  165.8 4.3 reshape.253
  170.1 3.6 all-to-all-start.3
  173.9 9.1 %all-to-all-done.3 = bf16[16,2,9216]{2,1,0:T(2,128)(2,1)S(1)} async-done(((bf16[16,2,9216]{2,1,0:T(2,128)(2,1)}), bf16[16,2,9216]{2,1,0:T(2,128)(2,1)S(1)}, u32[]{:S(2)}, u32[]{:S(2)}) %all-to-all-start.3) | async-done | bytes 589856 | tf_op jit(solution)/shard_map/all_to_all | solution.py:81
  183.0 5.1 reshape.254
  188.1 4.6 copy.73
  196.2 3.7 gather_fusion
  201.8 57.8 %all_to_all.84 = bf16[16,48,1152]{2,1,0:T(8,128)(2,1)} all-to-all(bf16[16,48,1152]{2,1,0:T(8,128)(2,1)S(1)} %select_select_fusion), channel_id=1, replica_groups=mesh['frame'=16,'tok'=16] {'frame'}, dimensions={0} | all-to-all | bytes 3538944 | tf_op jit(solution)/shard_map/all_to_all | solution.py:99
  260.3 90.5 %all-reduce.3.cloned.1.call-done = bf16[768,1152]{1,0:T(8,128)(2,1)} async-done(((bf16[768,1152]{1,0:T(8,128)(2,1)}), bf16[768,1152]{1,0:T(8,128)(2,1)}) %all-reduce.3.cloned.1.call-update) | async-done | bytes 1769488 | tf_op jit(solution)/shard_map/psum | solution.py:100
  350.8 5.3 fusion.9
  356.8 98.2 %all-reduce.5.cloned.1.call-done = bf16[1,768,1152]{2,1,0:T(8,128)(2,1)} async-done(((bf16[1,768,1152]{2,1,0:T(8,128)(2,1)}), bf16[1,768,1152]{2,1,0:T(8,128)(2,1)}) %all-reduce.5.cloned.1.call-update) | async-done | bytes 1769488 | tf_op jit(solution)/shard_map/psum | solution.py:109
  456.7 4.5 copy.95
  461.2 12.6 %reduce.13 = bf16[768,1152]{1,0:T(8,128)(2,1)} reduce(bf16[768,1,1152]{2,1,0:T(2,128)(2,1)} %bitcast.130, bf16[]{:T(256)} %broadcast.275), dimensions={1}, to_apply=%bitcast.120.reduce_sub_computation | reduce | bytes 3538946
  473.8 4.7 reshape.255
  478.5 9.2 %all-to-all-start.5 = ((bf16[16,2,27648]{2,1,0:T(2,128)(2,1)}), bf16[16,2,27648]{2,1,0:T(2,128)(2,1)}, u32[]{:S(2)}, u32[]{:S(2)}) async-start(bf16[16,2,27648]{2,1,0:T(2,128)(2,1)} %reshape.255), calls=%async_computation.5 | async-start | bytes 3538944 | tf_op jit(solution)/shard_map/all_to_all | solution.py:111
  488.4 6.7 %gather_fusion.1 = bf16[768]{0:T(1024)(128)(2,1)S(1)} fusion(bf16[16,256]{1,0:T(8,128)(2,1)S(1)} %fusion.22, s32[768]{0:T(1024)S(1)} %reshape.237), kind=kCustom, calls=%fused_computation.1 | custom fusion | bytes 9216 | tf_op jit(solution)/shard_map/jit(take_along_axis)/gather | solution.py:112
  495.2 35.0 %all-to-all-done.5 = bf16[16,2,27648]{2,1,0:T(2,128)(2,1)} async-done(((bf16[16,2,27648]{2,1,0:T(2,128)(2,1)}), bf16[16,2,27648]{2,1,0:T(2,128)(2,1)}, u32[]{:S(2)}, u32[]{:S(2)}) %all-to-all-start.5) | async-done | bytes 1769504 | tf_op jit(solution)/shard_map/all_to_all | solution.py:111
  530.2 10.0 %reshape.256 = bf16[768,1,1152]{2,1,0:T(2,128)(2,1)} reshape(bf16[16,2,27648]{2,1,0:T(2,128)(2,1)} %all-to-all-done.5) | data formatting | bytes 3538944
  540.2 3.9 fusion.16
  (87 shorter events, 29.3 us)
Async XLA Ops:
  6.5 186.5 %copy-start = (bf16[1152,1152]{1,0:T(8,128)(2,1)S(1)}, bf16[1152,1152]{1,0:T(8,128)(2,1)}, u32[]{:S(2)}) copy-start(bf16[1152,1152]{1,0:T(8,128)(2,1)} %param.21) | copy-start | bytes 7962628
  8.8 18.6 %all-to-all-start = ((bf16[16,1,72,256]{3,2,1,0:T(8,128)(2,1)}), bf16[16,1,72,256]{3,2,1,0:T(8,128)(2,1)S(1)}, u32[]{:S(2)}, u32[]{:S(2)}) async-start(bf16[16,1,72,256]{3,2,1,0:T(8,128)(2,1)} %bitcast.139), calls=%async_computation | async-start | bytes 1179648 | tf_op jit(solution)/shard_map/all_to_all | solution.py:76
  27.4 18.5 %copy-start.5 = (s32[16,1,48]{2,1,0:T(1,128)S(1)}, s32[16,1,48]{2,1,0:T(1,128)}, u32[]{:S(2)}) copy-start(s32[16,1,48]{2,1,0:T(1,128)} %param.29) | copy-start | bytes 9220
  27.4 18.7 %copy-start.4 = (f32[1,4,1152]{2,1,0:T(4,128)S(1)}, f32[1,4,1152]{2,1,0:T(4,128)}, u32[]{:S(2)}) copy-start(f32[1,4,1152]{2,1,0:T(4,128)} %param.20) | copy-start | bytes 55300
  27.4 13.8 %all-to-all-start.1 = ((bf16[16,1,72,256]{3,2,1,0:T(8,128)(2,1)}), bf16[16,1,72,256]{3,2,1,0:T(8,128)(2,1)}, u32[]{:S(2)}, u32[]{:S(2)}) async-start(bf16[16,1,72,256]{3,2,1,0:T(8,128)(2,1)} %bitcast.138), calls=%async_computation.1 | async-start | bytes 1179648 | tf_op jit(solution)/shard_map/all_to_all | solution.py:77
  41.2 14.1 %all-to-all-start.2 = ((bf16[16,1,72,256]{3,2,1,0:T(8,128)(2,1)}), bf16[16,1,72,256]{3,2,1,0:T(8,128)(2,1)}, u32[]{:S(2)}, u32[]{:S(2)}) async-start(bf16[16,1,72,256]{3,2,1,0:T(8,128)(2,1)} %bitcast.137), calls=%async_computation.2 | async-start | bytes 1179648 | tf_op jit(solution)/shard_map/all_to_all | solution.py:78
  62.2 1.5 copy-start.2
  71.5 1.5 copy-start.2
  80.8 1.5 copy-start.2
  90.1 1.5 copy-start.2
  99.4 1.5 copy-start.2
  108.7 1.5 copy-start.2
  117.9 1.5 copy-start.2
  127.2 1.5 copy-start.2
  165.8 8.0 %copy-start.8 = (s32[16,1]{0,1:T(1,128)S(1)}, s32[16,1]{0,1:T(1,128)}, u32[]{:S(2)}) copy-start(s32[16,1]{0,1:T(1,128)} %param.28) | copy-start | bytes 196
  170.1 12.9 %all-to-all-start.3 = ((bf16[16,2,9216]{2,1,0:T(2,128)(2,1)}), bf16[16,2,9216]{2,1,0:T(2,128)(2,1)S(1)}, u32[]{:S(2)}, u32[]{:S(2)}) async-start(bf16[16,2,9216]{2,1,0:T(2,128)(2,1)} %reshape.253), calls=%async_computation.3 | async-start | bytes 1179648 | tf_op jit(solution)/shard_map/all_to_all | solution.py:81
  173.7 177.1 %all-reduce.3.cloned.1.call-start = ((), (), s32[]{:S(2)}) async-start(), calls=%async_computation.6 | async-start | bytes 3538944 | tf_op jit(solution)/shard_map/psum | solution.py:100
  192.7 1.1 copy-start.9
  192.7 1.1 copy-start.10
  194.9 1.0 copy-start.1
  259.6 0.7 copy-start.7
  259.6 195.4 %all-reduce.5.cloned.1.call-start = ((), (), s32[]{:S(2)}) async-start(), calls=%async_computation.7 | async-start | bytes 3538944 | tf_op jit(solution)/shard_map/psum | solution.py:109
  356.1 0.7 copy-start.6
  478.5 9.7 %copy-start.3 = (bf16[1152,16]{0,1:T(8,128)(2,1)S(1)}, bf16[1152,16]{0,1:T(8,128)(2,1)}, u32[]{:S(2)}) copy-start(bf16[1152,16]{0,1:T(8,128)(2,1)} %param.23) | copy-start | bytes 110596
  478.5 51.7 %all-to-all-start.5 = ((bf16[16,2,27648]{2,1,0:T(2,128)(2,1)}), bf16[16,2,27648]{2,1,0:T(2,128)(2,1)}, u32[]{:S(2)}, u32[]{:S(2)}) async-start(bf16[16,2,27648]{2,1,0:T(2,128)(2,1)} %reshape.255), calls=%async_computation.5 | async-start | bytes 3538944 | tf_op jit(solution)/shard_map/all_to_all | solution.py:111
Sparse Core Ops, SparseCore 0:
  259.7 91.0 all-reduce.2
  356.2 98.6 all-reduce.4
where the time goes:
time: 553 us; the launch traced here: 551 us
  waiting for transfers between devices  256 us (46%)
  local copies, waits for them, and re-layouts  72.2 us (13%)
  blocking collectives  57.8 us (10%)
  other arithmetic  53.5 us (10%)
  matrix products  52.8 us (10%)
  starting transfers between devices  29.8 us (5%)
  loops' own time  15 us (3%)
  between operations  13.7 us (2%)
    psum x1, waiting for transfers between devices, per_device(): lax.psum(partial_out.astype(jnp.bfloat16), 'tok').astype(jnp.float32)  98.2 us
    psum x1, waiting for transfers between devices, per_device(): lax.psum(moved.astype(jnp.float32).astype(jnp.bfloat16), 'tok')  90.5 us
    all_to_all x1, blocking collectives, per_device(): lax.all_to_all(chosen, 'frame', split_axis=0, concat_axis=1, tiled=True)  57.8 us
    unnamed x32, local copies, waits for them, and re-layouts  37.8 us
    unnamed x4, other arithmetic  37 us
    all_to_all x1, waiting for transfers between devices, per_device(): lax.all_to_all(expert_out, 'frame', split_axis=1, concat_axis=0, tiled=True)  35 us
    dot_general x8, matrix products, one_block(): lax.dot_general(head_values, weights, (((1,), (1,)), ((), ())), preferred...  23.4 us
    dot_general x8, matrix products, one_block(): lax.dot_general(query_block, head_keys, (((0,), (0,)), ((), ())), preferr...  18.8 us
  transfers between devices with their start and end apart: 7, of which 7 were waited for; matrix products, arithmetic and copies ran while one was open for 3% of the time, Pallas kernels for 0%

commit v1 on v0

v1 whole, which is shorter than its diff:
```python
import functools
import math

import jax
import jax.numpy as jnp
from jax import lax
from jax.experimental import pallas as pl
from jax.experimental.pallas import tpu as pltpu
from jax.sharding import PartitionSpec as P

H = 16
HD = 72
D = 1152
TL = 256
F32 = jnp.float32
BF16 = jnp.bfloat16
EXP_SCALE = math.log2(math.e) / math.sqrt(HD)
PARAMS = pltpu.CompilerParams(vmem_limit_bytes=56 * 1024 * 1024)


def nt(left, right):
    return lax.dot_general(left, right, (((1,), (1,)), ((), ())), preferred_element_type=F32)


def nn(left, right):
    return jnp.dot(left, right, preferred_element_type=F32)


def eye(size):
    rows = lax.broadcasted_iota(jnp.int32, (size, size), 0)
    cols = lax.broadcasted_iota(jnp.int32, (size, size), 1)
    return (rows == cols).astype(F32).astype(BF16)


def one_hot(index, width, first=0):
    lanes = lax.broadcasted_iota(jnp.int32, (index.shape[0], width), 1)
    return (lanes == index - first).astype(F32).astype(BF16)


TILES = [(w * 256, min(256, D - w * 256)) for w in range(5)]


def split_kernel(k_ref, v_ref, q_ref, s_ref, out_ref):
    for i, ref in enumerate((k_ref, v_ref, q_ref, s_ref)):
        for start, size in TILES:
            turned = nt(eye(size), ref[:, start : start + size])
            for h in range(H):
                low, high = max(h * HD, start), min((h + 1) * HD, start + size)
                if low < high:
                    out_ref[h, i * HD + low - h * HD : i * HD + high - h * HD, :] = turned[
                        low - start : high - start
                    ].astype(BF16)


def fill_values(r_ref, v_ref):
    for j in range(16):
        v_ref[j, :HD, :] = r_ref[j, HD : 2 * HD, :]
        v_ref[j, HD:, :] = jnp.ones((8, TL), BF16)


def attend(q, r_ref, v_ref, s_ref):
    top = None
    for j in range(16):
        scores = nn(q, r_ref[j, :HD, :])
        s_ref[:, j * TL : (j + 1) * TL] = scores
        part = jnp.maximum(scores[:, :128], scores[:, 128:])
        top = part if top is None else jnp.maximum(top, part)
    top = jnp.max(top, axis=1, keepdims=True)
    total = None
    for j in range(16):
        weights = jnp.exp2((s_ref[:, j * TL : (j + 1) * TL] - top) * EXP_SCALE).astype(BF16)
        part = nt(weights, v_ref[j])
        total = part if total is None else total + part
    return total[:, :HD] / total[:, HD : HD + 1]


def picked_kernel(idx_ref, r_ref, out_ref, v_ref, s_ref):
    @pl.when(pl.program_id(0) == 0)
    def _():
        fill_values(r_ref, v_ref)

    index = idx_ref[...]
    rows = None
    for j in range(16):
        part = nt(one_hot(index, TL, j * TL), r_ref[j, 2 * HD :, :])
        rows = part if rows is None else rows + part
    out_ref[:, :HD] = attend(rows[:, :HD].astype(BF16), r_ref, v_ref, s_ref).astype(BF16)
    out_ref[:, HD:] = rows[:, HD:].astype(BF16)


def main_kernel(first, r_ref, out_ref, v_ref, s_ref):
    @pl.when(pl.program_id(0) == 0)
    def _():
        fill_values(r_ref, v_ref)

    q = nt(eye(TL), r_ref[first + pl.program_id(0), 2 * HD : 3 * HD, :]).astype(BF16)
    out = attend(q, r_ref, v_ref, s_ref).astype(BF16)
    out_ref[0] = nt(eye(HD), out).astype(BF16)


def attention(kernel, steps, ins, in_specs, out_shape, out_spec, name):
    whole = pl.BlockSpec((16, 4 * HD, TL), lambda i: (0, 0, 0))
    return pl.pallas_call(
        kernel,
        grid=(steps,),
        in_specs=in_specs + [whole],
        out_specs=out_spec,
        out_shape=jax.ShapeDtypeStruct(out_shape, BF16),
        scratch_shapes=[pltpu.VMEM((16, 80, TL), BF16), pltpu.VMEM((TL, 4096), F32)],
        compiler_params=PARAMS,
        cost_estimate=pl.CostEstimate(
            flops=steps * 4 * 256 * 4096 * 256, transcendentals=steps * 256 * 4096, bytes_accessed=2 << 20
        ),
        name=name,
    )(*ins)


def normed_kernel(x_ref, w_ref, b_ref, mod_ref, out_ref, att_ref, str_ref):
    for h in range(H):
        att_ref[:, h * HD : (h + 1) * HD] = x_ref[h, :, :HD].astype(F32)
        str_ref[:, h * HD : (h + 1) * HD] = x_ref[h, :, HD:].astype(F32)
    projected = nn(att_ref[...].astype(BF16), w_ref[...]) + b_ref[...]
    residual = (str_ref[...] + mod_ref[0:1, :] * projected).astype(BF16).astype(F32)
    centred = residual - jnp.mean(residual, axis=1, keepdims=True)
    variance = jnp.mean(centred * centred, axis=1, keepdims=True)
    normed = centred * lax.rsqrt(variance + 1e-06) * (1.0 + mod_ref[2:3, :]) + mod_ref[1:2, :]
    att_ref[...] = normed
    for e in range(16):
        out_ref[e] = att_ref[3 * e : 3 * e + 3, :].astype(BF16)


def compact_kernel(x_ref, idx_ref, out_ref, rows_ref):
    for g in range(16):
        rows_ref[3 * g : 3 * g + 3, :] = x_ref[g].astype(F32)
    lines = lax.broadcasted_iota(jnp.int32, (16, 48), 0)
    table = (lines == idx_ref[...]).astype(F32).astype(BF16)
    rows = nn(table, rows_ref[...].astype(BF16)).astype(BF16)
    for t in range(16):
        out_ref[t] = rows


def expert_kernel(x_ref, we_ref, be_ref, wr_ref, router_ref, out_ref, gate_ref):
    rows = x_ref[...]
    hidden = jax.nn.gelu(nn(rows, we_ref[...]) + be_ref[...], approximate=True).astype(BF16)
    for c in range(16):
        out_ref[c] = nt(wr_ref[c], hidden).astype(BF16)
    gate_ref[...] = jax.nn.sigmoid(nt(router_ref[...], rows)).astype(BF16).astype(F32)


def gather_kernel(x_ref, gate_ref, rb_ref, idx_ref, out_ref):
    total = x_ref[0, :HD, :].astype(F32)
    for t in range(1, 16):
        total = total + x_ref[t, :HD, :].astype(F32)
    rows = (total + rb_ref[...]).astype(BF16).astype(F32)
    rows = (rows * gate_ref[0:1, :]).astype(BF16)
    for i in range(3):
        index = idx_ref[i * 256 : (i + 1) * 256, :]
        out_ref[i * 256 : (i + 1) * 256, :] = nt(one_hot(index, 256), rows).astype(BF16)


def scatter_kernel(p_ref, idx_ref, out_ref):
    turned = nt(eye(HD), p_ref[...]).astype(BF16)
    index = idx_ref[...]
    for t in range(16):
        out_ref[t] = nn(turned, one_hot(index, TL, t * TL)).astype(BF16)


def residual_kernel(o_ref, s_ref, w_ref, b_ref, mod_ref, out_ref, att_ref):
    for h in range(H):
        att_ref[h * HD : (h + 1) * HD, :] = o_ref[h, HD:, :]
    projected = None
    for start, size in TILES:
        rows = nt(eye(TL), att_ref[start : start + size, :]).astype(BF16)
        part = nn(rows, w_ref[start : start + size, :])
        projected = part if projected is None else projected + part
    projected = projected + b_ref[...]
    out_ref[...] = (s_ref[...].astype(F32) + mod_ref[0:1, :] * projected).astype(BF16)


def final_kernel(m_ref, res_ref, mod_ref, out_ref, mix_ref):
    for c in range(16):
        mix_ref[c * HD : (c + 1) * HD, :] = m_ref[c]
    for start, size in TILES:
        cols = slice(start, start + size)
        mixed = nt(eye(TL), mix_ref[cols, :])
        out_ref[:, cols] = (
            res_ref[:, cols].astype(F32) + mod_ref[3:4, cols] * mixed
        ).astype(BF16)


def call(kernel, out_shape, name, scratch=()):
    return pl.pallas_call(
        kernel, out_shape=out_shape, scratch_shapes=list(scratch), compiler_params=PARAMS, name=name
    )


def shaped(*shape, dtype=BF16):
    return jax.ShapeDtypeStruct(shape, dtype)


def per_device(
    stream,
    queries,
    key_vectors,
    value_vectors,
    modulation,
    output_weight,
    output_bias,
    router_weight,
    expand_weight,
    expand_bias,
    reduce_weight,
    reduce_bias,
    counts,
    picked_rows,
):
    me_frame = lax.axis_index("frame").astype(jnp.int32)
    me_tok = lax.axis_index("tok").astype(jnp.int32)
    exchange = functools.partial(lax.all_to_all, split_axis=0, concat_axis=0, tiled=True)
    mod = modulation[0]
    out_bias = output_bias[None, :]

    sent = call(split_kernel, shaped(16, 4 * HD, TL), "split")(
        key_vectors[0], value_vectors[0], queries[0], stream[0]
    )
    heads = exchange(sent, "tok")

    own_counts = counts[:, 0]
    all_counts = lax.all_gather(own_counts, "frame", axis=1)
    frames = jnp.arange(16, dtype=jnp.int32)
    before = (frames[:, None] < frames[None, :]).astype(jnp.int32)
    offsets = jnp.sum(all_counts[:, :, None] * before[None, :, :], axis=1)
    is_own = (frames == me_frame).astype(jnp.int32)
    own_offsets = jnp.sum(offsets * is_own[None, :], axis=1)
    expert_offsets = jnp.sum(offsets * is_own[:, None], axis=0)
    expert_counts = jnp.sum(all_counts * is_own[:, None], axis=0)
    picked = picked_rows[:, 0, :]
    slots = jnp.arange(48, dtype=jnp.int32)
    thirds = jnp.arange(3, dtype=jnp.int32) * 16
    pick_slot = ((frames[:, None] - own_offsets[None, :]) & 15)[:, :, None] + thirds
    pick_pos = jnp.sum(
        jnp.where(pick_slot[:, :, :, None] == slots, picked[None, :, None, :], 0), axis=3
    )
    pick_index = jnp.where(pick_slot < own_counts[None, :, None], pick_pos, -1).reshape(768, 1)
    held_slot = ((me_tok - expert_offsets) & 15)[:, None] + thirds
    held_index = jnp.where(
        held_slot < expert_counts[:, None], (expert_offsets[:, None] + held_slot) >> 4, -1
    ).reshape(1, 48)
    row_id = expert_offsets[:, None] + slots[None, :]
    back_index = jnp.where(
        slots[None, :] < expert_counts[:, None], (row_id & 15) * 16 + (row_id >> 4), -1
    ).reshape(768, 1)
    spread_index = jnp.where(slots[None, :] < own_counts[:, None], picked, -1).reshape(768, 1)

    router_own = jnp.sum(
        jnp.where((frames == me_frame)[None, :], router_weight, jnp.zeros_like(router_weight)), axis=1
    )
    router_rows = jnp.broadcast_to(router_own[None, :], (8, D))
    bias_own = lax.dynamic_slice_in_dim(reduce_bias[0].reshape(16, HD), me_tok, 1, 0).reshape(HD, 1)
    reduce_turned = reduce_weight[0].T.reshape(16, HD, 288)

    picked_out = attention(
        picked_kernel,
        3,
        (pick_index, heads),
        [pl.BlockSpec((TL, 1), lambda i: (i, 0))],
        (768, 2 * HD),
        pl.BlockSpec((TL, 2 * HD), lambda i: (i, 0)),
        "picked_attention",
    )
    heads, picked_out = lax.optimization_barrier((heads, picked_out))

    def main_part(first, steps):
        return attention(
            functools.partial(main_kernel, first),
            steps,
            (heads,),
            [],
            (steps, HD, TL),
            pl.BlockSpec((1, HD, TL), lambda i: (i, 0, 0)),
            "main_attention",
        )

    rows = exchange(picked_out.reshape(16, 48, 2 * HD), "tok")
    part_a = main_part(0, 5)
    rows, part_a = lax.optimization_barrier((rows, part_a))
    normed = call(
        normed_kernel, shaped(16, 3, D), "normed", [pltpu.VMEM((48, D), F32), pltpu.VMEM((48, D), F32)]
    )(rows, output_weight, out_bias, mod)
    normed = exchange(normed, "frame")
    part_b = main_part(5, 6)
    normed, part_b = lax.optimization_barrier((normed, part_b))
    rows = call(compact_kernel, shaped(16, 16, D), "compact", [pltpu.VMEM((48, D), F32)])(
        normed, held_index
    )
    rows = exchange(rows, "tok")
    part_c = main_part(11, 5)
    rows, part_c = lax.optimization_barrier((rows, part_c))
    partial_out, gates = call(
        expert_kernel, (shaped(16, HD, TL), shaped(8, TL, dtype=F32)), "expert"
    )(rows.reshape(TL, D), expand_weight[0], expand_bias, reduce_turned, router_rows)
    attended = jnp.concatenate([part_a, part_b, part_c], axis=0)
    both = exchange(jnp.concatenate([partial_out, attended], axis=1), "tok")
    outs = call(gather_kernel, shaped(768, HD), "weighted")(both, gates, bias_own, back_index)
    outs = exchange(outs.reshape(16, 48, HD), "frame")
    residual = call(residual_kernel, shaped(TL, D), "residual", [pltpu.VMEM((D, TL), BF16)])(
        both, stream[0], output_weight, out_bias, mod
    )
    mixed = call(scatter_kernel, shaped(16, HD, TL), "scatter")(outs.reshape(768, HD), spread_index)
    mixed = exchange(mixed, "tok")
    layer_out = call(final_kernel, shaped(TL, D), "final", [pltpu.VMEM((D, TL), BF16)])(
        mixed, residual, mod
    )
    return layer_out[None]


def solution(mesh):
    return jax.shard_map(
        per_device,
        mesh=mesh,
        in_specs=(
            P("frame", "tok", None),
            P("frame", "tok", None),
            P("frame", "tok", None),
            P("frame", "tok", None),
            P("frame", None, None),
            P(),
            P(),
            P(),
            P("frame", None, "tok"),
            P("frame", "tok"),
            P("frame", "tok", None),
            P("frame", None),
            P(None, "frame"),
            P(None, "frame", None),
        ),
        out_specs=P("frame", "tok", None),
        check_vma=False,
    )
```

time: 553 us -> 219 us (0.40)
  waiting for transfers between devices: 256 us -> 37.8 us
  Pallas kernels: 0 us -> 90 us
  local copies, waits for them, and re-layouts: 72.2 us -> 13.6 us
  matrix products: 52.8 us -> 0 us
  other arithmetic: 53.5 us -> 5.44 us
  blocking collectives: 57.8 us -> 20.6 us
  starting transfers between devices: 29.8 us -> 50 us
  loops' own time: 15 us -> 0 us
  between operations: 13.7 us -> 0.2 us
    psum x2 -> x0, waiting for transfers between devices: 189 us -> none  [the longest x1 98.2 us: per_device(): lax.psum(partial_out.astype(jnp.bfloat16), 'tok').astype(jnp.float32)]
    pallas_call x0 -> x12, Pallas kernels: none -> 90 us  [the longest x4 63.2 us: attention(): pl.pallas_call(kernel, grid=(steps,), in_specs=in_specs + [whole], out_sp...]
    all_to_all x1 -> x0, blocking collectives: 57.8 us -> none  [per_device(): lax.all_to_all(chosen, 'frame', split_axis=0, concat_axis=1, tiled=True)]
    dot_general x20 -> x0, matrix products: 52.8 us -> none  [the longest x8 23.4 us: one_block(): lax.dot_general(head_values, weights, (((1,), (1,)), ((), ())), preferred...]
    unnamed x4 -> x2, other arithmetic: 37 us -> 0.68 us
    unnamed x32 -> x36, local copies, waits for them, and re-layouts: 37.8 us -> 7.39 us
    all_to_all x5 -> x7, waiting for transfers between devices: 67.5 us -> 37.8 us  [the longest x1 13.3 us: per_device(): both = exchange(jnp.concatenate([partial_out, attended], axis=1), 'tok')]
    all_gather x0 -> x1, blocking collectives: none -> 20.6 us  [per_device(): all_counts = lax.all_gather(own_counts, 'frame', axis=1)]
  transfers between devices with their start and end apart: 7 -> 7, of which waited for: 7 -> 4; matrix products, arithmetic and copies ran while one was open for 3% -> 5% of each run, Pallas kernels for 0% -> 26%
where the time goes in v1:
time: 219 us; the launch traced here: 218 us
  Pallas kernels  90 us (41%)
  starting transfers between devices  50 us (23%)
  waiting for transfers between devices  37.8 us (17%)
  blocking collectives  20.6 us (9%)
  local copies, waits for them, and re-layouts  13.6 us (6%)
  other arithmetic  5.44 us (2%)
    pallas_call x4, Pallas kernels, attention(): pl.pallas_call(kernel, grid=(steps,), in_specs=in_specs + [whole], out_sp...  63.2 us
    all_gather x1, blocking collectives, per_device(): all_counts = lax.all_gather(own_counts, 'frame', axis=1)  20.6 us
    all_to_all x1, waiting for transfers between devices, per_device(): both = exchange(jnp.concatenate([partial_out, attended], axis=1), 'tok')  13.3 us
    all_to_all x1, starting transfers between devices, per_device(): normed = exchange(normed, 'frame')  11.4 us
    all_to_all x1, starting transfers between devices, per_device(): outs = exchange(outs.reshape(16, 48, HD), 'frame')  10.2 us
    all_to_all x1, waiting for transfers between devices, per_device(): outs = exchange(outs.reshape(16, 48, HD), 'frame')  9.52 us
    all_to_all x1, waiting for transfers between devices, per_device(): mixed = exchange(mixed, 'tok')  7.76 us
    all_to_all x1, starting transfers between devices, per_device(): heads = exchange(sent, 'tok')  7.72 us
  transfers between devices with their start and end apart: 7, of which 4 were waited for; matrix products, arithmetic and copies ran while one was open for 5% of the time, Pallas kernels for 26%

profile of v1, /device:TPU:1, one launch (start us, length us, event | category | flops | bytes accessed | tf_op | source)
XLA Modules:
  0.0 217.7 jit_solution(2601542411220596723)
XLA Ops:
  0.0 3.9 %split.1 = bf16[16,288,256]{2,1,0:T(8,128)(2,1)} custom-call(bf16[256,1152]{1,0:T(8,128)(2,1)} %bitcast.32, bf16[256,1152]{1,0:T(8,128)(2,1)} %bitcast.33, bf16[256,1152]{1,0:T(8,128)(2,1)} %bitcast.34, bf16[256,1152]{1,0:T(8,128)(2,1)} %bitcast.26), custom_call_target="tpu_custom_call" | custom-call | tf_op jit(solution)/shard_map/split/pallas_call | solution.py:223
  3.9 7.7 %all-to-all-start = ((bf16[16,288,256]{2,1,0:T(8,128)(2,1)}), bf16[16,288,256]{2,1,0:T(8,128)(2,1)S(1)}, u32[]{:S(2)}, u32[]{:S(2)}) async-start(bf16[16,288,256]{2,1,0:T(8,128)(2,1)} %split.1), calls=%async_computation | async-start | bytes 4718592 | tf_op jit(solution)/shard_map/all_to_all | solution.py:226
  11.7 20.6 %all-gather = s32[16,1,16]{2,1,0:T(1,128)S(1)} all-gather(s32[1,1,16]{2,1,0:T(1,128)S(1)} %bitcast.41), channel_id=1, replica_groups=mesh['frame'=16,'tok'=16] {'frame'}, dimensions={0}, use_global_device_ids=true | all-gather | bytes 1088 | tf_op jit(solution)/shard_map/all_gather | solution.py:229
  32.5 0.1 multiply_reduce_fusion.2
  32.7 1.0 select_reduce_fusion
  33.8 0.2 copy.36
  34.0 0.9 select_n.70.idx_ref
  34.9 0.6 broadcast_in_dim.47.b_ref
  35.6 0.6 select_n.64.idx_ref
  36.1 7.2 %all-to-all-done.r_ref = bf16[16,288,256]{2,1,0:T(8,128)(2,1)S(1)} async-done(((bf16[16,288,256]{2,1,0:T(8,128)(2,1)}), bf16[16,288,256]{2,1,0:T(8,128)(2,1)S(1)}, u32[]{:S(2)}, u32[]{:S(2)}) %all-to-all-start) | async-done | bytes 2359328 | tf_op jit(solution)/shard_map/all_to_all | solution.py:226
  43.3 1.4 copy-done.1
  44.7 12.2 %picked_attention.1 = bf16[768,144]{1,0:T(8,128)(2,1)} custom-call(s32[768,1]{1,0:T(8,128)} %select_n.70.idx_ref, bf16[16,288,256]{2,1,0:T(8,128)(2,1)} %copy-done.1), custom_call_target="tpu_custom_call" | custom-call | flops 3221225472 | bytes 2097152 | tf_op jit(solution)/shard_map/picked_attention/pallas_call | solution.py:103
  56.9 3.6 %all-to-all-start.1 = ((bf16[16,48,144]{2,1,0:T(8,128)(2,1)}), bf16[16,48,144]{2,1,0:T(8,128)(2,1)S(1)}, u32[]{:S(2)}, u32[]{:S(2)}) async-start(bf16[16,48,144]{2,1,0:T(8,128)(2,1)} %bitcast.35), calls=%async_computation.1 | async-start | bytes 786432 | tf_op jit(solution)/shard_map/all_to_all | solution.py:284
  60.5 16.1 %main_attention.3 = bf16[5,72,256]{2,1,0:T(8,128)(2,1)} custom-call(bf16[16,288,256]{2,1,0:T(8,128)(2,1)} %copy-done.1), custom_call_target="tpu_custom_call" | custom-call | flops 5368709120 | bytes 2097152 | tf_op jit(solution)/shard_map/main_attention/pallas_call | solution.py:103
  76.6 0.7 copy-done.4
  77.3 3.4 %normed.1 = bf16[16,3,1152]{2,1,0:T(4,128)(2,1)} custom-call(bf16[16,48,144]{2,1,0:T(8,128)(2,1)} %copy-done.4, bf16[1152,1152]{1,0:T(8,128)(2,1)} %w_ref.3, f32[1,1152]{1,0:T(1,128)} %broadcast_in_dim.47.b_ref, f32[4,1152]{1,0:T(4,128)} %bitcast.36), custom_call_target="tpu_custom_call" | custom-call | tf_op jit(solution)/shard_map/normed/pallas_call | solution.py:287
  80.7 11.4 %all-to-all-start.2 = ((bf16[16,3,1152]{2,1,0:T(4,128)(2,1)}), bf16[16,3,1152]{2,1,0:T(4,128)(2,1)S(1)}, u32[]{:S(2)}, u32[]{:S(2)}) async-start(bf16[16,3,1152]{2,1,0:T(4,128)(2,1)} %normed.1), calls=%async_computation.2 | async-start | bytes 294912 | tf_op jit(solution)/shard_map/all_to_all | solution.py:290
  92.1 18.8 %main_attention.4 = bf16[6,72,256]{2,1,0:T(8,128)(2,1)} custom-call(bf16[16,288,256]{2,1,0:T(8,128)(2,1)} %copy-done.1), custom_call_target="tpu_custom_call" | custom-call | flops 6442450944 | bytes 2097152 | tf_op jit(solution)/shard_map/main_attention/pallas_call | solution.py:103
  111.0 0.7 copy-done.8
  111.7 1.9 compact.1
  113.6 6.9 %all-to-all-start.3 = ((bf16[16,16,1152]{2,1,0:T(8,128)(2,1)}), bf16[16,16,1152]{2,1,0:T(8,128)(2,1)S(1)}, u32[]{:S(2)}, u32[]{:S(2)}) async-start(bf16[16,16,1152]{2,1,0:T(8,128)(2,1)} %compact.1), calls=%async_computation.3 | async-start | bytes 1179648 | tf_op jit(solution)/shard_map/all_to_all | solution.py:296
  120.6 1.2 copy.38
  121.8 1.3 copy.39
  123.1 16.1 %main_attention.5 = bf16[5,72,256]{2,1,0:T(8,128)(2,1)} custom-call(bf16[16,288,256]{2,1,0:T(8,128)(2,1)} %copy-done.1), custom_call_target="tpu_custom_call" | custom-call | flops 5368709120 | bytes 2097152 | tf_op jit(solution)/shard_map/main_attention/pallas_call | solution.py:103
  139.2 0.6 broadcast_in_dim.81.router_ref
  139.8 0.2 copy-done.2
  140.0 4.2 %expert.1 = (bf16[16,72,256]{2,1,0:T(8,128)(2,1)}, f32[8,256]{1,0:T(8,128)}) custom-call(bf16[256,1152]{1,0:T(8,128)(2,1)} %bitcast.28, bf16[1152,288]{1,0:T(8,128)(2,1)} %bitcast.24, f32[1,288]{1,0:T(1,128)} %be_ref.1, bf16[16,72,288]{2,1,0:T(8,128)(2,1)} %bitcast.25, bf16[8,1152]{1,0:T(8,128)(2,1)} %broadcast_in_dim.81.router_ref), custom_call_target="tpu_custom_call" | custom-call | tf_op jit(solution)/shard_map/expert/pallas_call | solution.py:299
  144.3 2.2 maximum_maximum_fusion
  146.4 6.6 %all-to-all-start.4 = ((bf16[16,144,256]{2,1,0:T(8,128)(2,1)}), bf16[16,144,256]{2,1,0:T(8,128)(2,1)S(1)}, u32[]{:S(2)}, u32[]{:S(2)}) async-start(bf16[16,144,256]{2,1,0:T(8,128)(2,1)} %maximum_maximum_fusion), calls=%async_computation.4 | async-start | bytes 2359296 | tf_op jit(solution)/shard_map/all_to_all | solution.py:303
  153.2 0.7 copy.40.rb_ref
  154.0 0.9 reshape.300.idx_ref
  155.0 0.2 lt.117
  155.2 0.6 broadcast.169
  155.8 0.7 reduce.5
  156.5 0.2 squeeze.33
  156.6 13.3 %all-to-all-done.4.x_ref.o_ref = bf16[16,144,256]{2,1,0:T(8,128)(2,1)S(1)} async-done(((bf16[16,144,256]{2,1,0:T(8,128)(2,1)}), bf16[16,144,256]{2,1,0:T(8,128)(2,1)S(1)}, u32[]{:S(2)}, u32[]{:S(2)}) %all-to-all-start.4) | async-done | bytes 1179680 | tf_op jit(solution)/shard_map/all_to_all | solution.py:303
  169.9 1.0 copy-done
  170.9 2.4 %weighted.1 = bf16[768,72]{1,0:T(8,128)(2,1)} custom-call(bf16[16,144,256]{2,1,0:T(8,128)(2,1)} %copy-done, f32[8,256]{1,0:T(8,128)} %get-tuple-element.24.gate_ref, f32[72,1]{1,0:T(8,128)} %copy.40.rb_ref, s32[768,1]{1,0:T(8,128)} %reshape.300.idx_ref), custom_call_target="tpu_custom_call" | custom-call | tf_op jit(solution)/shard_map/weighted/pallas_call | solution.py:304
  173.4 10.2 %all-to-all-start.5 = ((bf16[16,48,72]{2,1,0:T(8,128)(2,1)}), bf16[16,48,72]{2,1,0:T(8,128)(2,1)S(1)}, u32[]{:S(2)}, u32[]{:S(2)}) async-start(bf16[16,48,72]{2,1,0:T(8,128)(2,1)} %bitcast.30), calls=%async_computation.5 | async-start | bytes 393216 | tf_op jit(solution)/shard_map/all_to_all | solution.py:305
  183.5 0.8 broadcast_select_fusion.idx_ref
  184.3 9.5 %all-to-all-done.5 = bf16[16,48,72]{2,1,0:T(8,128)(2,1)S(1)} async-done(((bf16[16,48,72]{2,1,0:T(8,128)(2,1)}), bf16[16,48,72]{2,1,0:T(8,128)(2,1)S(1)}, u32[]{:S(2)}, u32[]{:S(2)}) %all-to-all-start.5) | async-done | bytes 110624 | tf_op jit(solution)/shard_map/all_to_all | solution.py:305
  193.8 0.7 copy-done.5
  194.5 3.8 %scatter.1 = bf16[16,72,256]{2,1,0:T(8,128)(2,1)} custom-call(bf16[768,72]{1,0:T(8,128)(2,1)} %bitcast.29, s32[768,1]{1,0:T(8,128)} %broadcast_select_fusion.idx_ref), custom_call_target="tpu_custom_call" | custom-call | tf_op jit(solution)/shard_map/scatter/pallas_call | solution.py:309
  198.3 3.6 %all-to-all-start.6 = ((bf16[16,72,256]{2,1,0:T(8,128)(2,1)}), bf16[16,72,256]{2,1,0:T(8,128)(2,1)S(1)}, u32[]{:S(2)}, u32[]{:S(2)}) async-start(bf16[16,72,256]{2,1,0:T(8,128)(2,1)} %scatter.1), calls=%async_computation.6 | async-start | bytes 1179648 | tf_op jit(solution)/shard_map/all_to_all | solution.py:310
  201.9 4.8 %residual.1.res_ref = bf16[256,1152]{1,0:T(8,128)(2,1)} custom-call(bf16[16,144,256]{2,1,0:T(8,128)(2,1)} %copy-done, bf16[256,1152]{1,0:T(8,128)(2,1)} %bitcast.27, bf16[1152,1152]{1,0:T(8,128)(2,1)} %w_ref.3, f32[1,1152]{1,0:T(1,128)} %broadcast_in_dim.47.b_ref, f32[4,1152]{1,0:T(4,128)} %bitcast.37), custom_call_target="tpu_custom_call" | custom-call | tf_op jit(solution)/shard_map/residual/pallas_call | solution.py:306
  206.7 7.8 %all-to-all-done.6.m_ref = bf16[16,72,256]{2,1,0:T(8,128)(2,1)S(1)} async-done(((bf16[16,72,256]{2,1,0:T(8,128)(2,1)}), bf16[16,72,256]{2,1,0:T(8,128)(2,1)S(1)}, u32[]{:S(2)}, u32[]{:S(2)}) %all-to-all-start.6) | async-done | bytes 589856 | tf_op jit(solution)/shard_map/all_to_all | solution.py:310
  214.4 0.8 copy-done.3
  215.2 2.4 %final.1 = bf16[256,1152]{1,0:T(8,128)(2,1)} custom-call(bf16[16,72,256]{2,1,0:T(8,128)(2,1)} %copy-done.3, bf16[256,1152]{1,0:T(8,128)(2,1)} %residual.1.res_ref, f32[4,1152]{1,0:T(4,128)} %bitcast.38), custom_call_target="tpu_custom_call" | custom-call | tf_op jit(solution)/shard_map/final/pallas_call | solution.py:311
  (47 shorter events, 0.9 us)
Async XLA Ops:
  3.9 7.7 %copy-start.15 = (s32[16,1]{0,1:T(1,128)S(1)}, s32[16,1]{0,1:T(1,128)}, u32[]{:S(2)}) copy-start(s32[16,1]{0,1:T(1,128)} %param.26) | copy-start | bytes 196
  3.9 28.8 %copy-start.13 = (s32[16,1,48]{2,1,0:T(1,128)S(1)}, s32[16,1,48]{2,1,0:T(1,128)}, u32[]{:S(2)}) copy-start(s32[16,1,48]{2,1,0:T(1,128)} %param.27) | copy-start | bytes 9220
  3.9 31.0 %copy-start.14 = (f32[1152]{0:T(1024)S(1)}, f32[1152]{0:T(1024)}, u32[]{:S(2)}) copy-start(f32[1152]{0:T(1024)} %param.20) | copy-start | bytes 13828
  3.9 39.4 %all-to-all-start = ((bf16[16,288,256]{2,1,0:T(8,128)(2,1)}), bf16[16,288,256]{2,1,0:T(8,128)(2,1)S(1)}, u32[]{:S(2)}, u32[]{:S(2)}) async-start(bf16[16,288,256]{2,1,0:T(8,128)(2,1)} %split.1), calls=%async_computation | async-start | bytes 4718592 | tf_op jit(solution)/shard_map/all_to_all | solution.py:226
  43.3 1.4 copy-start.1
  56.9 19.7 %all-to-all-start.1 = ((bf16[16,48,144]{2,1,0:T(8,128)(2,1)}), bf16[16,48,144]{2,1,0:T(8,128)(2,1)S(1)}, u32[]{:S(2)}, u32[]{:S(2)}) async-start(bf16[16,48,144]{2,1,0:T(8,128)(2,1)} %bitcast.35), calls=%async_computation.1 | async-start | bytes 786432 | tf_op jit(solution)/shard_map/all_to_all | solution.py:284
  76.6 0.7 copy-start.4
  80.7 30.3 %all-to-all-start.2 = ((bf16[16,3,1152]{2,1,0:T(4,128)(2,1)}), bf16[16,3,1152]{2,1,0:T(4,128)(2,1)S(1)}, u32[]{:S(2)}, u32[]{:S(2)}) async-start(bf16[16,3,1152]{2,1,0:T(4,128)(2,1)} %normed.1), calls=%async_computation.2 | async-start | bytes 294912 | tf_op jit(solution)/shard_map/all_to_all | solution.py:290
  92.1 28.4 %copy-start.12 = (bf16[1152,16]{0,1:T(8,128)(2,1)S(1)}, bf16[1152,16]{0,1:T(8,128)(2,1)}, u32[]{:S(2)}) copy-start(bf16[1152,16]{0,1:T(8,128)(2,1)} %param.21) | copy-start | bytes 110596
  111.0 9.6 %copy-start.6 = (bf16[1,1152,288]{1,2,0:T(8,128)(2,1)S(1)}, bf16[1,1152,288]{1,2,0:T(8,128)(2,1)}, u32[]{:S(2)}) copy-start(bf16[1,1152,288]{1,2,0:T(8,128)(2,1)} %param.22) | copy-start | bytes 1990660
  111.0 10.9 %copy-start.7 = (bf16[1,288,1152]{2,1,0:T(8,128)(2,1)S(1)}, bf16[1,288,1152]{2,1,0:T(8,128)(2,1)}, u32[]{:S(2)}) copy-start(bf16[1,288,1152]{2,1,0:T(8,128)(2,1)} %param.24) | copy-start | bytes 1990660
  111.0 0.7 copy-start.8
  113.6 25.6 %all-to-all-start.3 = ((bf16[16,16,1152]{2,1,0:T(8,128)(2,1)}), bf16[16,16,1152]{2,1,0:T(8,128)(2,1)S(1)}, u32[]{:S(2)}, u32[]{:S(2)}) async-start(bf16[16,16,1152]{2,1,0:T(8,128)(2,1)} %compact.1), calls=%async_computation.3 | async-start | bytes 1179648 | tf_op jit(solution)/shard_map/all_to_all | solution.py:296
  139.2 5.1 %copy-start.9 = (bf16[6,72,256]{2,1,0:T(8,128)(2,1)S(1)}, bf16[6,72,256]{2,1,0:T(8,128)(2,1)}, u32[]{:S(2)}) copy-start(bf16[6,72,256]{2,1,0:T(8,128)(2,1)} %main_attention.4) | copy-start | bytes 663556
  139.2 5.1 %copy-start.10 = (bf16[5,72,256]{2,1,0:T(8,128)(2,1)S(1)}, bf16[5,72,256]{2,1,0:T(8,128)(2,1)}, u32[]{:S(2)}) copy-start(bf16[5,72,256]{2,1,0:T(8,128)(2,1)} %main_attention.3) | copy-start | bytes 552964
  139.2 5.1 %copy-start.11 = (bf16[5,72,256]{2,1,0:T(8,128)(2,1)S(1)}, bf16[5,72,256]{2,1,0:T(8,128)(2,1)}, u32[]{:S(2)}) copy-start(bf16[5,72,256]{2,1,0:T(8,128)(2,1)} %main_attention.5) | copy-start | bytes 552964
  139.2 0.8 copy-start.2
  144.2 8.8 %copy-start.16 = (f32[1,1152]{1,0:T(1,128)S(1)}, f32[1,1152]{1,0:T(1,128)}, u32[]{:S(2)}) copy-start(f32[1,1152]{1,0:T(1,128)} %param.25) | copy-start | bytes 13828
  146.4 23.5 %all-to-all-start.4 = ((bf16[16,144,256]{2,1,0:T(8,128)(2,1)}), bf16[16,144,256]{2,1,0:T(8,128)(2,1)S(1)}, u32[]{:S(2)}, u32[]{:S(2)}) async-start(bf16[16,144,256]{2,1,0:T(8,128)(2,1)} %maximum_maximum_fusion), calls=%async_computation.4 | async-start | bytes 2359296 | tf_op jit(solution)/shard_map/all_to_all | solution.py:303
  169.9 1.0 copy-start
  173.4 20.5 %all-to-all-start.5 = ((bf16[16,48,72]{2,1,0:T(8,128)(2,1)}), bf16[16,48,72]{2,1,0:T(8,128)(2,1)S(1)}, u32[]{:S(2)}, u32[]{:S(2)}) async-start(bf16[16,48,72]{2,1,0:T(8,128)(2,1)} %bitcast.30), calls=%async_computation.5 | async-start | bytes 393216 | tf_op jit(solution)/shard_map/all_to_all | solution.py:305
  193.8 0.7 copy-start.5
  198.3 16.1 %all-to-all-start.6 = ((bf16[16,72,256]{2,1,0:T(8,128)(2,1)}), bf16[16,72,256]{2,1,0:T(8,128)(2,1)S(1)}, u32[]{:S(2)}, u32[]{:S(2)}) async-start(bf16[16,72,256]{2,1,0:T(8,128)(2,1)} %scatter.1), calls=%async_computation.6 | async-start | bytes 1179648 | tf_op jit(solution)/shard_map/all_to_all | solution.py:310
  214.4 0.8 copy-start.3

commit v2 on v1

--- a/solution.py
+++ b/solution.py
@@ -14,8 +14,7 @@
 TL = 256
 F32 = jnp.float32
 BF16 = jnp.bfloat16
-EXP_SCALE = math.log2(math.e) / math.sqrt(HD)
-PARAMS = pltpu.CompilerParams(vmem_limit_bytes=56 * 1024 * 1024)
+SCALE = 1.0 / math.sqrt(HD)
 
 
 def nt(left, right):
@@ -52,67 +51,116 @@
                     ].astype(BF16)
 
 
-def fill_values(r_ref, v_ref):
+def prepare(r_ref, k_ref, v_ref):
     for j in range(16):
-        v_ref[j, :HD, :] = r_ref[j, HD : 2 * HD, :]
-        v_ref[j, HD:, :] = jnp.ones((8, TL), BF16)
-
-
-def attend(q, r_ref, v_ref, s_ref):
+        k_ref[j * TL : (j + 1) * TL, :] = nt(eye(TL), r_ref[j, :HD, :]).astype(BF16)
+        v_ref[:HD, j * TL : (j + 1) * TL] = r_ref[j, HD : 2 * HD, :]
+        v_ref[HD:, j * TL : (j + 1) * TL] = jnp.ones((8, TL), BF16)
+
+
+def score_part(q, k_ref, s_ref, j, top):
+    scores = nn(k_ref[j * 512 : (j + 1) * 512, :], q)
+    s_ref[j * 512 : (j + 1) * 512, :] = scores
+    for b in range(64):
+        part = scores[b * 8 : (b + 1) * 8]
+        top = part if top is None else jnp.maximum(top, part)
+    return top
+
+
+def value_part(top, v_ref, s_ref, j, total):
+    weights = jnp.exp((s_ref[j * TL : (j + 1) * TL, :] - top) * SCALE).astype(BF16)
+    part = nn(v_ref[:, j * TL : (j + 1) * TL], weights)
+    return part if total is None else total + part
+
+
+def interleave(q, top, k_ref, v_ref, next_ref, s_ref):
+    new_top, total = None, None
+    for j in range(16):
+        if q is not None and j % 2 == 0:
+            new_top = score_part(q, k_ref, next_ref, j // 2, new_top)
+        if top is not None:
+            total = value_part(top, v_ref, s_ref, j, total)
+    if q is not None:
+        new_top = jnp.max(new_top, axis=0, keepdims=True)
+    if top is not None:
+        total = (total[:HD] / total[HD : HD + 1]).astype(BF16)
+    return new_top, total
+
+
+def picked_kernel(idx_ref, r_ref, out_ref, k_ref, v_ref, s_ref, rows_ref):
+    prepare(r_ref, k_ref, v_ref)
+    lines = lax.broadcasted_iota(jnp.int32, (TL, TL), 0)
+    for i in range(3):
+        index = idx_ref[:, i * TL : (i + 1) * TL]
+        rows = None
+        for j in range(16):
+            table = (lines == index - j * TL).astype(F32).astype(BF16)
+            part = nn(r_ref[j, 2 * HD :, :], table)
+            rows = part if rows is None else rows + part
+        rows_ref[i] = rows.astype(BF16)
     top = None
-    for j in range(16):
-        scores = nn(q, r_ref[j, :HD, :])
-        s_ref[:, j * TL : (j + 1) * TL] = scores
-        part = jnp.maximum(scores[:, :128], scores[:, 128:])
-        top = part if top is None else jnp.maximum(top, part)
-    top = jnp.max(top, axis=1, keepdims=True)
-    total = None
-    for j in range(16):
-        weights = jnp.exp2((s_ref[:, j * TL : (j + 1) * TL] - top) * EXP_SCALE).astype(BF16)
-        part = nt(weights, v_ref[j])
-        total = part if total is None else total + part
-    return total[:, :HD] / total[:, HD : HD + 1]
-
-
-def picked_kernel(idx_ref, r_ref, out_ref, v_ref, s_ref):
-    @pl.when(pl.program_id(0) == 0)
+    for i in range(4):
+        q = rows_ref[i, :HD, :] if i < 3 else None
+        top, done = interleave(q, top, k_ref, v_ref, s_ref.at[i % 2], s_ref.at[1 - i % 2])
+        if i > 0:
+            both = jnp.concatenate([done, rows_ref[i - 1, HD:, :]], axis=0)
+            out_ref[(i - 1) * TL : i * TL, :] = nt(eye(TL), both).astype(BF16)
+
+
+def main_kernel(steps, aliased, *refs):
+    first_ref, q_ref, k_ref, v_ref = refs[:4]
+    out_ref, s_ref, top_ref = refs[4 + aliased :]
+    step = pl.program_id(0)
+
+    @pl.when(step == 0)
     def _():
-        fill_values(r_ref, v_ref)
-
-    index = idx_ref[...]
-    rows = None
-    for j in range(16):
-        part = nt(one_hot(index, TL, j * TL), r_ref[j, 2 * HD :, :])
-        rows = part if rows is None else rows + part
-    out_ref[:, :HD] = attend(rows[:, :HD].astype(BF16), r_ref, v_ref, s_ref).astype(BF16)
-    out_ref[:, HD:] = rows[:, HD:].astype(BF16)
-
-
-def main_kernel(first, r_ref, out_ref, v_ref, s_ref):
-    @pl.when(pl.program_id(0) == 0)
+        top, _ = interleave(first_ref[0], None, k_ref, v_ref, s_ref.at[0], None)
+        top_ref[0] = jnp.broadcast_to(top, (8, TL))
+
+    def one(now, last):
+        q = None if last else q_ref[0]
+        top, done = interleave(
+            q, top_ref[now, 0:1, :], k_ref, v_ref, s_ref.at[1 - now], s_ref.at[now]
+        )
+        if not last:
+            top_ref[1 - now] = jnp.broadcast_to(top, (8, TL))
+        out_ref[0] = done
+
+    for now in range(2):
+
+        @pl.when((step < steps - 1) & (lax.rem(step, 2) == now))
+        def _(now=now):
+            one(now, False)
+
+    @pl.when(step == steps - 1)
     def _():
-        fill_values(r_ref, v_ref)
-
-    q = nt(eye(TL), r_ref[first + pl.program_id(0), 2 * HD : 3 * HD, :]).astype(BF16)
-    out = attend(q, r_ref, v_ref, s_ref).astype(BF16)
-    out_ref[0] = nt(eye(HD), out).astype(BF16)
-
-
-def attention(kernel, steps, ins, in_specs, out_shape, out_spec, name):
-    whole = pl.BlockSpec((16, 4 * HD, TL), lambda i: (0, 0, 0))
+        one((steps - 1) % 2, True)
+
+
+def main_part(heads, keys, values, first, steps, before=None):
+    aliased = int(before is not None)
+    head_block = lambda f: pl.BlockSpec((1, HD, TL), f)
+    whole = lambda shape: pl.BlockSpec(shape, lambda i: (0, 0))
+    in_specs = [
+        head_block(lambda i: (first, 2, 0)),
+        head_block(lambda i: (first + jnp.minimum(i + 1, steps - 1), 2, 0)),
+        whole((4096, HD)),
+        whole((80, 4096)),
+    ] + [pl.BlockSpec(memory_space=pl.ANY)] * aliased
     return pl.pallas_call(
-        kernel,
+        functools.partial(main_kernel, steps, aliased),
         grid=(steps,),
-        in_specs=in_specs + [whole],
-        out_specs=out_spec,
-        out_shape=jax.ShapeDtypeStruct(out_shape, BF16),
-        scratch_shapes=[pltpu.VMEM((16, 80, TL), BF16), pltpu.VMEM((TL, 4096), F32)],
-        compiler_params=PARAMS,
+        in_specs=in_specs,
+        out_specs=head_block(lambda i: (first + i, 1, 0)),
+        out_shape=shaped(16, 2 * HD, TL),
+        scratch_shapes=[pltpu.VMEM((2, 4096, TL), F32), pltpu.VMEM((2, 8, TL), F32)],
+        input_output_aliases={4: 0} if aliased else {},
+        compiler_params=pltpu.CompilerParams(vmem_limit_bytes=18 << 20),
         cost_estimate=pl.CostEstimate(
             flops=steps * 4 * 256 * 4096 * 256, transcendentals=steps * 256 * 4096, bytes_accessed=2 << 20
         ),
-        name=name,
-    )(*ins)
+        name="main_attention",
+    )(*in_hbm(heads, heads, keys, values, *([before] if aliased else [])))
 
 
 def normed_kernel(x_ref, w_ref, b_ref, mod_ref, out_ref, att_ref, str_ref):
@@ -139,7 +187,7 @@
         out_ref[t] = rows
 
 
-def expert_kernel(x_ref, we_ref, be_ref, wr_ref, router_ref, out_ref, gate_ref):
+def expert_kernel(x_ref, we_ref, be_ref, wr_ref, router_ref, _, out_ref, gate_ref):
     rows = x_ref[...]
     hidden = jax.nn.gelu(nn(rows, we_ref[...]) + be_ref[...], approximate=True).astype(BF16)
     for c in range(16):
@@ -188,14 +236,22 @@
         ).astype(BF16)
 
 
-def call(kernel, out_shape, name, scratch=()):
+def call(kernel, out_shape, name, mib, scratch=()):
     return pl.pallas_call(
-        kernel, out_shape=out_shape, scratch_shapes=list(scratch), compiler_params=PARAMS, name=name
+        kernel,
+        out_shape=out_shape,
+        scratch_shapes=list(scratch),
+        compiler_params=pltpu.CompilerParams(vmem_limit_bytes=mib << 20),
+        name=name,
     )
 
 
 def shaped(*shape, dtype=BF16):
-    return jax.ShapeDtypeStruct(shape, dtype)
+    return pltpu.HBM(shape, dtype)
+
+
+def in_hbm(*arrays):
+    return [pltpu.with_memory_space_constraint(array, pltpu.HBM) for array in arrays]
 
 
 def per_device(
@@ -220,8 +276,8 @@
     mod = modulation[0]
     out_bias = output_bias[None, :]
 
-    sent = call(split_kernel, shaped(16, 4 * HD, TL), "split")(
-        key_vectors[0], value_vectors[0], queries[0], stream[0]
+    sent = call(split_kernel, shaped(16, 4 * HD, TL), "split", 12)(
+        *in_hbm(key_vectors[0], value_vectors[0], queries[0], stream[0])
     )
     heads = exchange(sent, "tok")
 
@@ -241,7 +297,7 @@
     pick_pos = jnp.sum(
         jnp.where(pick_slot[:, :, :, None] == slots, picked[None, :, None, :], 0), axis=3
     )
-    pick_index = jnp.where(pick_slot < own_counts[None, :, None], pick_pos, -1).reshape(768, 1)
+    pick_index = jnp.where(pick_slot < own_counts[None, :, None], pick_pos, -1).reshape(1, 768)
     held_slot = ((me_tok - expert_offsets) & 15)[:, None] + thirds
     held_index = jnp.where(
         held_slot < expert_counts[:, None], (expert_offsets[:, None] + held_slot) >> 4, -1
@@ -259,57 +315,57 @@
     bias_own = lax.dynamic_slice_in_dim(reduce_bias[0].reshape(16, HD), me_tok, 1, 0).reshape(HD, 1)
     reduce_turned = reduce_weight[0].T.reshape(16, HD, 288)
 
-    picked_out = attention(
+    picked_out, keys, values = call(
         picked_kernel,
-        3,
-        (pick_index, heads),
-        [pl.BlockSpec((TL, 1), lambda i: (i, 0))],
-        (768, 2 * HD),
-        pl.BlockSpec((TL, 2 * HD), lambda i: (i, 0)),
+        (shaped(768, 2 * HD), shaped(4096, HD), shaped(80, 4096)),
         "picked_attention",
-    )
-    heads, picked_out = lax.optimization_barrier((heads, picked_out))
-
-    def main_part(first, steps):
-        return attention(
-            functools.partial(main_kernel, first),
-            steps,
-            (heads,),
-            [],
-            (steps, HD, TL),
-            pl.BlockSpec((1, HD, TL), lambda i: (i, 0, 0)),
-            "main_attention",
-        )
+        24,
+        [pltpu.VMEM((2, 4096, TL), F32), pltpu.VMEM((3, 2 * HD, TL), BF16)],
+    )(pick_index, heads)
 
     rows = exchange(picked_out.reshape(16, 48, 2 * HD), "tok")
-    part_a = main_part(0, 5)
-    rows, part_a = lax.optimization_barrier((rows, part_a))
+    attended = main_part(heads, keys, values, 0, 5)
+    rows, attended = lax.optimization_barrier((rows, attended))
     normed = call(
-        normed_kernel, shaped(16, 3, D), "normed", [pltpu.VMEM((48, D), F32), pltpu.VMEM((48, D), F32)]
+        normed_kernel, shaped(16, 3, D), "normed", 10, [pltpu.VMEM((48, D), F32), pltpu.VMEM((48, D), F32)]
     )(rows, output_weight, out_bias, mod)
     normed = exchange(normed, "frame")
-    part_b = main_part(5, 6)
-    normed, part_b = lax.optimization_barrier((normed, part_b))
-    rows = call(compact_kernel, shaped(16, 16, D), "compact", [pltpu.VMEM((48, D), F32)])(
+    attended = main_part(heads, keys, values, 5, 6, attended)
+    normed, attended = lax.optimization_barrier((normed, attended))
+    rows = call(compact_kernel, shaped(16, 16, D), "compact", 6, [pltpu.VMEM((48, D), F32)])(
         normed, held_index
     )
     rows = exchange(rows, "tok")
-    part_c = main_part(11, 5)
-    rows, part_c = lax.optimization_barrier((rows, part_c))
-    partial_out, gates = call(
-        expert_kernel, (shaped(16, HD, TL), shaped(8, TL, dtype=F32)), "expert"
-    )(rows.reshape(TL, D), expand_weight[0], expand_bias, reduce_turned, router_rows)
-    attended = jnp.concatenate([part_a, part_b, part_c], axis=0)
-    both = exchange(jnp.concatenate([partial_out, attended], axis=1), "tok")
-    outs = call(gather_kernel, shaped(768, HD), "weighted")(both, gates, bias_own, back_index)
+    attended = main_part(heads, keys, values, 11, 5, attended)
+    rows, attended = lax.optimization_barrier((rows, attended))
+    whole = lambda shape: pl.BlockSpec(shape, lambda i: (0,) * len(shape))
+    both, gates = pl.pallas_call(
+        expert_kernel,
+        grid=(1,),
+        in_specs=[
+            whole((TL, D)),
+            whole((D, 288)),
+            whole((1, 288)),
+            whole((16, HD, 288)),
+            whole((8, D)),
+            pl.BlockSpec(memory_space=pl.ANY),
+        ],
+        out_specs=(whole((16, HD, TL)), whole((8, TL))),
+        out_shape=(shaped(16, 2 * HD, TL), shaped(8, TL, dtype=F32)),
+        input_output_aliases={5: 0},
+        compiler_params=pltpu.CompilerParams(vmem_limit_bytes=12 << 20),
+        name="expert",
+    )(rows.reshape(TL, D), *in_hbm(expand_weight[0], expand_bias, reduce_turned, router_rows, attended))
+    both = exchange(both, "tok")
+    outs = call(gather_kernel, shaped(768, HD), "weighted", 8)(both, *in_hbm(gates, bias_own, back_index))
     outs = exchange(outs.reshape(16, 48, HD), "frame")
-    residual = call(residual_kernel, shaped(TL, D), "residual", [pltpu.VMEM((D, TL), BF16)])(
-        both, stream[0], output_weight, out_bias, mod
-    )
-    mixed = call(scatter_kernel, shaped(16, HD, TL), "scatter")(outs.reshape(768, HD), spread_index)
+    residual = call(residual_kernel, shaped(TL, D), "residual", 12, [pltpu.VMEM((D, TL), BF16)])(
+        *in_hbm(both, stream[0], output_weight, out_bias, mod)
+    )
+    mixed = call(scatter_kernel, shaped(16, HD, TL), "scatter", 8)(outs.reshape(768, HD), *in_hbm(spread_index))
     mixed = exchange(mixed, "tok")
-    layer_out = call(final_kernel, shaped(TL, D), "final", [pltpu.VMEM((D, TL), BF16)])(
-        mixed, residual, mod
+    layer_out = call(final_kernel, shaped(TL, D), "final", 8, [pltpu.VMEM((D, TL), BF16)])(
+        mixed, *in_hbm(residual, mod)
     )
     return layer_out[None]
 

time: 219 us -> 179 us (0.82)
  Pallas kernels: 90 us -> 57.7 us
  local copies, waits for them, and re-layouts: 13.6 us -> 6.39 us
    pallas_call x12, Pallas kernels: 90 us -> 57.7 us  [the longest x3 25.8 us: main_part(): pl.pallas_call(functools.partial(main_kernel, steps, aliased), grid=(step...]
    unnamed x36 -> x26, local copies, waits for them, and re-layouts: 7.39 us -> 1.86 us
  transfers between devices with their start and end apart: 7 -> 7, of which waited for: 4 -> 4; matrix products, arithmetic and copies ran while one was open for 5% -> 5% of each run, Pallas kernels for 26% -> 17%
where the time goes in v2:
time: 179 us; the launch traced here: 178 us
  Pallas kernels  57.7 us (32%)
  starting transfers between devices  50.2 us (28%)
  waiting for transfers between devices  39.4 us (22%)
  blocking collectives  20.6 us (12%)
  local copies, waits for them, and re-layouts  6.39 us (4%)
  other arithmetic  3.31 us (2%)
    pallas_call x3, Pallas kernels, main_part(): pl.pallas_call(functools.partial(main_kernel, steps, aliased), grid=(step...  25.8 us
    all_gather x1, blocking collectives, per_device(): all_counts = lax.all_gather(own_counts, 'frame', axis=1)  20.6 us
    all_to_all x1, waiting for transfers between devices, per_device(): both = exchange(both, 'tok')  13.2 us
    all_to_all x1, starting transfers between devices, per_device(): normed = exchange(normed, 'frame')  11.9 us
    all_to_all x1, starting transfers between devices, per_device(): outs = exchange(outs.reshape(16, 48, HD), 'frame')  10.1 us
    all_to_all x1, waiting for transfers between devices, per_device(): outs = exchange(outs.reshape(16, 48, HD), 'frame')  9.52 us
    all_to_all x1, waiting for transfers between devices, per_device(): heads = exchange(sent, 'tok')  8.91 us
    pallas_call x1, Pallas kernels, per_device(): call(picked_kernel, (shaped(768, 2 * HD), shaped(4096, HD), shaped(80, 40...  8.04 us
  transfers between devices with their start and end apart: 7, of which 4 were waited for; matrix products, arithmetic and copies ran while one was open for 5% of the time, Pallas kernels for 17%

profile of v2, /device:TPU:1, one launch (start us, length us, event | category | flops | bytes accessed | tf_op | source)
XLA Modules:
  0.0 177.9 jit_solution(10993352082184827963)
XLA Ops:
  0.0 3.9 %split.1 = bf16[16,288,256]{2,1,0:T(8,128)(2,1)} custom-call(bf16[256,1152]{1,0:T(8,128)(2,1)} %bitcast.35, bf16[256,1152]{1,0:T(8,128)(2,1)} %bitcast.36, bf16[256,1152]{1,0:T(8,128)(2,1)} %bitcast.37, bf16[256,1152]{1,0:T(8,128)(2,1)} %bitcast.31), custom_call_target="tpu_custom_call" | custom-call | tf_op jit(solution)/shard_map/split/pallas_call | solution.py:279
  3.9 7.7 %all-to-all-start = ((bf16[16,288,256]{2,1,0:T(8,128)(2,1)}), bf16[16,288,256]{2,1,0:T(8,128)(2,1)S(1)}, u32[]{:S(2)}, u32[]{:S(2)}) async-start(bf16[16,288,256]{2,1,0:T(8,128)(2,1)} %split.1), calls=%async_computation | async-start | bytes 4718592 | tf_op jit(solution)/shard_map/all_to_all | solution.py:282
  11.7 20.6 %all-gather = s32[16,1,16]{2,1,0:T(1,128)S(1)} all-gather(s32[1,1,16]{2,1,0:T(1,128)S(1)} %bitcast.41), channel_id=1, replica_groups=mesh['frame'=16,'tok'=16] {'frame'}, dimensions={0}, use_global_device_ids=true | all-gather | bytes 1088 | tf_op jit(solution)/shard_map/all_gather | solution.py:285
  32.3 0.1 copy.36
  32.4 0.1 multiply_reduce_fusion
  32.5 0.1 multiply_reduce_fusion.2
  32.6 0.1 broadcast_add_fusion
  32.7 1.0 select_reduce_fusion
  33.7 0.1 compare_select_fusion
  33.8 0.2 copy.37
  34.0 0.2 select_n.62.idx_ref
  34.2 0.1 fusion.1
  34.3 0.1 select_n.64.idx_ref
  34.4 8.9 %all-to-all-done.r_ref.refs_0_.refs_1_ = bf16[16,288,256]{2,1,0:T(8,128)(2,1)S(1)} async-done(((bf16[16,288,256]{2,1,0:T(8,128)(2,1)}), bf16[16,288,256]{2,1,0:T(8,128)(2,1)S(1)}, u32[]{:S(2)}, u32[]{:S(2)}) %all-to-all-start) | async-done | bytes 2359328 | tf_op jit(solution)/shard_map/all_to_all | solution.py:282
  43.3 8.0 %picked_attention.1 = (bf16[768,144]{1,0:T(8,128)(2,1)}, bf16[4096,72]{1,0:T(8,128)(2,1)}, bf16[80,4096]{1,0:T(8,128)(2,1)}) custom-call(s32[1,768]{1,0:T(1,128)S(1)} %select_n.62.idx_ref, bf16[16,288,256]{2,1,0:T(8,128)(2,1)S(1)} %all-to-all-done.r_ref.refs_0_.refs_1_), custom_call_target="tpu_custom_call" | custom-call | tf_op jit(solution)/shard_map/picked_attention/pallas_call | solution.py:318
  51.4 3.7 %all-to-all-start.1 = ((bf16[16,48,144]{2,1,0:T(8,128)(2,1)}), bf16[16,48,144]{2,1,0:T(8,128)(2,1)S(1)}, u32[]{:S(2)}, u32[]{:S(2)}) async-start(bf16[16,48,144]{2,1,0:T(8,128)(2,1)} %bitcast.38), calls=%async_computation.1 | async-start | bytes 786432 | tf_op jit(solution)/shard_map/all_to_all | solution.py:326
  55.2 8.3 %main_attention.3.refs_4_ = bf16[16,144,256]{2,1,0:T(8,128)(2,1)} custom-call(bf16[16,288,256]{2,1,0:T(8,128)(2,1)} %copy-done.2, bf16[16,288,256]{2,1,0:T(8,128)(2,1)} %copy-done.2, bf16[4096,72]{1,0:T(8,128)(2,1)} %get-tuple-element.17.refs_2_, bf16[80,4096]{1,0:T(8,128)(2,1)} %get-tuple-element.18.refs_3_), custom_call_target="tpu_custom_call" | custom-call | flops 5368709120 | bytes 2097152 | tf_op jit(solution)/shard_map/main_attention/pallas_call | solution.py:150
  63.5 1.6 normed.1
  65.1 11.9 %all-to-all-start.2 = ((bf16[16,3,1152]{2,1,0:T(4,128)(2,1)}), bf16[16,3,1152]{2,1,0:T(4,128)(2,1)S(1)}, u32[]{:S(2)}, u32[]{:S(2)}) async-start(bf16[16,3,1152]{2,1,0:T(4,128)(2,1)} %normed.1), calls=%async_computation.2 | async-start | bytes 294912 | tf_op jit(solution)/shard_map/all_to_all | solution.py:332
  77.0 9.3 %main_attention.4.refs_4_ = bf16[16,144,256]{2,1,0:T(8,128)(2,1)} custom-call(bf16[16,288,256]{2,1,0:T(8,128)(2,1)} %copy-done.2, bf16[16,288,256]{2,1,0:T(8,128)(2,1)} %copy-done.2, bf16[4096,72]{1,0:T(8,128)(2,1)} %get-tuple-element.17.refs_2_, bf16[80,4096]{1,0:T(8,128)(2,1)} %get-tuple-element.18.refs_3_, ...), custom_call_target="tpu_custom_call", output_to_operand_aliasing={{}: (4, {})} | custom-call | flops 6442450944 | bytes 2097152 | tf_op jit(solution)/shard_map/main_attention/pallas_call | solution.py:150
  86.4 1.0 compact.1
  87.4 6.3 %all-to-all-start.3 = ((bf16[16,16,1152]{2,1,0:T(8,128)(2,1)}), bf16[16,16,1152]{2,1,0:T(8,128)(2,1)S(1)}, u32[]{:S(2)}, u32[]{:S(2)}) async-start(bf16[16,16,1152]{2,1,0:T(8,128)(2,1)} %compact.1), calls=%async_computation.3 | async-start | bytes 1179648 | tf_op jit(solution)/shard_map/all_to_all | solution.py:338
  93.7 0.1 select_reduce_fusion.1
  93.8 1.2 copy.38
  95.1 1.3 copy.39
  96.3 8.1 %main_attention.5._ = bf16[16,144,256]{2,1,0:T(8,128)(2,1)} custom-call(bf16[16,288,256]{2,1,0:T(8,128)(2,1)} %copy-done.2, bf16[16,288,256]{2,1,0:T(8,128)(2,1)} %copy-done.2, bf16[4096,72]{1,0:T(8,128)(2,1)} %get-tuple-element.17.refs_2_, bf16[80,4096]{1,0:T(8,128)(2,1)} %get-tuple-element.18.refs_3_, ...), custom_call_target="tpu_custom_call", output_to_operand_aliasing={{}: (4, {})} | custom-call | flops 5368709120 | bytes 2097152 | tf_op jit(solution)/shard_map/main_attention/pallas_call | solution.py:150
  104.5 0.6 broadcast_in_dim.81.router_ref
  105.1 4.2 %expert.1 = (bf16[16,144,256]{2,1,0:T(8,128)(2,1)}, f32[8,256]{1,0:T(8,128)}) custom-call(bf16[256,1152]{1,0:T(8,128)(2,1)S(1)} %bitcast.24, bf16[1152,288]{1,0:T(8,128)(2,1)} %bitcast.29, f32[1,288]{1,0:T(1,128)} %be_ref.1, bf16[16,72,288]{2,1,0:T(8,128)(2,1)} %bitcast.30, ...), custom_call_target="tpu_custom_call", output_to_operand_aliasing={{0}: (5, {})} | custom-call | tf_op jit(solution)/shard_map/expert/pallas_call | solution.py:342
  109.3 6.8 %all-to-all-start.4 = ((bf16[16,144,256]{2,1,0:T(8,128)(2,1)}), bf16[16,144,256]{2,1,0:T(8,128)(2,1)S(1)}, u32[]{:S(2)}, u32[]{:S(2)}) async-start(bf16[16,144,256]{2,1,0:T(8,128)(2,1)} %get-tuple-element.25), calls=%async_computation.4 | async-start | bytes 2359296 | tf_op jit(solution)/shard_map/all_to_all | solution.py:359
  116.1 0.1 add_select_fusion
  116.2 0.9 reshape.300.idx_ref
  117.1 0.1 reshape_squeeze.3
  117.2 0.7 copy.40.rb_ref
  117.9 0.1 iota_compare_fusion.1
  118.0 0.2 lt.117
  118.2 0.6 broadcast.169
  118.8 0.7 reduce.5
  119.5 0.2 squeeze.33
  119.7 13.2 %all-to-all-done.4.x_ref.o_ref = bf16[16,144,256]{2,1,0:T(8,128)(2,1)S(1)} async-done(((bf16[16,144,256]{2,1,0:T(8,128)(2,1)}), bf16[16,144,256]{2,1,0:T(8,128)(2,1)S(1)}, u32[]{:S(2)}, u32[]{:S(2)}) %all-to-all-start.4) | async-done | bytes 1179680 | tf_op jit(solution)/shard_map/all_to_all | solution.py:359
  132.9 2.4 %weighted.1 = bf16[768,72]{1,0:T(8,128)(2,1)} custom-call(bf16[16,144,256]{2,1,0:T(8,128)(2,1)S(1)} %all-to-all-done.4.x_ref.o_ref, f32[8,256]{1,0:T(8,128)} %get-tuple-element.26.gate_ref, f32[72,1]{1,0:T(8,128)} %copy.40.rb_ref, s32[768,1]{1,0:T(8,128)} %reshape.300.idx_ref), custom_call_target="tpu_custom_call" | custom-call | tf_op jit(solution)/shard_map/weighted/pallas_call | solution.py:360
  135.3 10.1 %all-to-all-start.5 = ((bf16[16,48,72]{2,1,0:T(8,128)(2,1)}), bf16[16,48,72]{2,1,0:T(8,128)(2,1)S(1)}, u32[]{:S(2)}, u32[]{:S(2)}) async-start(bf16[16,48,72]{2,1,0:T(8,128)(2,1)} %bitcast.33), calls=%async_computation.5 | async-start | bytes 393216 | tf_op jit(solution)/shard_map/all_to_all | solution.py:361
  145.5 0.8 broadcast_select_fusion.idx_ref
  146.3 9.5 %all-to-all-done.5 = bf16[16,48,72]{2,1,0:T(8,128)(2,1)S(1)} async-done(((bf16[16,48,72]{2,1,0:T(8,128)(2,1)}), bf16[16,48,72]{2,1,0:T(8,128)(2,1)S(1)}, u32[]{:S(2)}, u32[]{:S(2)}) %all-to-all-start.5) | async-done | bytes 110624 | tf_op jit(solution)/shard_map/all_to_all | solution.py:361
  155.8 3.7 %scatter.1 = bf16[16,72,256]{2,1,0:T(8,128)(2,1)} custom-call(bf16[768,72]{1,0:T(8,128)(2,1)S(1)} %bitcast.25, s32[768,1]{1,0:T(8,128)} %broadcast_select_fusion.idx_ref), custom_call_target="tpu_custom_call" | custom-call | tf_op jit(solution)/shard_map/scatter/pallas_call | solution.py:365
  159.5 3.6 %all-to-all-start.6 = ((bf16[16,72,256]{2,1,0:T(8,128)(2,1)}), bf16[16,72,256]{2,1,0:T(8,128)(2,1)S(1)}, u32[]{:S(2)}, u32[]{:S(2)}) async-start(bf16[16,72,256]{2,1,0:T(8,128)(2,1)} %scatter.1), calls=%async_computation.6 | async-start | bytes 1179648 | tf_op jit(solution)/shard_map/all_to_all | solution.py:366
  163.1 4.8 %residual.1.res_ref = bf16[256,1152]{1,0:T(8,128)(2,1)} custom-call(bf16[16,144,256]{2,1,0:T(8,128)(2,1)} %copy-done.1, bf16[256,1152]{1,0:T(8,128)(2,1)} %bitcast.32, bf16[1152,1152]{1,0:T(8,128)(2,1)} %w_ref.3, f32[1,1152]{1,0:T(1,128)} %copy-done.4, f32[4,1152]{1,0:T(4,128)} %bitcast.26), custom_call_target="tpu_custom_call" | custom-call | tf_op jit(solution)/shard_map/residual/pallas_call | solution.py:362
  167.8 7.7 %all-to-all-done.6.m_ref = bf16[16,72,256]{2,1,0:T(8,128)(2,1)S(1)} async-done(((bf16[16,72,256]{2,1,0:T(8,128)(2,1)}), bf16[16,72,256]{2,1,0:T(8,128)(2,1)S(1)}, u32[]{:S(2)}, u32[]{:S(2)}) %all-to-all-start.6) | async-done | bytes 589856 | tf_op jit(solution)/shard_map/all_to_all | solution.py:366
  175.6 2.3 %final.1 = bf16[256,1152]{1,0:T(8,128)(2,1)} custom-call(bf16[16,72,256]{2,1,0:T(8,128)(2,1)S(1)} %all-to-all-done.6.m_ref, bf16[256,1152]{1,0:T(8,128)(2,1)} %residual.1.res_ref, f32[4,1152]{1,0:T(4,128)} %bitcast.27), custom_call_target="tpu_custom_call" | custom-call | tf_op jit(solution)/shard_map/final/pallas_call | solution.py:367
  (36 shorter events, 0.1 us)
Async XLA Ops:
  3.9 7.7 %copy-start.10 = (s32[16,1]{0,1:T(1,128)S(1)}, s32[16,1]{0,1:T(1,128)}, u32[]{:S(2)}) copy-start(s32[16,1]{0,1:T(1,128)} %param.26) | copy-start | bytes 196
  3.9 28.8 %copy-start.8 = (s32[16,1,48]{2,1,0:T(1,128)S(1)}, s32[16,1,48]{2,1,0:T(1,128)}, u32[]{:S(2)}) copy-start(s32[16,1,48]{2,1,0:T(1,128)} %param.27) | copy-start | bytes 9220
  3.9 30.3 %copy-start.9 = (f32[1152]{0:T(1024)S(1)}, f32[1152]{0:T(1024)}, u32[]{:S(2)}) copy-start(f32[1152]{0:T(1024)} %param.20) | copy-start | bytes 13828
  3.9 39.4 %all-to-all-start = ((bf16[16,288,256]{2,1,0:T(8,128)(2,1)}), bf16[16,288,256]{2,1,0:T(8,128)(2,1)S(1)}, u32[]{:S(2)}, u32[]{:S(2)}) async-start(bf16[16,288,256]{2,1,0:T(8,128)(2,1)} %split.1), calls=%async_computation | async-start | bytes 4718592 | tf_op jit(solution)/shard_map/all_to_all | solution.py:282
  34.2 29.2 %copy-start.4 = (f32[1,1152]{1,0:T(1,128)}, f32[1,1152]{1,0:T(1,128)S(1)}, u32[]{:S(2)}) copy-start(f32[1,1152]{1,0:T(1,128)S(1)} %broadcast_in_dim.47.b_ref) | copy-start | bytes 13828
  43.3 8.0 %copy-start.2 = (bf16[16,288,256]{2,1,0:T(8,128)(2,1)}, bf16[16,288,256]{2,1,0:T(8,128)(2,1)S(1)}, u32[]{:S(2)}) copy-start(bf16[16,288,256]{2,1,0:T(8,128)(2,1)S(1)} %all-to-all-done.r_ref.refs_0_.refs_1_) | copy-start | bytes 7077892
  51.4 12.1 %all-to-all-start.1 = ((bf16[16,48,144]{2,1,0:T(8,128)(2,1)}), bf16[16,48,144]{2,1,0:T(8,128)(2,1)S(1)}, u32[]{:S(2)}, u32[]{:S(2)}) async-start(bf16[16,48,144]{2,1,0:T(8,128)(2,1)} %bitcast.38), calls=%async_computation.1 | async-start | bytes 786432 | tf_op jit(solution)/shard_map/all_to_all | solution.py:326
  55.1 8.3 %copy-start = (bf16[1152,1152]{1,0:T(8,128)(2,1)S(1)}, bf16[1152,1152]{1,0:T(8,128)(2,1)}, u32[]{:S(2)}) copy-start(bf16[1152,1152]{1,0:T(8,128)(2,1)} %w_ref.3) | copy-start | bytes 7962628
  55.1 8.3 %copy-start.3 = (f32[1,4,1152]{2,1,0:T(4,128)S(1)}, f32[1,4,1152]{2,1,0:T(4,128)}, u32[]{:S(2)}) copy-start(f32[1,4,1152]{2,1,0:T(4,128)} %param.18) | copy-start | bytes 55300
  65.1 21.3 %all-to-all-start.2 = ((bf16[16,3,1152]{2,1,0:T(4,128)(2,1)}), bf16[16,3,1152]{2,1,0:T(4,128)(2,1)S(1)}, u32[]{:S(2)}, u32[]{:S(2)}) async-start(bf16[16,3,1152]{2,1,0:T(4,128)(2,1)} %normed.1), calls=%async_computation.2 | async-start | bytes 294912 | tf_op jit(solution)/shard_map/all_to_all | solution.py:332
  86.3 7.4 %copy-start.7 = (bf16[1152,16]{0,1:T(8,128)(2,1)S(1)}, bf16[1152,16]{0,1:T(8,128)(2,1)}, u32[]{:S(2)}) copy-start(bf16[1152,16]{0,1:T(8,128)(2,1)} %param.21) | copy-start | bytes 110596
  86.3 7.5 %copy-start.5 = (bf16[1,1152,288]{1,2,0:T(8,128)(2,1)S(1)}, bf16[1,1152,288]{1,2,0:T(8,128)(2,1)}, u32[]{:S(2)}) copy-start(bf16[1,1152,288]{1,2,0:T(8,128)(2,1)} %param.22) | copy-start | bytes 1990660
  87.4 7.7 %copy-start.6 = (bf16[1,288,1152]{2,1,0:T(8,128)(2,1)S(1)}, bf16[1,288,1152]{2,1,0:T(8,128)(2,1)}, u32[]{:S(2)}) copy-start(bf16[1,288,1152]{2,1,0:T(8,128)(2,1)} %param.24) | copy-start | bytes 1990660
  87.4 17.1 %all-to-all-start.3 = ((bf16[16,16,1152]{2,1,0:T(8,128)(2,1)}), bf16[16,16,1152]{2,1,0:T(8,128)(2,1)S(1)}, u32[]{:S(2)}, u32[]{:S(2)}) async-start(bf16[16,16,1152]{2,1,0:T(8,128)(2,1)} %compact.1), calls=%async_computation.3 | async-start | bytes 1179648 | tf_op jit(solution)/shard_map/all_to_all | solution.py:338
  109.3 7.8 %copy-start.11 = (f32[1,1152]{1,0:T(1,128)S(1)}, f32[1,1152]{1,0:T(1,128)}, u32[]{:S(2)}) copy-start(f32[1,1152]{1,0:T(1,128)} %param.25) | copy-start | bytes 13828
  109.3 23.6 %all-to-all-start.4 = ((bf16[16,144,256]{2,1,0:T(8,128)(2,1)}), bf16[16,144,256]{2,1,0:T(8,128)(2,1)S(1)}, u32[]{:S(2)}, u32[]{:S(2)}) async-start(bf16[16,144,256]{2,1,0:T(8,128)(2,1)} %get-tuple-element.25), calls=%async_computation.4 | async-start | bytes 2359296 | tf_op jit(solution)/shard_map/all_to_all | solution.py:359
  132.9 13.3 %copy-start.1 = (bf16[16,144,256]{2,1,0:T(8,128)(2,1)}, bf16[16,144,256]{2,1,0:T(8,128)(2,1)S(1)}, u32[]{:S(2)}) copy-start(bf16[16,144,256]{2,1,0:T(8,128)(2,1)S(1)} %all-to-all-done.4.x_ref.o_ref) | copy-start | bytes 3538948
  135.3 20.5 %all-to-all-start.5 = ((bf16[16,48,72]{2,1,0:T(8,128)(2,1)}), bf16[16,48,72]{2,1,0:T(8,128)(2,1)S(1)}, u32[]{:S(2)}, u32[]{:S(2)}) async-start(bf16[16,48,72]{2,1,0:T(8,128)(2,1)} %bitcast.33), calls=%async_computation.5 | async-start | bytes 393216 | tf_op jit(solution)/shard_map/all_to_all | solution.py:361
  159.5 16.1 %all-to-all-start.6 = ((bf16[16,72,256]{2,1,0:T(8,128)(2,1)}), bf16[16,72,256]{2,1,0:T(8,128)(2,1)S(1)}, u32[]{:S(2)}, u32[]{:S(2)}) async-start(bf16[16,72,256]{2,1,0:T(8,128)(2,1)} %scatter.1), calls=%async_computation.6 | async-start | bytes 1179648 | tf_op jit(solution)/shard_map/all_to_all | solution.py:366

commit v3 on v2

--- a/solution.py
+++ b/solution.py
@@ -39,16 +39,31 @@
 TILES = [(w * 256, min(256, D - w * 256)) for w in range(5)]
 
 
-def split_kernel(k_ref, v_ref, q_ref, s_ref, out_ref):
-    for i, ref in enumerate((k_ref, v_ref, q_ref, s_ref)):
+def copy(source, target, sem):
+    return pltpu.make_async_copy(source, target, sem)
+
+
+def split_kernel(k_ref, v_ref, q_ref, s_ref, out_ref, in_ref, turned_ref, in_sem, out_sem):
+    loads = [copy(ref, in_ref.at[i], in_sem.at[i]) for i, ref in enumerate((k_ref, v_ref, q_ref, s_ref))]
+    for load in loads:
+        load.start()
+    stores = []
+    for i, load in enumerate(loads):
+        load.wait()
         for start, size in TILES:
-            turned = nt(eye(size), ref[:, start : start + size])
+            turned = nt(eye(size), in_ref[i, :, start : start + size])
             for h in range(H):
                 low, high = max(h * HD, start), min((h + 1) * HD, start + size)
                 if low < high:
-                    out_ref[h, i * HD + low - h * HD : i * HD + high - h * HD, :] = turned[
+                    turned_ref[i, h, low - h * HD : high - h * HD, :] = turned[
                         low - start : high - start
                     ].astype(BF16)
+        stores.append(
+            copy(turned_ref.at[i], out_ref.at[:, i * HD : (i + 1) * HD, :], out_sem.at[i])
+        )
+        stores[-1].start()
+    for store in stores:
+        store.wait()
 
 
 def prepare(r_ref, k_ref, v_ref):
@@ -87,8 +102,13 @@
     return new_top, total
 
 
-def picked_kernel(idx_ref, r_ref, out_ref, k_ref, v_ref, s_ref, rows_ref):
+def picked_kernel(
+    idx_ref, r_ref, out_ref, keys_ref, values_ref, k_ref, v_ref, s_ref, rows_ref, done_ref, sem
+):
     prepare(r_ref, k_ref, v_ref)
+    stores = [copy(k_ref, keys_ref, sem.at[0]), copy(v_ref, values_ref, sem.at[1])]
+    for store in stores:
+        store.start()
     lines = lax.broadcasted_iota(jnp.int32, (TL, TL), 0)
     for i in range(3):
         index = idx_ref[:, i * TL : (i + 1) * TL]
@@ -104,17 +124,33 @@
         top, done = interleave(q, top, k_ref, v_ref, s_ref.at[i % 2], s_ref.at[1 - i % 2])
         if i > 0:
             both = jnp.concatenate([done, rows_ref[i - 1, HD:, :]], axis=0)
-            out_ref[(i - 1) * TL : i * TL, :] = nt(eye(TL), both).astype(BF16)
+            block = slice((i - 1) * TL, i * TL)
+            done_ref[block, :] = nt(eye(TL), both).astype(BF16)
+            stores.append(copy(done_ref.at[block, :], out_ref.at[block, :], sem.at[i + 1]))
+            stores[-1].start()
+    for store in stores:
+        store.wait()
 
 
 def main_kernel(steps, aliased, *refs):
-    first_ref, q_ref, k_ref, v_ref = refs[:4]
-    out_ref, s_ref, top_ref = refs[4 + aliased :]
+    first_ref, q_ref, keys_ref, values_ref = refs[:4]
+    out_ref, s_ref, top_ref, k_ref, v_ref, sem = refs[4 + aliased :]
     step = pl.program_id(0)
 
     @pl.when(step == 0)
     def _():
-        top, _ = interleave(first_ref[0], None, k_ref, v_ref, s_ref.at[0], None)
+        loads = [
+            copy(keys_ref.at[j * 512 : (j + 1) * 512, :], k_ref.at[j * 512 : (j + 1) * 512, :], sem.at[j])
+            for j in range(8)
+        ] + [copy(values_ref, v_ref, sem.at[8])]
+        for load in loads:
+            load.start()
+        top = None
+        for j in range(8):
+            loads[j].wait()
+            top = score_part(first_ref[0], k_ref, s_ref.at[0], j, top)
+        top = jnp.max(top, axis=0, keepdims=True)
+        loads[8].wait()
         top_ref[0] = jnp.broadcast_to(top, (8, TL))
 
     def one(now, last):
@@ -140,20 +176,23 @@
 def main_part(heads, keys, values, first, steps, before=None):
     aliased = int(before is not None)
     head_block = lambda f: pl.BlockSpec((1, HD, TL), f)
-    whole = lambda shape: pl.BlockSpec(shape, lambda i: (0, 0))
     in_specs = [
         head_block(lambda i: (first, 2, 0)),
         head_block(lambda i: (first + jnp.minimum(i + 1, steps - 1), 2, 0)),
-        whole((4096, HD)),
-        whole((80, 4096)),
-    ] + [pl.BlockSpec(memory_space=pl.ANY)] * aliased
+    ] + [pl.BlockSpec(memory_space=pl.ANY)] * (2 + aliased)
     return pl.pallas_call(
         functools.partial(main_kernel, steps, aliased),
         grid=(steps,),
         in_specs=in_specs,
         out_specs=head_block(lambda i: (first + i, 1, 0)),
         out_shape=shaped(16, 2 * HD, TL),
-        scratch_shapes=[pltpu.VMEM((2, 4096, TL), F32), pltpu.VMEM((2, 8, TL), F32)],
+        scratch_shapes=[
+            pltpu.VMEM((2, 4096, TL), F32),
+            pltpu.VMEM((2, 8, TL), F32),
+            pltpu.VMEM((4096, HD), BF16),
+            pltpu.VMEM((80, 4096), BF16),
+            pltpu.SemaphoreType.DMA((9,)),
+        ],
         input_output_aliases={4: 0} if aliased else {},
         compiler_params=pltpu.CompilerParams(vmem_limit_bytes=18 << 20),
         cost_estimate=pl.CostEstimate(
@@ -187,30 +226,56 @@
         out_ref[t] = rows
 
 
-def expert_kernel(x_ref, we_ref, be_ref, wr_ref, router_ref, _, out_ref, gate_ref):
+def expert_kernel(
+    x_ref, be_ref, router_ref, we_ref, wr_ref, _, out_ref, gate_ref, we_s, wr_s, part_ref, sem
+):
+    loads = [copy(we_ref, we_s, sem.at[0]), copy(wr_ref, wr_s, sem.at[1])]
+    for load in loads:
+        load.start()
     rows = x_ref[...]
-    hidden = jax.nn.gelu(nn(rows, we_ref[...]) + be_ref[...], approximate=True).astype(BF16)
+    router = jnp.broadcast_to(router_ref[...].astype(F32), (8, D)).astype(BF16)
+    gate_ref[...] = jax.nn.sigmoid(nt(router, rows)).astype(BF16).astype(F32)
+    loads[0].wait()
+    hidden = jax.nn.gelu(nt(rows, we_s[...]) + be_ref[...], approximate=True).astype(BF16)
+    loads[1].wait()
+    stores = []
     for c in range(16):
-        out_ref[c] = nt(wr_ref[c], hidden).astype(BF16)
-    gate_ref[...] = jax.nn.sigmoid(nt(router_ref[...], rows)).astype(BF16).astype(F32)
-
-
-def gather_kernel(x_ref, gate_ref, rb_ref, idx_ref, out_ref):
-    total = x_ref[0, :HD, :].astype(F32)
+        part_ref[c] = nt(wr_s[c], hidden).astype(BF16)
+        if c % 4 == 3:
+            block = slice(c - 3, c + 1)
+            stores.append(copy(part_ref.at[block], out_ref.at[block, :HD, :], sem.at[2 + c // 4]))
+            stores[-1].start()
+    for store in stores:
+        store.wait()
+
+
+def weighted_kernel(x_ref, gate_ref, rb_ref, idx_ref, out_ref):
+    total = x_ref[0].astype(F32)
     for t in range(1, 16):
-        total = total + x_ref[t, :HD, :].astype(F32)
+        total = total + x_ref[t].astype(F32)
     rows = (total + rb_ref[...]).astype(BF16).astype(F32)
     rows = (rows * gate_ref[0:1, :]).astype(BF16)
+    lines = lax.broadcasted_iota(jnp.int32, (TL, TL), 0)
     for i in range(3):
-        index = idx_ref[i * 256 : (i + 1) * 256, :]
-        out_ref[i * 256 : (i + 1) * 256, :] = nt(one_hot(index, 256), rows).astype(BF16)
-
-
-def scatter_kernel(p_ref, idx_ref, out_ref):
+        block = slice(i * TL, (i + 1) * TL)
+        table = (lines == idx_ref[:, block]).astype(F32).astype(BF16)
+        out_ref[block, :] = nt(eye(TL), nn(rows, table).astype(BF16)).astype(BF16)
+
+
+def scatter_kernel(p_ref, idx_ref, out_ref, mix_ref, sem):
     turned = nt(eye(HD), p_ref[...]).astype(BF16)
     index = idx_ref[...]
+    lines = lax.broadcasted_iota(jnp.int32, (TL, 768), 0)
+    stores = []
     for t in range(16):
-        out_ref[t] = nn(turned, one_hot(index, TL, t * TL)).astype(BF16)
+        table = (lines == index - t * TL).astype(F32).astype(BF16)
+        mix_ref[t] = nt(turned, table).astype(BF16)
+        if t % 4 == 3:
+            block = slice(t - 3, t + 1)
+            stores.append(copy(mix_ref.at[block], out_ref.at[block], sem.at[t // 4]))
+            stores[-1].start()
+    for store in stores:
+        store.wait()
 
 
 def residual_kernel(o_ref, s_ref, w_ref, b_ref, mod_ref, out_ref, att_ref):
@@ -225,21 +290,20 @@
     out_ref[...] = (s_ref[...].astype(F32) + mod_ref[0:1, :] * projected).astype(BF16)
 
 
-def final_kernel(m_ref, res_ref, mod_ref, out_ref, mix_ref):
-    for c in range(16):
-        mix_ref[c * HD : (c + 1) * HD, :] = m_ref[c]
-    for start, size in TILES:
-        cols = slice(start, start + size)
-        mixed = nt(eye(TL), mix_ref[cols, :])
-        out_ref[:, cols] = (
-            res_ref[:, cols].astype(F32) + mod_ref[3:4, cols] * mixed
-        ).astype(BF16)
-
-
-def call(kernel, out_shape, name, mib, scratch=()):
+def final_kernel(m_ref, res_ref, mod_ref, out_ref):
+    mixed = nt(eye(TL), m_ref[...])
+    out_ref[...] = (res_ref[...].astype(F32) + mod_ref[3:4, :] * mixed).astype(BF16)
+
+
+ANY = pl.BlockSpec(memory_space=pl.ANY)
+VMEM = pl.BlockSpec(memory_space=pltpu.VMEM)
+
+
+def call(kernel, out_shape, name, mib, scratch=(), **specs):
     return pl.pallas_call(
         kernel,
         out_shape=out_shape,
+        **specs,
         scratch_shapes=list(scratch),
         compiler_params=pltpu.CompilerParams(vmem_limit_bytes=mib << 20),
         name=name,
@@ -276,7 +340,20 @@
     mod = modulation[0]
     out_bias = output_bias[None, :]
 
-    sent = call(split_kernel, shaped(16, 4 * HD, TL), "split", 12)(
+    sent = call(
+        split_kernel,
+        shaped(16, 4 * HD, TL),
+        "split",
+        12,
+        [
+            pltpu.VMEM((4, TL, D), BF16),
+            pltpu.VMEM((4, 16, HD, TL), BF16),
+            pltpu.SemaphoreType.DMA((4,)),
+            pltpu.SemaphoreType.DMA((4,)),
+        ],
+        in_specs=[ANY] * 4,
+        out_specs=ANY,
+    )(
         *in_hbm(key_vectors[0], value_vectors[0], queries[0], stream[0])
     )
     heads = exchange(sent, "tok")
@@ -305,22 +382,35 @@
     row_id = expert_offsets[:, None] + slots[None, :]
     back_index = jnp.where(
         slots[None, :] < expert_counts[:, None], (row_id & 15) * 16 + (row_id >> 4), -1
-    ).reshape(768, 1)
-    spread_index = jnp.where(slots[None, :] < own_counts[:, None], picked, -1).reshape(768, 1)
+    ).reshape(1, 768)
+    spread_index = jnp.where(slots[None, :] < own_counts[:, None], picked, -1).reshape(1, 768)
 
     router_own = jnp.sum(
         jnp.where((frames == me_frame)[None, :], router_weight, jnp.zeros_like(router_weight)), axis=1
     )
-    router_rows = jnp.broadcast_to(router_own[None, :], (8, D))
+    router_own = router_own[None, :]
     bias_own = lax.dynamic_slice_in_dim(reduce_bias[0].reshape(16, HD), me_tok, 1, 0).reshape(HD, 1)
     reduce_turned = reduce_weight[0].T.reshape(16, HD, 288)
+    expand_turned = expand_weight[0].T
+    heads, reduce_turned, bias_own, back_index, spread_index, router_own = lax.optimization_barrier(
+        (heads, reduce_turned, bias_own, back_index, spread_index, router_own)
+    )
 
     picked_out, keys, values = call(
         picked_kernel,
         (shaped(768, 2 * HD), shaped(4096, HD), shaped(80, 4096)),
         "picked_attention",
         24,
-        [pltpu.VMEM((2, 4096, TL), F32), pltpu.VMEM((3, 2 * HD, TL), BF16)],
+        [
+            pltpu.VMEM((4096, HD), BF16),
+            pltpu.VMEM((80, 4096), BF16),
+            pltpu.VMEM((2, 4096, TL), F32),
+            pltpu.VMEM((3, 2 * HD, TL), BF16),
+            pltpu.VMEM((768, 2 * HD), BF16),
+            pltpu.SemaphoreType.DMA((5,)),
+        ],
+        in_specs=[VMEM, VMEM],
+        out_specs=(ANY, ANY, ANY),
     )(pick_index, heads)
 
     rows = exchange(picked_out.reshape(16, 48, 2 * HD), "tok")
@@ -338,35 +428,67 @@
     rows = exchange(rows, "tok")
     attended = main_part(heads, keys, values, 11, 5, attended)
     rows, attended = lax.optimization_barrier((rows, attended))
-    whole = lambda shape: pl.BlockSpec(shape, lambda i: (0,) * len(shape))
-    both, gates = pl.pallas_call(
+    both, gates = call(
         expert_kernel,
+        (shaped(16, 2 * HD, TL), shaped(8, TL, dtype=F32)),
+        "expert",
+        10,
+        [
+            pltpu.VMEM((288, D), BF16),
+            pltpu.VMEM((16, HD, 288), BF16),
+            pltpu.VMEM((16, HD, TL), BF16),
+            pltpu.SemaphoreType.DMA((6,)),
+        ],
+        in_specs=[VMEM, VMEM, VMEM, ANY, ANY, ANY],
+        out_specs=(ANY, VMEM),
+        input_output_aliases={5: 0},
+    )(
+        rows.reshape(TL, D),
+        *in_hbm(expand_bias, router_own, expand_turned, reduce_turned, attended),
+    )
+    both = exchange(both, "tok")
+    first_block = lambda *shape: pl.BlockSpec(shape, lambda i: (0,) * len(shape))
+    outs = call(
+        weighted_kernel,
+        shaped(768, HD),
+        "weighted",
+        8,
         grid=(1,),
         in_specs=[
-            whole((TL, D)),
-            whole((D, 288)),
-            whole((1, 288)),
-            whole((16, HD, 288)),
-            whole((8, D)),
-            pl.BlockSpec(memory_space=pl.ANY),
+            first_block(16, HD, TL),
+            first_block(8, TL),
+            first_block(HD, 1),
+            first_block(1, 768),
         ],
-        out_specs=(whole((16, HD, TL)), whole((8, TL))),
-        out_shape=(shaped(16, 2 * HD, TL), shaped(8, TL, dtype=F32)),
-        input_output_aliases={5: 0},
-        compiler_params=pltpu.CompilerParams(vmem_limit_bytes=12 << 20),
-        name="expert",
-    )(rows.reshape(TL, D), *in_hbm(expand_weight[0], expand_bias, reduce_turned, router_rows, attended))
-    both = exchange(both, "tok")
-    outs = call(gather_kernel, shaped(768, HD), "weighted", 8)(both, *in_hbm(gates, bias_own, back_index))
+        out_specs=first_block(768, HD),
+    )(both, *in_hbm(gates, bias_own, back_index))
     outs = exchange(outs.reshape(16, 48, HD), "frame")
     residual = call(residual_kernel, shaped(TL, D), "residual", 12, [pltpu.VMEM((D, TL), BF16)])(
         *in_hbm(both, stream[0], output_weight, out_bias, mod)
     )
-    mixed = call(scatter_kernel, shaped(16, HD, TL), "scatter", 8)(outs.reshape(768, HD), *in_hbm(spread_index))
+    mixed = call(
+        scatter_kernel,
+        shaped(16, HD, TL),
+        "scatter",
+        8,
+        [pltpu.VMEM((16, HD, TL), BF16), pltpu.SemaphoreType.DMA((4,))],
+        in_specs=[VMEM, VMEM],
+        out_specs=ANY,
+    )(outs.reshape(768, HD), *in_hbm(spread_index))
     mixed = exchange(mixed, "tok")
-    layer_out = call(final_kernel, shaped(TL, D), "final", 8, [pltpu.VMEM((D, TL), BF16)])(
-        mixed, *in_hbm(residual, mod)
-    )
+    layer_out = call(
+        final_kernel,
+        shaped(TL, D),
+        "final",
+        8,
+        grid=(3,),
+        in_specs=[
+            pl.BlockSpec((384, TL), lambda i: (i, 0)),
+            pl.BlockSpec((TL, 384), lambda i: (0, i)),
+            pl.BlockSpec((4, 384), lambda i: (0, i)),
+        ],
+        out_specs=pl.BlockSpec((TL, 384), lambda i: (0, i)),
+    )(mixed.reshape(D, TL), *in_hbm(residual, mod))
     return layer_out[None]
 
 

time: 179 us -> 181 us (1.011)
  blocking collectives: 20.6 us -> 41.1 us
  starting transfers between devices: 50.2 us -> 39.1 us
  waiting for transfers between devices: 39.4 us -> 28.7 us
  Pallas kernels: 57.7 us -> 63.3 us
    all_to_all x0 -> x1, blocking collectives: none -> 20.5 us  [per_device(): outs = exchange(outs.reshape(16, 48, HD), 'frame')]
    all_to_all x1 -> x0, starting transfers between devices: 10.1 us -> none  [per_device(): outs = exchange(outs.reshape(16, 48, HD), 'frame')]
    all_to_all x1 -> x0, waiting for transfers between devices: 9.52 us -> none  [per_device(): outs = exchange(outs.reshape(16, 48, HD), 'frame')]
    pallas_call x3, Pallas kernels: 25.8 us -> 30.9 us  [main_part(): pl.pallas_call(functools.partial(main_kernel, steps, aliased), grid=(step...]
    all_to_all x1, waiting for transfers between devices: 8.91 us -> 3.99 us  [per_device(): heads = exchange(sent, 'tok')]
    all_to_all x1, waiting for transfers between devices: 13.2 us -> 16.1 us  [per_device(): both = exchange(both, 'tok')]
  transfers between devices with their start and end apart: 7 -> 6, of which waited for: 4 -> 4; matrix products, arithmetic and copies ran while one was open for 5% -> 4% of each run, Pallas kernels for 17% -> 20%
where the time goes in v3:
time: 181 us; the launch traced here: 180 us
  Pallas kernels  63.3 us (35%)
  blocking collectives  41.1 us (23%)
  starting transfers between devices  39.1 us (22%)
  waiting for transfers between devices  28.7 us (16%)
  local copies, waits for them, and re-layouts  4.63 us (3%)
  other arithmetic  3.06 us (2%)
    pallas_call x3, Pallas kernels, main_part(): pl.pallas_call(functools.partial(main_kernel, steps, aliased), grid=(step...  30.9 us
    all_gather x1, blocking collectives, per_device(): all_counts = lax.all_gather(own_counts, 'frame', axis=1)  20.6 us
    all_to_all x1, blocking collectives, per_device(): outs = exchange(outs.reshape(16, 48, HD), 'frame')  20.5 us
    all_to_all x1, waiting for transfers between devices, per_device(): both = exchange(both, 'tok')  16.1 us
    all_to_all x1, starting transfers between devices, per_device(): normed = exchange(normed, 'frame')  11.4 us
    pallas_call x1, Pallas kernels, per_device(): call(picked_kernel, (shaped(768, 2 * HD), shaped(4096, HD), shaped(80, 40...  7.99 us
    all_to_all x1, waiting for transfers between devices, per_device(): mixed = exchange(mixed, 'tok')  7.73 us
    all_to_all x1, starting transfers between devices, per_device(): heads = exchange(sent, 'tok')  7.72 us
  transfers between devices with their start and end apart: 6, of which 4 were waited for; matrix products, arithmetic and copies ran while one was open for 4% of the time, Pallas kernels for 20%

profile of v3, /device:TPU:1, one launch (start us, length us, event | category | flops | bytes accessed | tf_op | source)
XLA Modules:
  0.0 180.2 jit_solution(13102452046550783447)
XLA Ops:
  0.0 3.4 %split.1 = bf16[16,288,256]{2,1,0:T(8,128)(2,1)} custom-call(bf16[256,1152]{1,0:T(8,128)(2,1)} %bitcast.39, bf16[256,1152]{1,0:T(8,128)(2,1)} %bitcast.40, bf16[256,1152]{1,0:T(8,128)(2,1)} %bitcast.41, bf16[256,1152]{1,0:T(8,128)(2,1)} %bitcast.34), custom_call_target="tpu_custom_call" | custom-call | tf_op jit(solution)/shard_map/split/pallas_call | solution.py:343
  3.5 0.0 copy-start.9
  3.5 7.7 %all-to-all-start = ((bf16[16,288,256]{2,1,0:T(8,128)(2,1)}), bf16[16,288,256]{2,1,0:T(8,128)(2,1)S(1)}, u32[]{:S(2)}, u32[]{:S(2)}) async-start(bf16[16,288,256]{2,1,0:T(8,128)(2,1)} %split.1), calls=%async_computation | async-start | bytes 4718592 | tf_op jit(solution)/shard_map/all_to_all | solution.py:359
  11.3 0.1 iota_compare_fusion.1
  11.4 0.1 select_reduce_fusion.1
  11.5 0.1 lt.114
  11.6 0.6 broadcast_in_dim.77.router_ref
  12.2 0.5 broadcast.168
  12.7 0.7 reduce.5
  13.4 0.1 squeeze.30
  13.5 0.1 reshape_squeeze.3
  13.6 20.6 %all-gather = s32[16,1,16]{2,1,0:T(1,128)S(1)} all-gather(s32[1,1,16]{2,1,0:T(1,128)S(1)} %bitcast.46), channel_id=1, replica_groups=mesh['frame'=16,'tok'=16] {'frame'}, dimensions={0}, use_global_device_ids=true | all-gather | bytes 1088 | tf_op jit(solution)/shard_map/all_gather | solution.py:362
  34.2 0.1 copy.27
  34.3 0.1 multiply_reduce_fusion
  34.4 0.1 multiply_reduce_fusion.1
  34.5 0.1 fusion.1
  34.6 0.1 select_n.68.idx_ref
  34.7 0.1 add_select_fusion
  34.8 0.7 reshape.298.idx_ref
  35.5 0.1 broadcast_add_fusion
  35.5 1.0 select_reduce_fusion
  36.6 0.1 compare_select_fusion
  36.7 0.2 copy.28
  36.8 0.2 select_n.62.idx_ref
  37.1 1.3 copy.29
  38.3 0.6 broadcast_select_fusion.idx_ref
  38.9 4.0 %all-to-all-done.r_ref.refs_0_.refs_1_ = bf16[16,288,256]{2,1,0:T(8,128)(2,1)S(1)} async-done(((bf16[16,288,256]{2,1,0:T(8,128)(2,1)}), bf16[16,288,256]{2,1,0:T(8,128)(2,1)S(1)}, u32[]{:S(2)}, u32[]{:S(2)}) %all-to-all-start) | async-done | bytes 2359328 | tf_op jit(solution)/shard_map/all_to_all | solution.py:359
  42.9 8.0 %picked_attention.1 = (bf16[768,144]{1,0:T(8,128)(2,1)}, bf16[4096,72]{1,0:T(8,128)(2,1)}, bf16[80,4096]{1,0:T(8,128)(2,1)}) custom-call(s32[1,768]{1,0:T(1,128)S(1)} %select_n.62.idx_ref, bf16[16,288,256]{2,1,0:T(8,128)(2,1)S(1)} %all-to-all-done.r_ref.refs_0_.refs_1_), custom_call_target="tpu_custom_call" | custom-call | tf_op jit(solution)/shard_map/picked_attention/pallas_call | solution.py:399
  50.9 3.7 %all-to-all-start.1 = ((bf16[16,48,144]{2,1,0:T(8,128)(2,1)}), bf16[16,48,144]{2,1,0:T(8,128)(2,1)S(1)}, u32[]{:S(2)}, u32[]{:S(2)}) async-start(bf16[16,48,144]{2,1,0:T(8,128)(2,1)} %bitcast.42), calls=%async_computation.1 | async-start | bytes 786432 | tf_op jit(solution)/shard_map/all_to_all | solution.py:416
  54.7 10.0 %main_attention.3.refs_4_ = bf16[16,144,256]{2,1,0:T(8,128)(2,1)} custom-call(bf16[16,288,256]{2,1,0:T(8,128)(2,1)} %copy-done.2, bf16[16,288,256]{2,1,0:T(8,128)(2,1)} %copy-done.2, bf16[4096,72]{1,0:T(8,128)(2,1)} %get-tuple-element.24.refs_2_, bf16[80,4096]{1,0:T(8,128)(2,1)} %get-tuple-element.25.refs_3_), custom_call_target="tpu_custom_call" | custom-call | flops 5368709120 | bytes 2097152 | tf_op jit(solution)/shard_map/main_attention/pallas_call | solution.py:183
  64.8 1.6 normed.1
  66.4 11.4 %all-to-all-start.2 = ((bf16[16,3,1152]{2,1,0:T(4,128)(2,1)}), bf16[16,3,1152]{2,1,0:T(4,128)(2,1)S(1)}, u32[]{:S(2)}, u32[]{:S(2)}) async-start(bf16[16,3,1152]{2,1,0:T(4,128)(2,1)} %normed.1), calls=%async_computation.2 | async-start | bytes 294912 | tf_op jit(solution)/shard_map/all_to_all | solution.py:422
  77.8 11.0 %main_attention.4.refs_4_ = bf16[16,144,256]{2,1,0:T(8,128)(2,1)} custom-call(bf16[16,288,256]{2,1,0:T(8,128)(2,1)} %copy-done.2, bf16[16,288,256]{2,1,0:T(8,128)(2,1)} %copy-done.2, bf16[4096,72]{1,0:T(8,128)(2,1)} %get-tuple-element.24.refs_2_, bf16[80,4096]{1,0:T(8,128)(2,1)} %get-tuple-element.25.refs_3_, ...), custom_call_target="tpu_custom_call", output_to_operand_aliasing={{}: (4, {})} | custom-call | flops 6442450944 | bytes 2097152 | tf_op jit(solution)/shard_map/main_attention/pallas_call | solution.py:183
  88.8 1.0 compact.1
  89.8 6.7 %all-to-all-start.3 = ((bf16[16,16,1152]{2,1,0:T(8,128)(2,1)}), bf16[16,16,1152]{2,1,0:T(8,128)(2,1)S(1)}, u32[]{:S(2)}, u32[]{:S(2)}) async-start(bf16[16,16,1152]{2,1,0:T(8,128)(2,1)} %compact.1), calls=%async_computation.3 | async-start | bytes 1179648 | tf_op jit(solution)/shard_map/all_to_all | solution.py:428
  96.6 9.9 %main_attention.5._ = bf16[16,144,256]{2,1,0:T(8,128)(2,1)} custom-call(bf16[16,288,256]{2,1,0:T(8,128)(2,1)} %copy-done.2, bf16[16,288,256]{2,1,0:T(8,128)(2,1)} %copy-done.2, bf16[4096,72]{1,0:T(8,128)(2,1)} %get-tuple-element.24.refs_2_, bf16[80,4096]{1,0:T(8,128)(2,1)} %get-tuple-element.25.refs_3_, ...), custom_call_target="tpu_custom_call", output_to_operand_aliasing={{}: (4, {})} | custom-call | flops 5368709120 | bytes 2097152 | tf_op jit(solution)/shard_map/main_attention/pallas_call | solution.py:183
  106.4 0.8 all-to-all-done.3
  107.3 4.9 %expert.1 = (bf16[16,144,256]{2,1,0:T(8,128)(2,1)}, f32[8,256]{1,0:T(8,128)}) custom-call(bf16[256,1152]{1,0:T(8,128)(2,1)S(1)} %bitcast.27, f32[1,288]{1,0:T(1,128)} %be_ref.1, bf16[1,1152]{1,0:T(2,128)(2,1)} %broadcast_in_dim.77.router_ref, bf16[288,1152]{1,0:T(8,128)(2,1)} %bitcast.38, ...), custom_call_target="tpu_custom_call", output_to_operand_aliasing={{0}: (5, {})} | custom-call | tf_op jit(solution)/shard_map/expert/pallas_call | solution.py:431
  112.1 5.9 %all-to-all-start.4 = ((bf16[16,144,256]{2,1,0:T(8,128)(2,1)}), bf16[16,144,256]{2,1,0:T(8,128)(2,1)S(1)}, u32[]{:S(2)}, u32[]{:S(2)}) async-start(bf16[16,144,256]{2,1,0:T(8,128)(2,1)} %get-tuple-element.34), calls=%async_computation.4 | async-start | bytes 2359296 | tf_op jit(solution)/shard_map/all_to_all | solution.py:449
  118.0 0.7 copy.30.rb_ref
  118.7 16.1 %all-to-all-done.4.x_ref.o_ref = bf16[16,144,256]{2,1,0:T(8,128)(2,1)S(1)} async-done(((bf16[16,144,256]{2,1,0:T(8,128)(2,1)}), bf16[16,144,256]{2,1,0:T(8,128)(2,1)S(1)}, u32[]{:S(2)}, u32[]{:S(2)}) %all-to-all-start.4) | async-done | bytes 1179680 | tf_op jit(solution)/shard_map/all_to_all | solution.py:449
  134.9 2.1 %weighted.1 = bf16[768,72]{1,0:T(8,128)(2,1)} custom-call(bf16[16,144,256]{2,1,0:T(8,128)(2,1)S(1)} %all-to-all-done.4.x_ref.o_ref, f32[8,256]{1,0:T(8,128)} %get-tuple-element.35.gate_ref, f32[72,1]{1,0:T(8,128)} %copy.30.rb_ref, s32[1,768]{1,0:T(1,128)} %reshape.298.idx_ref), custom_call_target="tpu_custom_call" | custom-call | tf_op jit(solution)/shard_map/weighted/pallas_call | solution.py:451
  136.9 20.5 %all_to_all.35 = bf16[16,48,72]{2,1,0:T(8,128)(2,1)S(1)} all-to-all(bf16[16,48,72]{2,1,0:T(8,128)(2,1)} %bitcast.36), channel_id=1, replica_groups=mesh['frame'=16,'tok'=16] {'frame'}, dimensions={0} | all-to-all | bytes 221184 | tf_op jit(solution)/shard_map/all_to_all | solution.py:465
  157.4 3.5 %scatter.1 = bf16[16,72,256]{2,1,0:T(8,128)(2,1)} custom-call(bf16[768,72]{1,0:T(8,128)(2,1)S(1)} %bitcast.29, s32[1,768]{1,0:T(1,128)} %broadcast_select_fusion.idx_ref), custom_call_target="tpu_custom_call" | custom-call | tf_op jit(solution)/shard_map/scatter/pallas_call | solution.py:469
  160.9 3.6 %all-to-all-start.6 = ((bf16[16,72,256]{2,1,0:T(8,128)(2,1)}), bf16[16,72,256]{2,1,0:T(8,128)(2,1)S(1)}, u32[]{:S(2)}, u32[]{:S(2)}) async-start(bf16[16,72,256]{2,1,0:T(8,128)(2,1)} %scatter.1), calls=%async_computation.6 | async-start | bytes 1179648 | tf_op jit(solution)/shard_map/all_to_all | solution.py:478
  164.5 4.8 %residual.1.res_ref = bf16[256,1152]{1,0:T(8,128)(2,1)} custom-call(bf16[16,144,256]{2,1,0:T(8,128)(2,1)} %copy-done.1, bf16[256,1152]{1,0:T(8,128)(2,1)} %bitcast.35, bf16[1152,1152]{1,0:T(8,128)(2,1)} %w_ref.3, f32[1,1152]{1,0:T(1,128)} %copy-done.4, f32[4,1152]{1,0:T(4,128)} %bitcast.30), custom_call_target="tpu_custom_call" | custom-call | tf_op jit(solution)/shard_map/residual/pallas_call | solution.py:466
  169.3 7.7 %all-to-all-done.6 = bf16[16,72,256]{2,1,0:T(8,128)(2,1)S(1)} async-done(((bf16[16,72,256]{2,1,0:T(8,128)(2,1)}), bf16[16,72,256]{2,1,0:T(8,128)(2,1)S(1)}, u32[]{:S(2)}, u32[]{:S(2)}) %all-to-all-start.6) | async-done | bytes 589856 | tf_op jit(solution)/shard_map/all_to_all | solution.py:478
  177.0 3.1 %final.1 = bf16[256,1152]{1,0:T(8,128)(2,1)} custom-call(bf16[1152,256]{1,0:T(8,128)(2,1)S(1)} %bitcast.28, bf16[256,1152]{1,0:T(8,128)(2,1)} %residual.1.res_ref, f32[4,1152]{1,0:T(4,128)} %bitcast.31), custom_call_target="tpu_custom_call" | custom-call | tf_op jit(solution)/shard_map/final/pallas_call | solution.py:479
  (32 shorter events, 0.1 us)
Async XLA Ops:
  3.5 7.8 %copy-start.9 = (s32[16,1]{0,1:T(1,128)S(1)}, s32[16,1]{0,1:T(1,128)}, u32[]{:S(2)}) copy-start(s32[16,1]{0,1:T(1,128)} %param.26) | copy-start | bytes 196
  3.5 7.9 %copy-start.6 = (bf16[1152,16]{0,1:T(8,128)(2,1)S(1)}, bf16[1152,16]{0,1:T(8,128)(2,1)}, u32[]{:S(2)}) copy-start(bf16[1152,16]{0,1:T(8,128)(2,1)} %param.21) | copy-start | bytes 110596
  3.5 8.7 %copy-start.8 = (f32[1152]{0:T(1024)S(1)}, f32[1152]{0:T(1024)}, u32[]{:S(2)}) copy-start(f32[1152]{0:T(1024)} %param.20) | copy-start | bytes 13828
  3.5 9.2 %copy-start.7 = (s32[16,1,48]{2,1,0:T(1,128)S(1)}, s32[16,1,48]{2,1,0:T(1,128)}, u32[]{:S(2)}) copy-start(s32[16,1,48]{2,1,0:T(1,128)} %param.27) | copy-start | bytes 9220
  3.5 10.0 %copy-start.10 = (f32[1,1152]{1,0:T(1,128)S(1)}, f32[1,1152]{1,0:T(1,128)}, u32[]{:S(2)}) copy-start(f32[1,1152]{1,0:T(1,128)} %param.25) | copy-start | bytes 13828
  3.5 39.4 %all-to-all-start = ((bf16[16,288,256]{2,1,0:T(8,128)(2,1)}), bf16[16,288,256]{2,1,0:T(8,128)(2,1)S(1)}, u32[]{:S(2)}, u32[]{:S(2)}) async-start(bf16[16,288,256]{2,1,0:T(8,128)(2,1)} %split.1), calls=%async_computation | async-start | bytes 4718592 | tf_op jit(solution)/shard_map/all_to_all | solution.py:359
  11.2 25.8 %copy-start.5 = (bf16[1,288,1152]{2,1,0:T(8,128)(2,1)S(1)}, bf16[1,288,1152]{2,1,0:T(8,128)(2,1)}, u32[]{:S(2)}) copy-start(bf16[1,288,1152]{2,1,0:T(8,128)(2,1)} %param.24) | copy-start | bytes 1990660
  12.2 52.6 %copy-start.4 = (f32[1,1152]{1,0:T(1,128)}, f32[1,1152]{1,0:T(1,128)S(1)}, u32[]{:S(2)}) copy-start(f32[1,1152]{1,0:T(1,128)S(1)} %broadcast_in_dim.78.b_ref) | copy-start | bytes 13828
  42.9 8.0 %copy-start.2 = (bf16[16,288,256]{2,1,0:T(8,128)(2,1)}, bf16[16,288,256]{2,1,0:T(8,128)(2,1)S(1)}, u32[]{:S(2)}) copy-start(bf16[16,288,256]{2,1,0:T(8,128)(2,1)S(1)} %all-to-all-done.r_ref.refs_0_.refs_1_) | copy-start | bytes 7077892
  50.9 13.8 %all-to-all-start.1 = ((bf16[16,48,144]{2,1,0:T(8,128)(2,1)}), bf16[16,48,144]{2,1,0:T(8,128)(2,1)S(1)}, u32[]{:S(2)}, u32[]{:S(2)}) async-start(bf16[16,48,144]{2,1,0:T(8,128)(2,1)} %bitcast.42), calls=%async_computation.1 | async-start | bytes 786432 | tf_op jit(solution)/shard_map/all_to_all | solution.py:416
  54.7 10.1 %copy-start = (bf16[1152,1152]{1,0:T(8,128)(2,1)S(1)}, bf16[1152,1152]{1,0:T(8,128)(2,1)}, u32[]{:S(2)}) copy-start(bf16[1152,1152]{1,0:T(8,128)(2,1)} %w_ref.3) | copy-start | bytes 7962628
  54.7 10.1 %copy-start.3 = (f32[1,4,1152]{2,1,0:T(4,128)S(1)}, f32[1,4,1152]{2,1,0:T(4,128)}, u32[]{:S(2)}) copy-start(f32[1,4,1152]{2,1,0:T(4,128)} %param.18) | copy-start | bytes 55300
  66.4 22.4 %all-to-all-start.2 = ((bf16[16,3,1152]{2,1,0:T(4,128)(2,1)}), bf16[16,3,1152]{2,1,0:T(4,128)(2,1)S(1)}, u32[]{:S(2)}, u32[]{:S(2)}) async-start(bf16[16,3,1152]{2,1,0:T(4,128)(2,1)} %normed.1), calls=%async_computation.2 | async-start | bytes 294912 | tf_op jit(solution)/shard_map/all_to_all | solution.py:422
  89.8 17.4 %all-to-all-start.3 = ((bf16[16,16,1152]{2,1,0:T(8,128)(2,1)}), bf16[16,16,1152]{2,1,0:T(8,128)(2,1)S(1)}, u32[]{:S(2)}, u32[]{:S(2)}) async-start(bf16[16,16,1152]{2,1,0:T(8,128)(2,1)} %compact.1), calls=%async_computation.3 | async-start | bytes 1179648 | tf_op jit(solution)/shard_map/all_to_all | solution.py:428
  112.1 22.7 %all-to-all-start.4 = ((bf16[16,144,256]{2,1,0:T(8,128)(2,1)}), bf16[16,144,256]{2,1,0:T(8,128)(2,1)S(1)}, u32[]{:S(2)}, u32[]{:S(2)}) async-start(bf16[16,144,256]{2,1,0:T(8,128)(2,1)} %get-tuple-element.34), calls=%async_computation.4 | async-start | bytes 2359296 | tf_op jit(solution)/shard_map/all_to_all | solution.py:449
  134.9 26.0 %copy-start.1 = (bf16[16,144,256]{2,1,0:T(8,128)(2,1)}, bf16[16,144,256]{2,1,0:T(8,128)(2,1)S(1)}, u32[]{:S(2)}) copy-start(bf16[16,144,256]{2,1,0:T(8,128)(2,1)S(1)} %all-to-all-done.4.x_ref.o_ref) | copy-start | bytes 3538948
  160.9 16.1 %all-to-all-start.6 = ((bf16[16,72,256]{2,1,0:T(8,128)(2,1)}), bf16[16,72,256]{2,1,0:T(8,128)(2,1)S(1)}, u32[]{:S(2)}, u32[]{:S(2)}) async-start(bf16[16,72,256]{2,1,0:T(8,128)(2,1)} %scatter.1), calls=%async_computation.6 | async-start | bytes 1179648 | tf_op jit(solution)/shard_map/all_to_all | solution.py:478

commit v4 on v3

--- a/solution.py
+++ b/solution.py
@@ -68,7 +68,10 @@
 
 def prepare(r_ref, k_ref, v_ref):
     for j in range(16):
-        k_ref[j * TL : (j + 1) * TL, :] = nt(eye(TL), r_ref[j, :HD, :]).astype(BF16)
+        keys = nt(eye(TL), r_ref[j, :HD, :])
+        k_ref[j * TL : (j + 1) * TL, :] = jnp.concatenate(
+            [keys, jnp.zeros((TL, 128 - HD), F32)], axis=1
+        ).astype(BF16)
         v_ref[:HD, j * TL : (j + 1) * TL] = r_ref[j, HD : 2 * HD, :]
         v_ref[HD:, j * TL : (j + 1) * TL] = jnp.ones((8, TL), BF16)
 
@@ -86,6 +89,10 @@
     weights = jnp.exp((s_ref[j * TL : (j + 1) * TL, :] - top) * SCALE).astype(BF16)
     part = nn(v_ref[:, j * TL : (j + 1) * TL], weights)
     return part if total is None else total + part
+
+
+def padded(q):
+    return jnp.concatenate([q.astype(F32), jnp.zeros((128 - HD, TL), F32)], axis=0).astype(BF16)
 
 
 def interleave(q, top, k_ref, v_ref, next_ref, s_ref):
@@ -120,7 +127,7 @@
         rows_ref[i] = rows.astype(BF16)
     top = None
     for i in range(4):
-        q = rows_ref[i, :HD, :] if i < 3 else None
+        q = padded(rows_ref[i, :HD, :]) if i < 3 else None
         top, done = interleave(q, top, k_ref, v_ref, s_ref.at[i % 2], s_ref.at[1 - i % 2])
         if i > 0:
             both = jnp.concatenate([done, rows_ref[i - 1, HD:, :]], axis=0)
@@ -133,28 +140,17 @@
 
 
 def main_kernel(steps, aliased, *refs):
-    first_ref, q_ref, keys_ref, values_ref = refs[:4]
-    out_ref, s_ref, top_ref, k_ref, v_ref, sem = refs[4 + aliased :]
+    first_ref, q_ref, k_ref, v_ref = refs[:4]
+    out_ref, s_ref, top_ref = refs[4 + aliased :]
     step = pl.program_id(0)
 
     @pl.when(step == 0)
     def _():
-        loads = [
-            copy(keys_ref.at[j * 512 : (j + 1) * 512, :], k_ref.at[j * 512 : (j + 1) * 512, :], sem.at[j])
-            for j in range(8)
-        ] + [copy(values_ref, v_ref, sem.at[8])]
-        for load in loads:
-            load.start()
-        top = None
-        for j in range(8):
-            loads[j].wait()
-            top = score_part(first_ref[0], k_ref, s_ref.at[0], j, top)
-        top = jnp.max(top, axis=0, keepdims=True)
-        loads[8].wait()
+        top, _ = interleave(padded(first_ref[0]), None, k_ref, v_ref, s_ref.at[0], None)
         top_ref[0] = jnp.broadcast_to(top, (8, TL))
 
     def one(now, last):
-        q = None if last else q_ref[0]
+        q = None if last else padded(q_ref[0])
         top, done = interleave(
             q, top_ref[now, 0:1, :], k_ref, v_ref, s_ref.at[1 - now], s_ref.at[now]
         )
@@ -179,7 +175,9 @@
     in_specs = [
         head_block(lambda i: (first, 2, 0)),
         head_block(lambda i: (first + jnp.minimum(i + 1, steps - 1), 2, 0)),
-    ] + [pl.BlockSpec(memory_space=pl.ANY)] * (2 + aliased)
+        pl.BlockSpec((4096, 128), lambda i: (0, 0)),
+        pl.BlockSpec((80, 4096), lambda i: (0, 0)),
+    ] + [pl.BlockSpec(memory_space=pl.ANY)] * aliased
     return pl.pallas_call(
         functools.partial(main_kernel, steps, aliased),
         grid=(steps,),
@@ -189,9 +187,6 @@
         scratch_shapes=[
             pltpu.VMEM((2, 4096, TL), F32),
             pltpu.VMEM((2, 8, TL), F32),
-            pltpu.VMEM((4096, HD), BF16),
-            pltpu.VMEM((80, 4096), BF16),
-            pltpu.SemaphoreType.DMA((9,)),
         ],
         input_output_aliases={4: 0} if aliased else {},
         compiler_params=pltpu.CompilerParams(vmem_limit_bytes=18 << 20),
@@ -205,7 +200,7 @@
 def normed_kernel(x_ref, w_ref, b_ref, mod_ref, out_ref, att_ref, str_ref):
     for h in range(H):
         att_ref[:, h * HD : (h + 1) * HD] = x_ref[h, :, :HD].astype(F32)
-        str_ref[:, h * HD : (h + 1) * HD] = x_ref[h, :, HD:].astype(F32)
+        str_ref[:, h * HD : (h + 1) * HD] = x_ref[h, :, HD : 2 * HD].astype(F32)
     projected = nn(att_ref[...].astype(BF16), w_ref[...]) + b_ref[...]
     residual = (str_ref[...] + mod_ref[0:1, :] * projected).astype(BF16).astype(F32)
     centred = residual - jnp.mean(residual, axis=1, keepdims=True)
@@ -226,24 +221,17 @@
         out_ref[t] = rows
 
 
-def expert_kernel(
-    x_ref, be_ref, router_ref, we_ref, wr_ref, _, out_ref, gate_ref, we_s, wr_s, part_ref, sem
-):
-    loads = [copy(we_ref, we_s, sem.at[0]), copy(wr_ref, wr_s, sem.at[1])]
-    for load in loads:
-        load.start()
+def expert_kernel(x_ref, be_ref, router_ref, we_ref, wr_ref, _, out_ref, gate_ref, part_ref, sem):
     rows = x_ref[...]
     router = jnp.broadcast_to(router_ref[...].astype(F32), (8, D)).astype(BF16)
     gate_ref[...] = jax.nn.sigmoid(nt(router, rows)).astype(BF16).astype(F32)
-    loads[0].wait()
-    hidden = jax.nn.gelu(nt(rows, we_s[...]) + be_ref[...], approximate=True).astype(BF16)
-    loads[1].wait()
+    hidden = jax.nn.gelu(nt(rows, we_ref[...]) + be_ref[...], approximate=True).astype(BF16)
     stores = []
     for c in range(16):
-        part_ref[c] = nt(wr_s[c], hidden).astype(BF16)
+        part_ref[c] = nt(wr_ref[c], hidden).astype(BF16)
         if c % 4 == 3:
             block = slice(c - 3, c + 1)
-            stores.append(copy(part_ref.at[block], out_ref.at[block, :HD, :], sem.at[2 + c // 4]))
+            stores.append(copy(part_ref.at[block], out_ref.at[block, :HD, :], sem.at[c // 4]))
             stores[-1].start()
     for store in stores:
         store.wait()
@@ -259,11 +247,12 @@
     for i in range(3):
         block = slice(i * TL, (i + 1) * TL)
         table = (lines == idx_ref[:, block]).astype(F32).astype(BF16)
-        out_ref[block, :] = nt(eye(TL), nn(rows, table).astype(BF16)).astype(BF16)
+        slots = jnp.concatenate([nn(rows, table), jnp.zeros((128 - HD, TL), F32)], axis=0)
+        out_ref[block, :] = nt(eye(TL), slots.astype(BF16)).astype(BF16)
 
 
 def scatter_kernel(p_ref, idx_ref, out_ref, mix_ref, sem):
-    turned = nt(eye(HD), p_ref[...]).astype(BF16)
+    turned = nt(eye(128)[:HD], p_ref[...]).astype(BF16)
     index = idx_ref[...]
     lines = lax.broadcasted_iota(jnp.int32, (TL, 768), 0)
     stores = []
@@ -291,8 +280,10 @@
 
 
 def final_kernel(m_ref, res_ref, mod_ref, out_ref):
-    mixed = nt(eye(TL), m_ref[...])
-    out_ref[...] = (res_ref[...].astype(F32) + mod_ref[3:4, :] * mixed).astype(BF16)
+    for start, size in TILES:
+        cols = slice(start, start + size)
+        mixed = nt(eye(TL), m_ref[cols, :])
+        out_ref[:, cols] = (res_ref[:, cols].astype(F32) + mod_ref[3:4, cols] * mixed).astype(BF16)
 
 
 ANY = pl.BlockSpec(memory_space=pl.ANY)
@@ -398,11 +389,11 @@
 
     picked_out, keys, values = call(
         picked_kernel,
-        (shaped(768, 2 * HD), shaped(4096, HD), shaped(80, 4096)),
+        (shaped(768, 2 * HD), shaped(4096, 128), shaped(80, 4096)),
         "picked_attention",
         24,
         [
-            pltpu.VMEM((4096, HD), BF16),
+            pltpu.VMEM((4096, 128), BF16),
             pltpu.VMEM((80, 4096), BF16),
             pltpu.VMEM((2, 4096, TL), F32),
             pltpu.VMEM((3, 2 * HD, TL), BF16),
@@ -414,43 +405,37 @@
     )(pick_index, heads)
 
     rows = exchange(picked_out.reshape(16, 48, 2 * HD), "tok")
-    attended = main_part(heads, keys, values, 0, 5)
+    attended = main_part(heads, keys, values, 0, 4)
     rows, attended = lax.optimization_barrier((rows, attended))
     normed = call(
         normed_kernel, shaped(16, 3, D), "normed", 10, [pltpu.VMEM((48, D), F32), pltpu.VMEM((48, D), F32)]
-    )(rows, output_weight, out_bias, mod)
+    )(rows, output_weight, *in_hbm(out_bias, mod))
     normed = exchange(normed, "frame")
-    attended = main_part(heads, keys, values, 5, 6, attended)
+    attended = main_part(heads, keys, values, 4, 4, attended)
     normed, attended = lax.optimization_barrier((normed, attended))
     rows = call(compact_kernel, shaped(16, 16, D), "compact", 6, [pltpu.VMEM((48, D), F32)])(
         normed, held_index
     )
     rows = exchange(rows, "tok")
-    attended = main_part(heads, keys, values, 11, 5, attended)
+    attended = main_part(heads, keys, values, 8, 8, attended)
     rows, attended = lax.optimization_barrier((rows, attended))
     both, gates = call(
         expert_kernel,
         (shaped(16, 2 * HD, TL), shaped(8, TL, dtype=F32)),
         "expert",
         10,
-        [
-            pltpu.VMEM((288, D), BF16),
-            pltpu.VMEM((16, HD, 288), BF16),
-            pltpu.VMEM((16, HD, TL), BF16),
-            pltpu.SemaphoreType.DMA((6,)),
-        ],
-        in_specs=[VMEM, VMEM, VMEM, ANY, ANY, ANY],
+        [pltpu.VMEM((16, HD, TL), BF16), pltpu.SemaphoreType.DMA((4,))],
+        in_specs=[VMEM, VMEM, VMEM, VMEM, VMEM, ANY],
         out_specs=(ANY, VMEM),
         input_output_aliases={5: 0},
     )(
-        rows.reshape(TL, D),
-        *in_hbm(expand_bias, router_own, expand_turned, reduce_turned, attended),
+        rows.reshape(TL, D), expand_bias, router_own, expand_turned, reduce_turned, *in_hbm(attended)
     )
     both = exchange(both, "tok")
     first_block = lambda *shape: pl.BlockSpec(shape, lambda i: (0,) * len(shape))
     outs = call(
         weighted_kernel,
-        shaped(768, HD),
+        shaped(768, 128),
         "weighted",
         8,
         grid=(1,),
@@ -460,9 +445,9 @@
             first_block(HD, 1),
             first_block(1, 768),
         ],
-        out_specs=first_block(768, HD),
+        out_specs=first_block(768, 128),
     )(both, *in_hbm(gates, bias_own, back_index))
-    outs = exchange(outs.reshape(16, 48, HD), "frame")
+    outs = exchange(outs.reshape(16, 48, 128), "frame")
     residual = call(residual_kernel, shaped(TL, D), "residual", 12, [pltpu.VMEM((D, TL), BF16)])(
         *in_hbm(both, stream[0], output_weight, out_bias, mod)
     )
@@ -474,21 +459,11 @@
         [pltpu.VMEM((16, HD, TL), BF16), pltpu.SemaphoreType.DMA((4,))],
         in_specs=[VMEM, VMEM],
         out_specs=ANY,
-    )(outs.reshape(768, HD), *in_hbm(spread_index))
+    )(outs.reshape(768, 128), *in_hbm(spread_index))
     mixed = exchange(mixed, "tok")
-    layer_out = call(
-        final_kernel,
-        shaped(TL, D),
-        "final",
-        8,
-        grid=(3,),
-        in_specs=[
-            pl.BlockSpec((384, TL), lambda i: (i, 0)),
-            pl.BlockSpec((TL, 384), lambda i: (0, i)),
-            pl.BlockSpec((4, 384), lambda i: (0, i)),
-        ],
-        out_specs=pl.BlockSpec((TL, 384), lambda i: (0, i)),
-    )(mixed.reshape(D, TL), *in_hbm(residual, mod))
+    layer_out = call(final_kernel, shaped(TL, D), "final", 8)(
+        mixed.reshape(D, TL), *in_hbm(residual, mod)
+    )
     return layer_out[None]
 
 

time: 181 us -> 175 us (0.967)
  Pallas kernels: 63.3 us -> 56.6 us
  blocking collectives: 41.1 us -> 38.6 us
  waiting for transfers between devices: 28.7 us -> 30.9 us
    pallas_call x3, Pallas kernels: 30.9 us -> 25.8 us  [main_part(): pl.pallas_call(functools.partial(main_kernel, steps, aliased), grid=(step...]
    all_to_all x1, blocking collectives: 20.5 us -> 18 us  [per_device(): outs = exchange(outs.reshape(16, 48, 128), 'frame')]
    all_to_all x1, waiting for transfers between devices: 0.01 us -> 2.3 us  [per_device(): normed = exchange(normed, 'frame')]
    all_to_all x1, starting transfers between devices: 6.73 us -> 4.88 us  [per_device(): rows = exchange(rows, 'tok')]
  transfers between devices with their start and end apart: 6 -> 6, of which waited for: 4 -> 6; matrix products, arithmetic and copies ran while one was open for 4% -> 5% of each run, Pallas kernels for 20% -> 18%
where the time goes in v4:
time: 175 us; the launch traced here: 174 us
  Pallas kernels  56.6 us (32%)
  starting transfers between devices  39.7 us (23%)
  blocking collectives  38.6 us (22%)
  waiting for transfers between devices  30.9 us (18%)
  local copies, waits for them, and re-layouts  4.86 us (3%)
  other arithmetic  3.07 us (2%)
    pallas_call x3, Pallas kernels, main_part(): pl.pallas_call(functools.partial(main_kernel, steps, aliased), grid=(step...  25.8 us
    all_gather x1, blocking collectives, per_device(): all_counts = lax.all_gather(own_counts, 'frame', axis=1)  20.6 us
    all_to_all x1, blocking collectives, per_device(): outs = exchange(outs.reshape(16, 48, 128), 'frame')  18 us
    all_to_all x1, waiting for transfers between devices, per_device(): both = exchange(both, 'tok')  16.3 us
    all_to_all x1, starting transfers between devices, per_device(): normed = exchange(normed, 'frame')  12.5 us
    pallas_call x1, Pallas kernels, per_device(): call(picked_kernel, (shaped(768, 2 * HD), shaped(4096, 128), shaped(80, 4...  8 us
    all_to_all x1, waiting for transfers between devices, per_device(): mixed = exchange(mixed, 'tok')  7.74 us
    all_to_all x1, starting transfers between devices, per_device(): heads = exchange(sent, 'tok')  7.72 us
  transfers between devices with their start and end apart: 6, of which 6 were waited for; matrix products, arithmetic and copies ran while one was open for 5% of the time, Pallas kernels for 18%

profile of v4, /device:TPU:1, one launch (start us, length us, event | category | flops | bytes accessed | tf_op | source)
XLA Modules:
  0.0 174.1 jit_solution(14478058794848832123)
XLA Ops:
  0.0 3.5 %split.1 = bf16[16,288,256]{2,1,0:T(8,128)(2,1)} custom-call(bf16[256,1152]{1,0:T(8,128)(2,1)} %bitcast.36, bf16[256,1152]{1,0:T(8,128)(2,1)} %bitcast.37, bf16[256,1152]{1,0:T(8,128)(2,1)} %bitcast.38, bf16[256,1152]{1,0:T(8,128)(2,1)} %bitcast.32), custom_call_target="tpu_custom_call" | custom-call | tf_op jit(solution)/shard_map/split/pallas_call | solution.py:334
  3.5 7.7 %all-to-all-start = ((bf16[16,288,256]{2,1,0:T(8,128)(2,1)}), bf16[16,288,256]{2,1,0:T(8,128)(2,1)S(1)}, u32[]{:S(2)}, u32[]{:S(2)}) async-start(bf16[16,288,256]{2,1,0:T(8,128)(2,1)} %split.1), calls=%async_computation | async-start | bytes 4718592 | tf_op jit(solution)/shard_map/all_to_all | solution.py:350
  11.3 0.1 iota_compare_fusion.1
  11.4 0.1 select_reduce_fusion.1
  11.5 0.1 lt.114
  11.6 0.6 broadcast_in_dim.78.b_ref
  12.2 0.5 broadcast.168
  12.7 0.7 reduce.5
  13.4 0.1 squeeze.30
  13.5 0.1 reshape_squeeze.3
  13.6 20.6 %all-gather = s32[16,1,16]{2,1,0:T(1,128)S(1)} all-gather(s32[1,1,16]{2,1,0:T(1,128)S(1)} %bitcast.46), channel_id=1, replica_groups=mesh['frame'=16,'tok'=16] {'frame'}, dimensions={0}, use_global_device_ids=true | all-gather | bytes 1088 | tf_op jit(solution)/shard_map/all_gather | solution.py:353
  34.3 0.1 multiply_reduce_fusion
  34.4 0.1 multiply_reduce_fusion.1
  34.5 0.1 fusion.1
  34.6 0.1 select_n.68.idx_ref
  34.7 0.1 add_select_fusion
  34.8 0.7 reshape.298.idx_ref
  35.5 0.1 broadcast_add_fusion
  35.5 1.0 select_reduce_fusion
  36.6 0.1 compare_select_fusion
  36.7 0.2 copy.28
  36.8 0.2 select_n.62.idx_ref
  37.1 1.5 copy.29
  38.6 0.6 broadcast_select_fusion.idx_ref
  39.2 3.8 %all-to-all-done.r_ref.refs_0_.refs_1_ = bf16[16,288,256]{2,1,0:T(8,128)(2,1)S(1)} async-done(((bf16[16,288,256]{2,1,0:T(8,128)(2,1)}), bf16[16,288,256]{2,1,0:T(8,128)(2,1)S(1)}, u32[]{:S(2)}, u32[]{:S(2)}) %all-to-all-start) | async-done | bytes 2359328 | tf_op jit(solution)/shard_map/all_to_all | solution.py:350
  42.9 8.0 %picked_attention.1 = (bf16[768,144]{1,0:T(8,128)(2,1)}, bf16[4096,128]{1,0:T(8,128)(2,1)}, bf16[80,4096]{1,0:T(8,128)(2,1)}) custom-call(s32[1,768]{1,0:T(1,128)S(1)} %select_n.62.idx_ref, bf16[16,288,256]{2,1,0:T(8,128)(2,1)S(1)} %all-to-all-done.r_ref.refs_0_.refs_1_), custom_call_target="tpu_custom_call" | custom-call | tf_op jit(solution)/shard_map/picked_attention/pallas_call | solution.py:390
  50.9 4.4 %all-to-all-start.1 = ((bf16[16,48,144]{2,1,0:T(8,128)(2,1)}), bf16[16,48,144]{2,1,0:T(8,128)(2,1)}, u32[]{:S(2)}, u32[]{:S(2)}) async-start(bf16[16,48,144]{2,1,0:T(8,128)(2,1)} %bitcast.39), calls=%async_computation.1 | async-start | bytes 786432 | tf_op jit(solution)/shard_map/all_to_all | solution.py:407
  55.4 7.2 %main_attention.3.refs_4_ = bf16[16,144,256]{2,1,0:T(8,128)(2,1)} custom-call(bf16[16,288,256]{2,1,0:T(8,128)(2,1)} %copy-done.2, bf16[16,288,256]{2,1,0:T(8,128)(2,1)} %copy-done.2, bf16[4096,128]{1,0:T(8,128)(2,1)} %get-tuple-element.24.refs_2_, bf16[80,4096]{1,0:T(8,128)(2,1)} %get-tuple-element.25.refs_3_), custom_call_target="tpu_custom_call" | custom-call | flops 4294967296 | bytes 2097152 | tf_op jit(solution)/shard_map/main_attention/pallas_call | solution.py:181
  62.5 0.7 all-to-all-done.1.x_ref
  63.2 2.6 %normed.1 = bf16[16,3,1152]{2,1,0:T(4,128)(2,1)} custom-call(bf16[16,48,144]{2,1,0:T(8,128)(2,1)} %all-to-all-done.1.x_ref, bf16[1152,1152]{1,0:T(8,128)(2,1)S(1)} %copy-done, f32[1,1152]{1,0:T(1,128)} %broadcast_in_dim.78.b_ref, f32[4,1152]{1,0:T(4,128)} %bitcast.40), custom_call_target="tpu_custom_call" | custom-call | tf_op jit(solution)/shard_map/normed/pallas_call | solution.py:410
  65.8 12.5 %all-to-all-start.2 = ((bf16[16,3,1152]{2,1,0:T(4,128)(2,1)}), bf16[16,3,1152]{2,1,0:T(4,128)(2,1)S(1)}, u32[]{:S(2)}, u32[]{:S(2)}) async-start(bf16[16,3,1152]{2,1,0:T(4,128)(2,1)} %normed.1), calls=%async_computation.2 | async-start | bytes 294912 | tf_op jit(solution)/shard_map/all_to_all | solution.py:413
  78.3 7.0 %main_attention.4.refs_4_ = bf16[16,144,256]{2,1,0:T(8,128)(2,1)} custom-call(bf16[16,288,256]{2,1,0:T(8,128)(2,1)} %copy-done.2, bf16[16,288,256]{2,1,0:T(8,128)(2,1)} %copy-done.2, bf16[4096,128]{1,0:T(8,128)(2,1)} %get-tuple-element.24.refs_2_, bf16[80,4096]{1,0:T(8,128)(2,1)} %get-tuple-element.25.refs_3_, ...), custom_call_target="tpu_custom_call", output_to_operand_aliasing={{}: (4, {})} | custom-call | flops 4294967296 | bytes 2097152 | tf_op jit(solution)/shard_map/main_attention/pallas_call | solution.py:181
  85.4 2.3 %all-to-all-done.2.x_ref = bf16[16,3,1152]{2,1,0:T(4,128)(2,1)S(1)} async-done(((bf16[16,3,1152]{2,1,0:T(4,128)(2,1)}), bf16[16,3,1152]{2,1,0:T(4,128)(2,1)S(1)}, u32[]{:S(2)}, u32[]{:S(2)}) %all-to-all-start.2) | async-done | bytes 110624 | tf_op jit(solution)/shard_map/all_to_all | solution.py:413
  87.7 1.0 compact.1
  88.7 4.9 %all-to-all-start.3 = ((bf16[16,16,1152]{2,1,0:T(8,128)(2,1)}), bf16[16,16,1152]{2,1,0:T(8,128)(2,1)S(1)}, u32[]{:S(2)}, u32[]{:S(2)}) async-start(bf16[16,16,1152]{2,1,0:T(8,128)(2,1)} %compact.1), calls=%async_computation.3 | async-start | bytes 1179648 | tf_op jit(solution)/shard_map/all_to_all | solution.py:419
  93.6 11.6 %main_attention.5._ = bf16[16,144,256]{2,1,0:T(8,128)(2,1)} custom-call(bf16[16,288,256]{2,1,0:T(8,128)(2,1)} %copy-done.2, bf16[16,288,256]{2,1,0:T(8,128)(2,1)} %copy-done.2, bf16[4096,128]{1,0:T(8,128)(2,1)} %get-tuple-element.24.refs_2_, bf16[80,4096]{1,0:T(8,128)(2,1)} %get-tuple-element.25.refs_3_, ...), custom_call_target="tpu_custom_call", output_to_operand_aliasing={{}: (4, {})} | custom-call | flops 8589934592 | bytes 2097152 | tf_op jit(solution)/shard_map/main_attention/pallas_call | solution.py:181
  105.2 0.1 all-to-all-done.3
  105.3 3.2 %expert.1 = (bf16[16,144,256]{2,1,0:T(8,128)(2,1)}, f32[8,256]{1,0:T(8,128)}) custom-call(bf16[256,1152]{1,0:T(8,128)(2,1)S(1)} %bitcast.28, f32[1,288]{1,0:T(1,128)S(1)} %copy-done.4, bf16[1,1152]{1,0:T(2,128)(2,1)S(1)} %broadcast_in_dim.77.router_ref, bf16[288,1152]{1,0:T(8,128)(2,1)S(1)} %bitcast.31, ...), custom_call_target="tpu_custom_call", output_to_operand_aliasing={{0}: (5, {})} | custom-call | tf_op jit(solution)/shard_map/expert/pallas_call | solution.py:422
  108.5 6.6 %all-to-all-start.4 = ((bf16[16,144,256]{2,1,0:T(8,128)(2,1)}), bf16[16,144,256]{2,1,0:T(8,128)(2,1)S(1)}, u32[]{:S(2)}, u32[]{:S(2)}) async-start(bf16[16,144,256]{2,1,0:T(8,128)(2,1)} %get-tuple-element.34), calls=%async_computation.4 | async-start | bytes 2359296 | tf_op jit(solution)/shard_map/all_to_all | solution.py:434
  115.1 0.7 copy.30.rb_ref
  115.8 16.3 %all-to-all-done.4.x_ref.o_ref = bf16[16,144,256]{2,1,0:T(8,128)(2,1)S(1)} async-done(((bf16[16,144,256]{2,1,0:T(8,128)(2,1)}), bf16[16,144,256]{2,1,0:T(8,128)(2,1)S(1)}, u32[]{:S(2)}, u32[]{:S(2)}) %all-to-all-start.4) | async-done | bytes 1179680 | tf_op jit(solution)/shard_map/all_to_all | solution.py:434
  132.1 2.1 %weighted.1 = bf16[768,128]{1,0:T(8,128)(2,1)} custom-call(bf16[16,144,256]{2,1,0:T(8,128)(2,1)S(1)} %all-to-all-done.4.x_ref.o_ref, f32[8,256]{1,0:T(8,128)} %get-tuple-element.35.gate_ref, f32[72,1]{1,0:T(8,128)} %copy.30.rb_ref, s32[1,768]{1,0:T(1,128)} %reshape.298.idx_ref), custom_call_target="tpu_custom_call" | custom-call | tf_op jit(solution)/shard_map/weighted/pallas_call | solution.py:436
  134.2 18.0 %all_to_all.35 = bf16[16,48,128]{2,1,0:T(8,128)(2,1)S(1)} all-to-all(bf16[16,48,128]{2,1,0:T(8,128)(2,1)} %bitcast.34), channel_id=1, replica_groups=mesh['frame'=16,'tok'=16] {'frame'}, dimensions={0} | all-to-all | bytes 393216 | tf_op jit(solution)/shard_map/all_to_all | solution.py:450
  152.2 3.5 %scatter.1 = bf16[16,72,256]{2,1,0:T(8,128)(2,1)} custom-call(bf16[768,128]{1,0:T(8,128)(2,1)S(1)} %bitcast.30, s32[1,768]{1,0:T(1,128)} %broadcast_select_fusion.idx_ref), custom_call_target="tpu_custom_call" | custom-call | tf_op jit(solution)/shard_map/scatter/pallas_call | solution.py:454
  155.7 3.6 %all-to-all-start.6 = ((bf16[16,72,256]{2,1,0:T(8,128)(2,1)}), bf16[16,72,256]{2,1,0:T(8,128)(2,1)S(1)}, u32[]{:S(2)}, u32[]{:S(2)}) async-start(bf16[16,72,256]{2,1,0:T(8,128)(2,1)} %scatter.1), calls=%async_computation.6 | async-start | bytes 1179648 | tf_op jit(solution)/shard_map/all_to_all | solution.py:463
  159.3 4.8 %residual.1.res_ref = bf16[256,1152]{1,0:T(8,128)(2,1)} custom-call(bf16[16,144,256]{2,1,0:T(8,128)(2,1)} %copy-done.1, bf16[256,1152]{1,0:T(8,128)(2,1)} %bitcast.33, bf16[1152,1152]{1,0:T(8,128)(2,1)} %w_ref.3, f32[1,1152]{1,0:T(1,128)} %broadcast_in_dim.78.b_ref, f32[4,1152]{1,0:T(4,128)} %bitcast.41), custom_call_target="tpu_custom_call" | custom-call | tf_op jit(solution)/shard_map/residual/pallas_call | solution.py:451
  164.1 7.7 %all-to-all-done.6 = bf16[16,72,256]{2,1,0:T(8,128)(2,1)S(1)} async-done(((bf16[16,72,256]{2,1,0:T(8,128)(2,1)}), bf16[16,72,256]{2,1,0:T(8,128)(2,1)S(1)}, u32[]{:S(2)}, u32[]{:S(2)}) %all-to-all-start.6) | async-done | bytes 589856 | tf_op jit(solution)/shard_map/all_to_all | solution.py:463
  171.8 2.2 %final.1 = bf16[256,1152]{1,0:T(8,128)(2,1)} custom-call(bf16[1152,256]{1,0:T(8,128)(2,1)S(1)} %bitcast.29, bf16[256,1152]{1,0:T(8,128)(2,1)} %residual.1.res_ref, f32[4,1152]{1,0:T(4,128)} %bitcast.42), custom_call_target="tpu_custom_call" | custom-call | tf_op jit(solution)/shard_map/final/pallas_call | solution.py:464
  (30 shorter events, 0.2 us)
Async XLA Ops:
  3.5 7.8 %copy-start.8 = (s32[16,1]{0,1:T(1,128)S(1)}, s32[16,1]{0,1:T(1,128)}, u32[]{:S(2)}) copy-start(s32[16,1]{0,1:T(1,128)} %param.26) | copy-start | bytes 196
  3.5 7.9 %copy-start.5 = (bf16[1152,16]{0,1:T(8,128)(2,1)S(1)}, bf16[1152,16]{0,1:T(8,128)(2,1)}, u32[]{:S(2)}) copy-start(bf16[1152,16]{0,1:T(8,128)(2,1)} %param.21) | copy-start | bytes 110596
  3.5 8.1 %copy-start.7 = (f32[1152]{0:T(1024)S(1)}, f32[1152]{0:T(1024)}, u32[]{:S(2)}) copy-start(f32[1152]{0:T(1024)} %param.20) | copy-start | bytes 13828
  3.5 9.2 %copy-start.6 = (s32[16,1,48]{2,1,0:T(1,128)S(1)}, s32[16,1,48]{2,1,0:T(1,128)}, u32[]{:S(2)}) copy-start(s32[16,1,48]{2,1,0:T(1,128)} %param.27) | copy-start | bytes 9220
  3.5 10.0 %copy-start.9 = (f32[1,1152]{1,0:T(1,128)S(1)}, f32[1,1152]{1,0:T(1,128)}, u32[]{:S(2)}) copy-start(f32[1,1152]{1,0:T(1,128)} %param.25) | copy-start | bytes 13828
  3.5 39.4 %all-to-all-start = ((bf16[16,288,256]{2,1,0:T(8,128)(2,1)}), bf16[16,288,256]{2,1,0:T(8,128)(2,1)S(1)}, u32[]{:S(2)}, u32[]{:S(2)}) async-start(bf16[16,288,256]{2,1,0:T(8,128)(2,1)} %split.1), calls=%async_computation | async-start | bytes 4718592 | tf_op jit(solution)/shard_map/all_to_all | solution.py:350
  42.9 8.0 %copy-start.2 = (bf16[16,288,256]{2,1,0:T(8,128)(2,1)}, bf16[16,288,256]{2,1,0:T(8,128)(2,1)S(1)}, u32[]{:S(2)}) copy-start(bf16[16,288,256]{2,1,0:T(8,128)(2,1)S(1)} %all-to-all-done.r_ref.refs_0_.refs_1_) | copy-start | bytes 7077892
  50.9 12.3 %all-to-all-start.1 = ((bf16[16,48,144]{2,1,0:T(8,128)(2,1)}), bf16[16,48,144]{2,1,0:T(8,128)(2,1)}, u32[]{:S(2)}, u32[]{:S(2)}) async-start(bf16[16,48,144]{2,1,0:T(8,128)(2,1)} %bitcast.39), calls=%async_computation.1 | async-start | bytes 786432 | tf_op jit(solution)/shard_map/all_to_all | solution.py:407
  55.4 7.8 %copy-start = (bf16[1152,1152]{1,0:T(8,128)(2,1)S(1)}, bf16[1152,1152]{1,0:T(8,128)(2,1)}, u32[]{:S(2)}) copy-start(bf16[1152,1152]{1,0:T(8,128)(2,1)} %w_ref.3) | copy-start | bytes 7962628
  65.8 21.9 %all-to-all-start.2 = ((bf16[16,3,1152]{2,1,0:T(4,128)(2,1)}), bf16[16,3,1152]{2,1,0:T(4,128)(2,1)S(1)}, u32[]{:S(2)}, u32[]{:S(2)}) async-start(bf16[16,3,1152]{2,1,0:T(4,128)(2,1)} %normed.1), calls=%async_computation.2 | async-start | bytes 294912 | tf_op jit(solution)/shard_map/all_to_all | solution.py:413
  88.7 16.6 %all-to-all-start.3 = ((bf16[16,16,1152]{2,1,0:T(8,128)(2,1)}), bf16[16,16,1152]{2,1,0:T(8,128)(2,1)S(1)}, u32[]{:S(2)}, u32[]{:S(2)}) async-start(bf16[16,16,1152]{2,1,0:T(8,128)(2,1)} %compact.1), calls=%async_computation.3 | async-start | bytes 1179648 | tf_op jit(solution)/shard_map/all_to_all | solution.py:419
  93.6 11.7 %copy-start.3 = (bf16[1,1152,288]{1,2,0:T(8,128)(2,1)S(1)}, bf16[1,1152,288]{1,2,0:T(8,128)(2,1)}, u32[]{:S(2)}) copy-start(bf16[1,1152,288]{1,2,0:T(8,128)(2,1)} %param.22) | copy-start | bytes 1990660
  93.6 11.7 %copy-start.4 = (f32[1,288]{1,0:T(1,128)S(1)}, f32[1,288]{1,0:T(1,128)}, u32[]{:S(2)}) copy-start(f32[1,288]{1,0:T(1,128)} %be_ref.1) | copy-start | bytes 3460
  108.5 23.7 %all-to-all-start.4 = ((bf16[16,144,256]{2,1,0:T(8,128)(2,1)}), bf16[16,144,256]{2,1,0:T(8,128)(2,1)S(1)}, u32[]{:S(2)}, u32[]{:S(2)}) async-start(bf16[16,144,256]{2,1,0:T(8,128)(2,1)} %get-tuple-element.34), calls=%async_computation.4 | async-start | bytes 2359296 | tf_op jit(solution)/shard_map/all_to_all | solution.py:434
  132.1 23.6 %copy-start.1 = (bf16[16,144,256]{2,1,0:T(8,128)(2,1)}, bf16[16,144,256]{2,1,0:T(8,128)(2,1)S(1)}, u32[]{:S(2)}) copy-start(bf16[16,144,256]{2,1,0:T(8,128)(2,1)S(1)} %all-to-all-done.4.x_ref.o_ref) | copy-start | bytes 3538948
  155.7 16.1 %all-to-all-start.6 = ((bf16[16,72,256]{2,1,0:T(8,128)(2,1)}), bf16[16,72,256]{2,1,0:T(8,128)(2,1)S(1)}, u32[]{:S(2)}, u32[]{:S(2)}) async-start(bf16[16,72,256]{2,1,0:T(8,128)(2,1)} %scatter.1), calls=%async_computation.6 | async-start | bytes 1179648 | tf_op jit(solution)/shard_map/all_to_all | solution.py:463

commit v5 on v4

--- a/solution.py
+++ b/solution.py
@@ -68,10 +68,8 @@
 
 def prepare(r_ref, k_ref, v_ref):
     for j in range(16):
-        keys = nt(eye(TL), r_ref[j, :HD, :])
-        k_ref[j * TL : (j + 1) * TL, :] = jnp.concatenate(
-            [keys, jnp.zeros((TL, 128 - HD), F32)], axis=1
-        ).astype(BF16)
+        keys = jnp.concatenate([r_ref[j, :HD, :].astype(F32), jnp.zeros((128 - HD, TL), F32)], axis=0)
+        k_ref[j * TL : (j + 1) * TL, :] = keys.T.astype(BF16)
         v_ref[:HD, j * TL : (j + 1) * TL] = r_ref[j, HD : 2 * HD, :]
         v_ref[HD:, j * TL : (j + 1) * TL] = jnp.ones((8, TL), BF16)
 
@@ -238,9 +236,9 @@
 
 
 def weighted_kernel(x_ref, gate_ref, rb_ref, idx_ref, out_ref):
-    total = x_ref[0].astype(F32)
+    total = x_ref[0, :HD, :].astype(F32)
     for t in range(1, 16):
-        total = total + x_ref[t].astype(F32)
+        total = total + x_ref[t, :HD, :].astype(F32)
     rows = (total + rb_ref[...]).astype(BF16).astype(F32)
     rows = (rows * gate_ref[0:1, :]).astype(BF16)
     lines = lax.broadcasted_iota(jnp.int32, (TL, TL), 0)
@@ -370,22 +368,14 @@
     held_index = jnp.where(
         held_slot < expert_counts[:, None], (expert_offsets[:, None] + held_slot) >> 4, -1
     ).reshape(1, 48)
-    row_id = expert_offsets[:, None] + slots[None, :]
-    back_index = jnp.where(
-        slots[None, :] < expert_counts[:, None], (row_id & 15) * 16 + (row_id >> 4), -1
-    ).reshape(1, 768)
-    spread_index = jnp.where(slots[None, :] < own_counts[:, None], picked, -1).reshape(1, 768)
 
     router_own = jnp.sum(
         jnp.where((frames == me_frame)[None, :], router_weight, jnp.zeros_like(router_weight)), axis=1
     )
     router_own = router_own[None, :]
-    bias_own = lax.dynamic_slice_in_dim(reduce_bias[0].reshape(16, HD), me_tok, 1, 0).reshape(HD, 1)
     reduce_turned = reduce_weight[0].T.reshape(16, HD, 288)
     expand_turned = expand_weight[0].T
-    heads, reduce_turned, bias_own, back_index, spread_index, router_own = lax.optimization_barrier(
-        (heads, reduce_turned, bias_own, back_index, spread_index, router_own)
-    )
+    heads, reduce_turned, router_own = lax.optimization_barrier((heads, reduce_turned, router_own))
 
     picked_out, keys, values = call(
         picked_kernel,
@@ -431,24 +421,21 @@
     )(
         rows.reshape(TL, D), expand_bias, router_own, expand_turned, reduce_turned, *in_hbm(attended)
     )
+    gates, offsets, used, own_used, own_picked, own_bias = lax.optimization_barrier(
+        (gates, expert_offsets, expert_counts, own_counts, picked, reduce_bias)
+    )
+    row_id = offsets[:, None] + slots[None, :]
+    back_index = jnp.where(
+        slots[None, :] < used[:, None], (row_id & 15) * 16 + (row_id >> 4), -1
+    ).reshape(1, 768)
+    spread_index = jnp.where(slots[None, :] < own_used[:, None], own_picked, -1).reshape(1, 768)
+    bias_own = lax.dynamic_slice_in_dim(own_bias[0].reshape(16, HD), me_tok, 1, 0).reshape(HD, 1)
     both = exchange(both, "tok")
-    first_block = lambda *shape: pl.BlockSpec(shape, lambda i: (0,) * len(shape))
     outs = call(
-        weighted_kernel,
-        shaped(768, 128),
-        "weighted",
-        8,
-        grid=(1,),
-        in_specs=[
-            first_block(16, HD, TL),
-            first_block(8, TL),
-            first_block(HD, 1),
-            first_block(1, 768),
-        ],
-        out_specs=first_block(768, 128),
-    )(both, *in_hbm(gates, bias_own, back_index))
+        weighted_kernel, shaped(768, 128), "weighted", 8, in_specs=[VMEM] * 4, out_specs=VMEM
+    )(both, *in_hbm(gates), bias_own, back_index)
     outs = exchange(outs.reshape(16, 48, 128), "frame")
-    residual = call(residual_kernel, shaped(TL, D), "residual", 12, [pltpu.VMEM((D, TL), BF16)])(
+    residual = call(residual_kernel, pltpu.VMEM((TL, D), BF16), "residual", 12, [pltpu.VMEM((D, TL), BF16)])(
         *in_hbm(both, stream[0], output_weight, out_bias, mod)
     )
     mixed = call(
@@ -462,7 +449,7 @@
     )(outs.reshape(768, 128), *in_hbm(spread_index))
     mixed = exchange(mixed, "tok")
     layer_out = call(final_kernel, shaped(TL, D), "final", 8)(
-        mixed.reshape(D, TL), *in_hbm(residual, mod)
+        mixed.reshape(D, TL), residual, *in_hbm(mod)
     )
     return layer_out[None]
 

time: 175 us -> 174 us (level)
  blocking collectives: 38.6 us -> 20.6 us
  waiting for transfers between devices: 30.9 us -> 44 us
  starting transfers between devices: 39.7 us -> 47.4 us
  Pallas kernels: 56.6 us -> 54.6 us
    all_to_all x1 -> x0, blocking collectives: 18 us -> none  [per_device(): outs = exchange(outs.reshape(16, 48, 128), 'frame')]
    all_to_all x0 -> x1, waiting for transfers between devices: none -> 9.58 us  [per_device(): outs = exchange(outs.reshape(16, 48, 128), 'frame')]
    all_to_all x0 -> x1, starting transfers between devices: none -> 7.67 us  [per_device(): outs = exchange(outs.reshape(16, 48, 128), 'frame')]
    all_to_all x1, waiting for transfers between devices: 3.76 us -> 6.19 us  [per_device(): heads = exchange(sent, 'tok')]
  transfers between devices with their start and end apart: 6 -> 7, of which waited for: 6 -> 7; matrix products, arithmetic and copies ran while one was open for 5% -> 3% of each run, Pallas kernels for 18% -> 17%
where the time goes in v5:
time: 174 us; the launch traced here: 173 us
  Pallas kernels  54.6 us (31%)
  starting transfers between devices  47.4 us (27%)
  waiting for transfers between devices  44 us (25%)
  blocking collectives  20.6 us (12%)
  local copies, waits for them, and re-layouts  4.16 us (2%)
  other arithmetic  1.8 us (1%)
    pallas_call x3, Pallas kernels, main_part(): pl.pallas_call(functools.partial(main_kernel, steps, aliased), grid=(step...  25.8 us
    all_gather x1, blocking collectives, per_device(): all_counts = lax.all_gather(own_counts, 'frame', axis=1)  20.6 us
    all_to_all x1, waiting for transfers between devices, per_device(): both = exchange(both, 'tok')  16.6 us
    all_to_all x1, starting transfers between devices, per_device(): normed = exchange(normed, 'frame')  12.5 us
    all_to_all x1, waiting for transfers between devices, per_device(): outs = exchange(outs.reshape(16, 48, 128), 'frame')  9.58 us
    all_to_all x1, waiting for transfers between devices, per_device(): mixed = exchange(mixed, 'tok')  8.6 us
    all_to_all x1, starting transfers between devices, per_device(): heads = exchange(sent, 'tok')  7.72 us
    all_to_all x1, starting transfers between devices, per_device(): outs = exchange(outs.reshape(16, 48, 128), 'frame')  7.67 us
  transfers between devices with their start and end apart: 7, of which 7 were waited for; matrix products, arithmetic and copies ran while one was open for 3% of the time, Pallas kernels for 17%

profile of v5, /device:TPU:1, one launch (start us, length us, event | category | flops | bytes accessed | tf_op | source)
XLA Modules:
  0.0 172.9 jit_solution(3758035729134799961)
XLA Ops:
  0.0 3.5 %split.1 = bf16[16,288,256]{2,1,0:T(8,128)(2,1)} custom-call(bf16[256,1152]{1,0:T(8,128)(2,1)} %bitcast.36, bf16[256,1152]{1,0:T(8,128)(2,1)} %bitcast.37, bf16[256,1152]{1,0:T(8,128)(2,1)} %bitcast.38, bf16[256,1152]{1,0:T(8,128)(2,1)} %bitcast.32), custom_call_target="tpu_custom_call" | custom-call | tf_op jit(solution)/shard_map/split/pallas_call | solution.py:332
  3.5 0.0 copy-start.5
  3.5 7.7 %all-to-all-start = ((bf16[16,288,256]{2,1,0:T(8,128)(2,1)}), bf16[16,288,256]{2,1,0:T(8,128)(2,1)S(1)}, u32[]{:S(2)}, u32[]{:S(2)}) async-start(bf16[16,288,256]{2,1,0:T(8,128)(2,1)} %split.1), calls=%async_computation | async-start | bytes 4718592 | tf_op jit(solution)/shard_map/all_to_all | solution.py:348
  11.3 0.1 select_reduce_fusion.1
  11.4 0.6 broadcast_in_dim.80.b_ref
  12.0 20.6 %all-gather = s32[16,1,16]{2,1,0:T(1,128)S(1)} all-gather(s32[1,1,16]{2,1,0:T(1,128)S(1)} %bitcast.46), channel_id=1, replica_groups=mesh['frame'=16,'tok'=16] {'frame'}, dimensions={0}, use_global_device_ids=true | all-gather | bytes 1088 | tf_op jit(solution)/shard_map/all_gather | solution.py:351
  32.6 0.1 copy.27
  32.7 0.1 multiply_reduce_fusion
  32.8 0.1 multiply_reduce_fusion.2
  32.9 0.5 copy-done.10
  33.4 0.1 fusion.1
  33.5 0.1 select_n.58.idx_ref
  33.6 0.1 broadcast_add_fusion
  33.7 1.0 select_reduce_fusion
  34.8 0.1 compare_select_fusion
  34.8 0.2 copy.28
  35.0 0.2 select_n.55.idx_ref
  35.2 1.5 copy.29
  36.7 6.2 %all-to-all-done.r_ref.refs_0_.refs_1_ = bf16[16,288,256]{2,1,0:T(8,128)(2,1)S(1)} async-done(((bf16[16,288,256]{2,1,0:T(8,128)(2,1)}), bf16[16,288,256]{2,1,0:T(8,128)(2,1)S(1)}, u32[]{:S(2)}, u32[]{:S(2)}) %all-to-all-start) | async-done | bytes 2359328 | tf_op jit(solution)/shard_map/all_to_all | solution.py:348
  42.9 7.3 %picked_attention.1 = (bf16[768,144]{1,0:T(8,128)(2,1)}, bf16[4096,128]{1,0:T(8,128)(2,1)}, bf16[80,4096]{1,0:T(8,128)(2,1)}) custom-call(s32[1,768]{1,0:T(1,128)S(1)} %select_n.55.idx_ref, bf16[16,288,256]{2,1,0:T(8,128)(2,1)S(1)} %all-to-all-done.r_ref.refs_0_.refs_1_), custom_call_target="tpu_custom_call" | custom-call | tf_op jit(solution)/shard_map/picked_attention/pallas_call | solution.py:380
  50.2 4.4 %all-to-all-start.1 = ((bf16[16,48,144]{2,1,0:T(8,128)(2,1)}), bf16[16,48,144]{2,1,0:T(8,128)(2,1)}, u32[]{:S(2)}, u32[]{:S(2)}) async-start(bf16[16,48,144]{2,1,0:T(8,128)(2,1)} %bitcast.39), calls=%async_computation.1 | async-start | bytes 786432 | tf_op jit(solution)/shard_map/all_to_all | solution.py:397
  54.6 7.2 %main_attention.3.refs_4_ = bf16[16,144,256]{2,1,0:T(8,128)(2,1)} custom-call(bf16[16,288,256]{2,1,0:T(8,128)(2,1)} %copy-done.2, bf16[16,288,256]{2,1,0:T(8,128)(2,1)} %copy-done.2, bf16[4096,128]{1,0:T(8,128)(2,1)} %get-tuple-element.27.refs_2_, bf16[80,4096]{1,0:T(8,128)(2,1)} %get-tuple-element.28.refs_3_), custom_call_target="tpu_custom_call" | custom-call | flops 4294967296 | bytes 2097152 | tf_op jit(solution)/shard_map/main_attention/pallas_call | solution.py:179
  61.8 0.7 all-to-all-done.1.x_ref
  62.4 2.6 %normed.1 = bf16[16,3,1152]{2,1,0:T(4,128)(2,1)} custom-call(bf16[16,48,144]{2,1,0:T(8,128)(2,1)} %all-to-all-done.1.x_ref, bf16[1152,1152]{1,0:T(8,128)(2,1)S(1)} %copy-done, f32[1,1152]{1,0:T(1,128)} %broadcast_in_dim.80.b_ref, f32[4,1152]{1,0:T(4,128)} %bitcast.40), custom_call_target="tpu_custom_call" | custom-call | tf_op jit(solution)/shard_map/normed/pallas_call | solution.py:400
  65.0 12.5 %all-to-all-start.2 = ((bf16[16,3,1152]{2,1,0:T(4,128)(2,1)}), bf16[16,3,1152]{2,1,0:T(4,128)(2,1)S(1)}, u32[]{:S(2)}, u32[]{:S(2)}) async-start(bf16[16,3,1152]{2,1,0:T(4,128)(2,1)} %normed.1), calls=%async_computation.2 | async-start | bytes 294912 | tf_op jit(solution)/shard_map/all_to_all | solution.py:403
  77.6 7.0 %main_attention.4.refs_4_ = bf16[16,144,256]{2,1,0:T(8,128)(2,1)} custom-call(bf16[16,288,256]{2,1,0:T(8,128)(2,1)} %copy-done.2, bf16[16,288,256]{2,1,0:T(8,128)(2,1)} %copy-done.2, bf16[4096,128]{1,0:T(8,128)(2,1)} %get-tuple-element.27.refs_2_, bf16[80,4096]{1,0:T(8,128)(2,1)} %get-tuple-element.28.refs_3_, ...), custom_call_target="tpu_custom_call", output_to_operand_aliasing={{}: (4, {})} | custom-call | flops 4294967296 | bytes 2097152 | tf_op jit(solution)/shard_map/main_attention/pallas_call | solution.py:179
  84.6 2.3 %all-to-all-done.2.x_ref = bf16[16,3,1152]{2,1,0:T(4,128)(2,1)S(1)} async-done(((bf16[16,3,1152]{2,1,0:T(4,128)(2,1)}), bf16[16,3,1152]{2,1,0:T(4,128)(2,1)S(1)}, u32[]{:S(2)}, u32[]{:S(2)}) %all-to-all-start.2) | async-done | bytes 110624 | tf_op jit(solution)/shard_map/all_to_all | solution.py:403
  86.9 1.0 compact.1
  87.9 4.9 %all-to-all-start.3 = ((bf16[16,16,1152]{2,1,0:T(8,128)(2,1)}), bf16[16,16,1152]{2,1,0:T(8,128)(2,1)S(1)}, u32[]{:S(2)}, u32[]{:S(2)}) async-start(bf16[16,16,1152]{2,1,0:T(8,128)(2,1)} %compact.1), calls=%async_computation.3 | async-start | bytes 1179648 | tf_op jit(solution)/shard_map/all_to_all | solution.py:409
  92.8 11.6 %main_attention.5._ = bf16[16,144,256]{2,1,0:T(8,128)(2,1)} custom-call(bf16[16,288,256]{2,1,0:T(8,128)(2,1)} %copy-done.2, bf16[16,288,256]{2,1,0:T(8,128)(2,1)} %copy-done.2, bf16[4096,128]{1,0:T(8,128)(2,1)} %get-tuple-element.27.refs_2_, bf16[80,4096]{1,0:T(8,128)(2,1)} %get-tuple-element.28.refs_3_, ...), custom_call_target="tpu_custom_call", output_to_operand_aliasing={{}: (4, {})} | custom-call | flops 8589934592 | bytes 2097152 | tf_op jit(solution)/shard_map/main_attention/pallas_call | solution.py:179
  104.4 0.1 all-to-all-done.3
  104.5 3.2 %expert.1 = (bf16[16,144,256]{2,1,0:T(8,128)(2,1)}, f32[8,256]{1,0:T(8,128)}) custom-call(bf16[256,1152]{1,0:T(8,128)(2,1)S(1)} %bitcast.28, f32[1,288]{1,0:T(1,128)S(1)} %copy-done.4, bf16[1,1152]{1,0:T(2,128)(2,1)S(1)} %broadcast_in_dim.79.router_ref, bf16[288,1152]{1,0:T(8,128)(2,1)S(1)} %bitcast.31, ...), custom_call_target="tpu_custom_call", output_to_operand_aliasing={{0}: (5, {})} | custom-call | tf_op jit(solution)/shard_map/expert/pallas_call | solution.py:412
  107.8 6.6 %all-to-all-start.4 = ((bf16[16,144,256]{2,1,0:T(8,128)(2,1)}), bf16[16,144,256]{2,1,0:T(8,128)(2,1)S(1)}, u32[]{:S(2)}, u32[]{:S(2)}) async-start(bf16[16,144,256]{2,1,0:T(8,128)(2,1)} %get-tuple-element.37), calls=%async_computation.4 | async-start | bytes 2359296 | tf_op jit(solution)/shard_map/all_to_all | solution.py:433
  114.4 0.1 reshape_squeeze.3
  114.5 0.1 add_select_fusion
  114.6 0.1 reshape.272.idx_ref
  114.7 0.1 copy.30.rb_ref
  114.8 16.6 %all-to-all-done.4.x_ref.o_ref = bf16[16,144,256]{2,1,0:T(8,128)(2,1)S(1)} async-done(((bf16[16,144,256]{2,1,0:T(8,128)(2,1)}), bf16[16,144,256]{2,1,0:T(8,128)(2,1)S(1)}, u32[]{:S(2)}, u32[]{:S(2)}) %all-to-all-start.4) | async-done | bytes 1179680 | tf_op jit(solution)/shard_map/all_to_all | solution.py:433
  131.4 2.0 %weighted.1 = bf16[768,128]{1,0:T(8,128)(2,1)} custom-call(bf16[16,144,256]{2,1,0:T(8,128)(2,1)S(1)} %all-to-all-done.4.x_ref.o_ref, f32[8,256]{1,0:T(8,128)} %get-tuple-element.39.gate_ref, f32[72,1]{1,0:T(8,128)S(1)} %copy.30.rb_ref, s32[1,768]{1,0:T(1,128)S(1)} %reshape.272.idx_ref), custom_call_target="tpu_custom_call" | custom-call | tf_op jit(solution)/shard_map/weighted/pallas_call | solution.py:434
  133.4 7.7 %all-to-all-start.5 = ((bf16[16,48,128]{2,1,0:T(8,128)(2,1)}), bf16[16,48,128]{2,1,0:T(8,128)(2,1)S(1)}, u32[]{:S(2)}, u32[]{:S(2)}) async-start(bf16[16,48,128]{2,1,0:T(8,128)(2,1)} %bitcast.34), calls=%async_computation.5 | async-start | bytes 393216 | tf_op jit(solution)/shard_map/all_to_all | solution.py:437
  141.1 0.1 fusion.3
  141.2 0.7 reshape.269.idx_ref
  141.8 9.6 %all-to-all-done.5 = bf16[16,48,128]{2,1,0:T(8,128)(2,1)S(1)} async-done(((bf16[16,48,128]{2,1,0:T(8,128)(2,1)}), bf16[16,48,128]{2,1,0:T(8,128)(2,1)S(1)}, u32[]{:S(2)}, u32[]{:S(2)}) %all-to-all-start.5) | async-done | bytes 196640 | tf_op jit(solution)/shard_map/all_to_all | solution.py:437
  151.4 3.5 %scatter.1 = bf16[16,72,256]{2,1,0:T(8,128)(2,1)} custom-call(bf16[768,128]{1,0:T(8,128)(2,1)S(1)} %bitcast.30, s32[1,768]{1,0:T(1,128)} %reshape.269.idx_ref), custom_call_target="tpu_custom_call" | custom-call | tf_op jit(solution)/shard_map/scatter/pallas_call | solution.py:441
  154.9 3.6 %all-to-all-start.6 = ((bf16[16,72,256]{2,1,0:T(8,128)(2,1)}), bf16[16,72,256]{2,1,0:T(8,128)(2,1)S(1)}, u32[]{:S(2)}, u32[]{:S(2)}) async-start(bf16[16,72,256]{2,1,0:T(8,128)(2,1)} %scatter.1), calls=%async_computation.6 | async-start | bytes 1179648 | tf_op jit(solution)/shard_map/all_to_all | solution.py:450
  158.5 3.9 %residual.1.res_ref = bf16[256,1152]{1,0:T(8,128)(2,1)S(1)} custom-call(bf16[16,144,256]{2,1,0:T(8,128)(2,1)} %copy-done.1, bf16[256,1152]{1,0:T(8,128)(2,1)} %bitcast.33, bf16[1152,1152]{1,0:T(8,128)(2,1)} %w_ref.3, f32[1,1152]{1,0:T(1,128)} %broadcast_in_dim.80.b_ref, f32[4,1152]{1,0:T(4,128)} %bitcast.41), custom_call_target="tpu_custom_call" | custom-call | tf_op jit(solution)/shard_map/residual/pallas_call | solution.py:438
  162.4 8.6 %all-to-all-done.6 = bf16[16,72,256]{2,1,0:T(8,128)(2,1)S(1)} async-done(((bf16[16,72,256]{2,1,0:T(8,128)(2,1)}), bf16[16,72,256]{2,1,0:T(8,128)(2,1)S(1)}, u32[]{:S(2)}, u32[]{:S(2)}) %all-to-all-start.6) | async-done | bytes 589856 | tf_op jit(solution)/shard_map/all_to_all | solution.py:450
  171.0 1.9 %final.1 = bf16[256,1152]{1,0:T(8,128)(2,1)} custom-call(bf16[1152,256]{1,0:T(8,128)(2,1)S(1)} %bitcast.29, bf16[256,1152]{1,0:T(8,128)(2,1)S(1)} %residual.1.res_ref, f32[4,1152]{1,0:T(4,128)} %bitcast.42), custom_call_target="tpu_custom_call" | custom-call | tf_op jit(solution)/shard_map/final/pallas_call | solution.py:451
  (37 shorter events, 0.1 us)
Async XLA Ops:
  3.5 7.8 %copy-start.5 = (bf16[1152,16]{0,1:T(8,128)(2,1)S(1)}, bf16[1152,16]{0,1:T(8,128)(2,1)}, u32[]{:S(2)}) copy-start(bf16[1152,16]{0,1:T(8,128)(2,1)} %param.21) | copy-start | bytes 110596
  3.5 7.9 %copy-start.8 = (f32[1152]{0:T(1024)S(1)}, f32[1152]{0:T(1024)}, u32[]{:S(2)}) copy-start(f32[1152]{0:T(1024)} %param.20) | copy-start | bytes 13828
  3.5 8.5 %copy-start.9 = (s32[16,1]{0,1:T(1,128)S(1)}, s32[16,1]{0,1:T(1,128)}, u32[]{:S(2)}) copy-start(s32[16,1]{0,1:T(1,128)} %param.26) | copy-start | bytes 196
  3.5 30.2 %copy-start.6 = (s32[16,1,48]{2,1,0:T(1,128)S(1)}, s32[16,1,48]{2,1,0:T(1,128)}, u32[]{:S(2)}) copy-start(s32[16,1,48]{2,1,0:T(1,128)} %param.27) | copy-start | bytes 9220
  3.5 39.4 %all-to-all-start = ((bf16[16,288,256]{2,1,0:T(8,128)(2,1)}), bf16[16,288,256]{2,1,0:T(8,128)(2,1)S(1)}, u32[]{:S(2)}, u32[]{:S(2)}) async-start(bf16[16,288,256]{2,1,0:T(8,128)(2,1)} %split.1), calls=%async_computation | async-start | bytes 4718592 | tf_op jit(solution)/shard_map/all_to_all | solution.py:348
  32.9 0.5 copy-start.10
  32.9 0.8 copy-start.12
  42.9 7.3 %copy-start.2 = (bf16[16,288,256]{2,1,0:T(8,128)(2,1)}, bf16[16,288,256]{2,1,0:T(8,128)(2,1)S(1)}, u32[]{:S(2)}) copy-start(bf16[16,288,256]{2,1,0:T(8,128)(2,1)S(1)} %all-to-all-done.r_ref.refs_0_.refs_1_) | copy-start | bytes 7077892
  50.2 12.3 %all-to-all-start.1 = ((bf16[16,48,144]{2,1,0:T(8,128)(2,1)}), bf16[16,48,144]{2,1,0:T(8,128)(2,1)}, u32[]{:S(2)}, u32[]{:S(2)}) async-start(bf16[16,48,144]{2,1,0:T(8,128)(2,1)} %bitcast.39), calls=%async_computation.1 | async-start | bytes 786432 | tf_op jit(solution)/shard_map/all_to_all | solution.py:397
  54.6 7.9 %copy-start = (bf16[1152,1152]{1,0:T(8,128)(2,1)S(1)}, bf16[1152,1152]{1,0:T(8,128)(2,1)}, u32[]{:S(2)}) copy-start(bf16[1152,1152]{1,0:T(8,128)(2,1)} %w_ref.3) | copy-start | bytes 7962628
  65.0 21.9 %all-to-all-start.2 = ((bf16[16,3,1152]{2,1,0:T(4,128)(2,1)}), bf16[16,3,1152]{2,1,0:T(4,128)(2,1)S(1)}, u32[]{:S(2)}, u32[]{:S(2)}) async-start(bf16[16,3,1152]{2,1,0:T(4,128)(2,1)} %normed.1), calls=%async_computation.2 | async-start | bytes 294912 | tf_op jit(solution)/shard_map/all_to_all | solution.py:403
  87.9 16.6 %all-to-all-start.3 = ((bf16[16,16,1152]{2,1,0:T(8,128)(2,1)}), bf16[16,16,1152]{2,1,0:T(8,128)(2,1)S(1)}, u32[]{:S(2)}, u32[]{:S(2)}) async-start(bf16[16,16,1152]{2,1,0:T(8,128)(2,1)} %compact.1), calls=%async_computation.3 | async-start | bytes 1179648 | tf_op jit(solution)/shard_map/all_to_all | solution.py:409
  92.8 11.7 %copy-start.3 = (bf16[1,1152,288]{1,2,0:T(8,128)(2,1)S(1)}, bf16[1,1152,288]{1,2,0:T(8,128)(2,1)}, u32[]{:S(2)}) copy-start(bf16[1,1152,288]{1,2,0:T(8,128)(2,1)} %param.22) | copy-start | bytes 1990660
  92.8 11.7 %copy-start.4 = (f32[1,288]{1,0:T(1,128)S(1)}, f32[1,288]{1,0:T(1,128)}, u32[]{:S(2)}) copy-start(f32[1,288]{1,0:T(1,128)} %be_ref.1) | copy-start | bytes 3460
  107.7 6.6 %copy-start.14 = (f32[1,1152]{1,0:T(1,128)S(1)}, f32[1,1152]{1,0:T(1,128)}, u32[]{:S(2)}) copy-start(f32[1,1152]{1,0:T(1,128)} %param.25) | copy-start | bytes 13828
  107.7 6.8 %copy-start.11 = (s32[16]{0:T(128)S(1)}, s32[16]{0:T(128)}, u32[]{:S(2)}) copy-start(s32[16]{0:T(128)} %copy-done.10) | copy-start | bytes 196
  107.8 6.8 %copy-start.13 = (s32[16]{0:T(128)S(1)}, s32[16]{0:T(128)}, u32[]{:S(2)}) copy-start(s32[16]{0:T(128)} %copy-done.12) | copy-start | bytes 196
  107.8 23.6 %all-to-all-start.4 = ((bf16[16,144,256]{2,1,0:T(8,128)(2,1)}), bf16[16,144,256]{2,1,0:T(8,128)(2,1)S(1)}, u32[]{:S(2)}, u32[]{:S(2)}) async-start(bf16[16,144,256]{2,1,0:T(8,128)(2,1)} %get-tuple-element.37), calls=%async_computation.4 | async-start | bytes 2359296 | tf_op jit(solution)/shard_map/all_to_all | solution.py:433
  114.4 26.7 %copy-start.7 = (s32[16,1,48]{2,1,0:T(1,128)S(1)}, s32[16,1,48]{2,1,0:T(1,128)}, u32[]{:S(2)}) copy-start(s32[16,1,48]{2,1,0:T(1,128)} %param.27) | copy-start | bytes 9220
  131.4 23.5 %copy-start.1 = (bf16[16,144,256]{2,1,0:T(8,128)(2,1)}, bf16[16,144,256]{2,1,0:T(8,128)(2,1)S(1)}, u32[]{:S(2)}) copy-start(bf16[16,144,256]{2,1,0:T(8,128)(2,1)S(1)} %all-to-all-done.4.x_ref.o_ref) | copy-start | bytes 3538948
  133.4 18.0 %all-to-all-start.5 = ((bf16[16,48,128]{2,1,0:T(8,128)(2,1)}), bf16[16,48,128]{2,1,0:T(8,128)(2,1)S(1)}, u32[]{:S(2)}, u32[]{:S(2)}) async-start(bf16[16,48,128]{2,1,0:T(8,128)(2,1)} %bitcast.34), calls=%async_computation.5 | async-start | bytes 393216 | tf_op jit(solution)/shard_map/all_to_all | solution.py:437
  154.9 16.1 %all-to-all-start.6 = ((bf16[16,72,256]{2,1,0:T(8,128)(2,1)}), bf16[16,72,256]{2,1,0:T(8,128)(2,1)S(1)}, u32[]{:S(2)}, u32[]{:S(2)}) async-start(bf16[16,72,256]{2,1,0:T(8,128)(2,1)} %scatter.1), calls=%async_computation.6 | async-start | bytes 1179648 | tf_op jit(solution)/shard_map/all_to_all | solution.py:450

commit v6 on v5

--- a/solution.py
+++ b/solution.py
@@ -14,7 +14,7 @@
 TL = 256
 F32 = jnp.float32
 BF16 = jnp.bfloat16
-SCALE = 1.0 / math.sqrt(HD)
+EXP_SCALE = math.log2(math.e) / math.sqrt(HD)
 
 
 def nt(left, right):
@@ -84,7 +84,7 @@
 
 
 def value_part(top, v_ref, s_ref, j, total):
-    weights = jnp.exp((s_ref[j * TL : (j + 1) * TL, :] - top) * SCALE).astype(BF16)
+    weights = jnp.exp2((s_ref[j * TL : (j + 1) * TL, :] - top) * EXP_SCALE).astype(BF16)
     part = nn(v_ref[:, j * TL : (j + 1) * TL], weights)
     return part if total is None else total + part
 

time: 174 us -> 173 us (level)
  no operation moved by 1% of the time
where the time goes in v6:
time: 173 us; the launch traced here: 172 us
  Pallas kernels  53.9 us (31%)
  starting transfers between devices  46.9 us (27%)
  waiting for transfers between devices  44.5 us (26%)
  blocking collectives  20.6 us (12%)
  local copies, waits for them, and re-layouts  4.16 us (2%)
  other arithmetic  1.8 us (1%)
    pallas_call x3, Pallas kernels, main_part(): pl.pallas_call(functools.partial(main_kernel, steps, aliased), grid=(step...  25.3 us
    all_gather x1, blocking collectives, per_device(): all_counts = lax.all_gather(own_counts, 'frame', axis=1)  20.6 us
    all_to_all x1, waiting for transfers between devices, per_device(): both = exchange(both, 'tok')  16.6 us
    all_to_all x1, starting transfers between devices, per_device(): normed = exchange(normed, 'frame')  12.5 us
    all_to_all x1, waiting for transfers between devices, per_device(): outs = exchange(outs.reshape(16, 48, 128), 'frame')  9.58 us
    all_to_all x1, waiting for transfers between devices, per_device(): mixed = exchange(mixed, 'tok')  8.6 us
    all_to_all x1, starting transfers between devices, per_device(): heads = exchange(sent, 'tok')  7.72 us
    all_to_all x1, starting transfers between devices, per_device(): outs = exchange(outs.reshape(16, 48, 128), 'frame')  7.54 us
  transfers between devices with their start and end apart: 7, of which 7 were waited for; matrix products, arithmetic and copies ran while one was open for 3% of the time, Pallas kernels for 17%

profile of v6, /device:TPU:1, one launch (start us, length us, event | category | flops | bytes accessed | tf_op | source)
XLA Modules:
  0.0 172.2 jit_solution(17130428178632504191)
XLA Ops:
  0.0 3.5 %split.1 = bf16[16,288,256]{2,1,0:T(8,128)(2,1)} custom-call(bf16[256,1152]{1,0:T(8,128)(2,1)} %bitcast.36, bf16[256,1152]{1,0:T(8,128)(2,1)} %bitcast.37, bf16[256,1152]{1,0:T(8,128)(2,1)} %bitcast.38, bf16[256,1152]{1,0:T(8,128)(2,1)} %bitcast.32), custom_call_target="tpu_custom_call" | custom-call | tf_op jit(solution)/shard_map/split/pallas_call | solution.py:332
  3.5 0.0 copy-start.5
  3.5 7.7 %all-to-all-start = ((bf16[16,288,256]{2,1,0:T(8,128)(2,1)}), bf16[16,288,256]{2,1,0:T(8,128)(2,1)S(1)}, u32[]{:S(2)}, u32[]{:S(2)}) async-start(bf16[16,288,256]{2,1,0:T(8,128)(2,1)} %split.1), calls=%async_computation | async-start | bytes 4718592 | tf_op jit(solution)/shard_map/all_to_all | solution.py:348
  11.3 0.1 select_reduce_fusion.1
  11.4 0.6 broadcast_in_dim.80.b_ref
  12.0 20.6 %all-gather = s32[16,1,16]{2,1,0:T(1,128)S(1)} all-gather(s32[1,1,16]{2,1,0:T(1,128)S(1)} %bitcast.46), channel_id=1, replica_groups=mesh['frame'=16,'tok'=16] {'frame'}, dimensions={0}, use_global_device_ids=true | all-gather | bytes 1088 | tf_op jit(solution)/shard_map/all_gather | solution.py:351
  32.6 0.1 copy.27
  32.7 0.1 multiply_reduce_fusion
  32.8 0.1 multiply_reduce_fusion.2
  32.9 0.5 copy-done.10
  33.4 0.1 fusion.1
  33.5 0.1 select_n.58.idx_ref
  33.6 0.1 broadcast_add_fusion
  33.7 1.0 select_reduce_fusion
  34.8 0.1 compare_select_fusion
  34.8 0.2 copy.28
  35.0 0.2 select_n.55.idx_ref
  35.2 1.5 copy.29
  36.7 6.2 %all-to-all-done.r_ref.refs_0_.refs_1_ = bf16[16,288,256]{2,1,0:T(8,128)(2,1)S(1)} async-done(((bf16[16,288,256]{2,1,0:T(8,128)(2,1)}), bf16[16,288,256]{2,1,0:T(8,128)(2,1)S(1)}, u32[]{:S(2)}, u32[]{:S(2)}) %all-to-all-start) | async-done | bytes 2359328 | tf_op jit(solution)/shard_map/all_to_all | solution.py:348
  42.9 7.0 %picked_attention.1 = (bf16[768,144]{1,0:T(8,128)(2,1)}, bf16[4096,128]{1,0:T(8,128)(2,1)}, bf16[80,4096]{1,0:T(8,128)(2,1)}) custom-call(s32[1,768]{1,0:T(1,128)S(1)} %select_n.55.idx_ref, bf16[16,288,256]{2,1,0:T(8,128)(2,1)S(1)} %all-to-all-done.r_ref.refs_0_.refs_1_), custom_call_target="tpu_custom_call" | custom-call | tf_op jit(solution)/shard_map/picked_attention/pallas_call | solution.py:380
  49.9 4.4 %all-to-all-start.1 = ((bf16[16,48,144]{2,1,0:T(8,128)(2,1)}), bf16[16,48,144]{2,1,0:T(8,128)(2,1)}, u32[]{:S(2)}, u32[]{:S(2)}) async-start(bf16[16,48,144]{2,1,0:T(8,128)(2,1)} %bitcast.39), calls=%async_computation.1 | async-start | bytes 786432 | tf_op jit(solution)/shard_map/all_to_all | solution.py:397
  54.3 7.0 %main_attention.3.refs_4_ = bf16[16,144,256]{2,1,0:T(8,128)(2,1)} custom-call(bf16[16,288,256]{2,1,0:T(8,128)(2,1)} %copy-done.2, bf16[16,288,256]{2,1,0:T(8,128)(2,1)} %copy-done.2, bf16[4096,128]{1,0:T(8,128)(2,1)} %get-tuple-element.27.refs_2_, bf16[80,4096]{1,0:T(8,128)(2,1)} %get-tuple-element.28.refs_3_), custom_call_target="tpu_custom_call" | custom-call | flops 4294967296 | bytes 2097152 | tf_op jit(solution)/shard_map/main_attention/pallas_call | solution.py:179
  61.4 0.8 all-to-all-done.1.x_ref
  62.2 2.6 %normed.1 = bf16[16,3,1152]{2,1,0:T(4,128)(2,1)} custom-call(bf16[16,48,144]{2,1,0:T(8,128)(2,1)} %all-to-all-done.1.x_ref, bf16[1152,1152]{1,0:T(8,128)(2,1)S(1)} %copy-done, f32[1,1152]{1,0:T(1,128)} %broadcast_in_dim.80.b_ref, f32[4,1152]{1,0:T(4,128)} %bitcast.40), custom_call_target="tpu_custom_call" | custom-call | tf_op jit(solution)/shard_map/normed/pallas_call | solution.py:400
  64.8 12.5 %all-to-all-start.2 = ((bf16[16,3,1152]{2,1,0:T(4,128)(2,1)}), bf16[16,3,1152]{2,1,0:T(4,128)(2,1)S(1)}, u32[]{:S(2)}, u32[]{:S(2)}) async-start(bf16[16,3,1152]{2,1,0:T(4,128)(2,1)} %normed.1), calls=%async_computation.2 | async-start | bytes 294912 | tf_op jit(solution)/shard_map/all_to_all | solution.py:403
  77.3 6.9 %main_attention.4.refs_4_ = bf16[16,144,256]{2,1,0:T(8,128)(2,1)} custom-call(bf16[16,288,256]{2,1,0:T(8,128)(2,1)} %copy-done.2, bf16[16,288,256]{2,1,0:T(8,128)(2,1)} %copy-done.2, bf16[4096,128]{1,0:T(8,128)(2,1)} %get-tuple-element.27.refs_2_, bf16[80,4096]{1,0:T(8,128)(2,1)} %get-tuple-element.28.refs_3_, ...), custom_call_target="tpu_custom_call", output_to_operand_aliasing={{}: (4, {})} | custom-call | flops 4294967296 | bytes 2097152 | tf_op jit(solution)/shard_map/main_attention/pallas_call | solution.py:179
  84.2 2.4 %all-to-all-done.2.x_ref = bf16[16,3,1152]{2,1,0:T(4,128)(2,1)S(1)} async-done(((bf16[16,3,1152]{2,1,0:T(4,128)(2,1)}), bf16[16,3,1152]{2,1,0:T(4,128)(2,1)S(1)}, u32[]{:S(2)}, u32[]{:S(2)}) %all-to-all-start.2) | async-done | bytes 110624 | tf_op jit(solution)/shard_map/all_to_all | solution.py:403
  86.6 1.0 compact.1
  87.7 4.8 %all-to-all-start.3 = ((bf16[16,16,1152]{2,1,0:T(8,128)(2,1)}), bf16[16,16,1152]{2,1,0:T(8,128)(2,1)S(1)}, u32[]{:S(2)}, u32[]{:S(2)}) async-start(bf16[16,16,1152]{2,1,0:T(8,128)(2,1)} %compact.1), calls=%async_computation.3 | async-start | bytes 1179648 | tf_op jit(solution)/shard_map/all_to_all | solution.py:409
  92.5 11.4 %main_attention.5._ = bf16[16,144,256]{2,1,0:T(8,128)(2,1)} custom-call(bf16[16,288,256]{2,1,0:T(8,128)(2,1)} %copy-done.2, bf16[16,288,256]{2,1,0:T(8,128)(2,1)} %copy-done.2, bf16[4096,128]{1,0:T(8,128)(2,1)} %get-tuple-element.27.refs_2_, bf16[80,4096]{1,0:T(8,128)(2,1)} %get-tuple-element.28.refs_3_, ...), custom_call_target="tpu_custom_call", output_to_operand_aliasing={{}: (4, {})} | custom-call | flops 8589934592 | bytes 2097152 | tf_op jit(solution)/shard_map/main_attention/pallas_call | solution.py:179
  103.8 0.3 all-to-all-done.3
  104.2 3.2 %expert.1 = (bf16[16,144,256]{2,1,0:T(8,128)(2,1)}, f32[8,256]{1,0:T(8,128)}) custom-call(bf16[256,1152]{1,0:T(8,128)(2,1)S(1)} %bitcast.28, f32[1,288]{1,0:T(1,128)S(1)} %copy-done.4, bf16[1,1152]{1,0:T(2,128)(2,1)S(1)} %broadcast_in_dim.79.router_ref, bf16[288,1152]{1,0:T(8,128)(2,1)S(1)} %bitcast.31, ...), custom_call_target="tpu_custom_call", output_to_operand_aliasing={{0}: (5, {})} | custom-call | tf_op jit(solution)/shard_map/expert/pallas_call | solution.py:412
  107.4 6.4 %all-to-all-start.4 = ((bf16[16,144,256]{2,1,0:T(8,128)(2,1)}), bf16[16,144,256]{2,1,0:T(8,128)(2,1)S(1)}, u32[]{:S(2)}, u32[]{:S(2)}) async-start(bf16[16,144,256]{2,1,0:T(8,128)(2,1)} %get-tuple-element.37), calls=%async_computation.4 | async-start | bytes 2359296 | tf_op jit(solution)/shard_map/all_to_all | solution.py:433
  113.8 0.1 reshape_squeeze.3
  113.9 0.1 add_select_fusion
  114.0 0.1 reshape.272.idx_ref
  114.1 0.1 copy.30.rb_ref
  114.2 16.6 %all-to-all-done.4.x_ref.o_ref = bf16[16,144,256]{2,1,0:T(8,128)(2,1)S(1)} async-done(((bf16[16,144,256]{2,1,0:T(8,128)(2,1)}), bf16[16,144,256]{2,1,0:T(8,128)(2,1)S(1)}, u32[]{:S(2)}, u32[]{:S(2)}) %all-to-all-start.4) | async-done | bytes 1179680 | tf_op jit(solution)/shard_map/all_to_all | solution.py:433
  130.8 2.0 %weighted.1 = bf16[768,128]{1,0:T(8,128)(2,1)} custom-call(bf16[16,144,256]{2,1,0:T(8,128)(2,1)S(1)} %all-to-all-done.4.x_ref.o_ref, f32[8,256]{1,0:T(8,128)} %get-tuple-element.39.gate_ref, f32[72,1]{1,0:T(8,128)S(1)} %copy.30.rb_ref, s32[1,768]{1,0:T(1,128)S(1)} %reshape.272.idx_ref), custom_call_target="tpu_custom_call" | custom-call | tf_op jit(solution)/shard_map/weighted/pallas_call | solution.py:434
  132.8 7.5 %all-to-all-start.5 = ((bf16[16,48,128]{2,1,0:T(8,128)(2,1)}), bf16[16,48,128]{2,1,0:T(8,128)(2,1)S(1)}, u32[]{:S(2)}, u32[]{:S(2)}) async-start(bf16[16,48,128]{2,1,0:T(8,128)(2,1)} %bitcast.34), calls=%async_computation.5 | async-start | bytes 393216 | tf_op jit(solution)/shard_map/all_to_all | solution.py:437
  140.4 0.1 fusion.3
  140.4 0.7 reshape.269.idx_ref
  141.1 9.6 %all-to-all-done.5 = bf16[16,48,128]{2,1,0:T(8,128)(2,1)S(1)} async-done(((bf16[16,48,128]{2,1,0:T(8,128)(2,1)}), bf16[16,48,128]{2,1,0:T(8,128)(2,1)S(1)}, u32[]{:S(2)}, u32[]{:S(2)}) %all-to-all-start.5) | async-done | bytes 196640 | tf_op jit(solution)/shard_map/all_to_all | solution.py:437
  150.7 3.5 %scatter.1 = bf16[16,72,256]{2,1,0:T(8,128)(2,1)} custom-call(bf16[768,128]{1,0:T(8,128)(2,1)S(1)} %bitcast.30, s32[1,768]{1,0:T(1,128)} %reshape.269.idx_ref), custom_call_target="tpu_custom_call" | custom-call | tf_op jit(solution)/shard_map/scatter/pallas_call | solution.py:441
  154.2 3.6 %all-to-all-start.6 = ((bf16[16,72,256]{2,1,0:T(8,128)(2,1)}), bf16[16,72,256]{2,1,0:T(8,128)(2,1)S(1)}, u32[]{:S(2)}, u32[]{:S(2)}) async-start(bf16[16,72,256]{2,1,0:T(8,128)(2,1)} %scatter.1), calls=%async_computation.6 | async-start | bytes 1179648 | tf_op jit(solution)/shard_map/all_to_all | solution.py:450
  157.8 3.9 %residual.1.res_ref = bf16[256,1152]{1,0:T(8,128)(2,1)S(1)} custom-call(bf16[16,144,256]{2,1,0:T(8,128)(2,1)} %copy-done.1, bf16[256,1152]{1,0:T(8,128)(2,1)} %bitcast.33, bf16[1152,1152]{1,0:T(8,128)(2,1)} %w_ref.3, f32[1,1152]{1,0:T(1,128)} %broadcast_in_dim.80.b_ref, f32[4,1152]{1,0:T(4,128)} %bitcast.41), custom_call_target="tpu_custom_call" | custom-call | tf_op jit(solution)/shard_map/residual/pallas_call | solution.py:438
  161.7 8.6 %all-to-all-done.6 = bf16[16,72,256]{2,1,0:T(8,128)(2,1)S(1)} async-done(((bf16[16,72,256]{2,1,0:T(8,128)(2,1)}), bf16[16,72,256]{2,1,0:T(8,128)(2,1)S(1)}, u32[]{:S(2)}, u32[]{:S(2)}) %all-to-all-start.6) | async-done | bytes 589856 | tf_op jit(solution)/shard_map/all_to_all | solution.py:450
  170.3 1.9 %final.1 = bf16[256,1152]{1,0:T(8,128)(2,1)} custom-call(bf16[1152,256]{1,0:T(8,128)(2,1)S(1)} %bitcast.29, bf16[256,1152]{1,0:T(8,128)(2,1)S(1)} %residual.1.res_ref, f32[4,1152]{1,0:T(4,128)} %bitcast.42), custom_call_target="tpu_custom_call" | custom-call | tf_op jit(solution)/shard_map/final/pallas_call | solution.py:451
  (37 shorter events, 0.1 us)
Async XLA Ops:
  3.5 7.8 %copy-start.5 = (bf16[1152,16]{0,1:T(8,128)(2,1)S(1)}, bf16[1152,16]{0,1:T(8,128)(2,1)}, u32[]{:S(2)}) copy-start(bf16[1152,16]{0,1:T(8,128)(2,1)} %param.21) | copy-start | bytes 110596
  3.5 7.9 %copy-start.8 = (f32[1152]{0:T(1024)S(1)}, f32[1152]{0:T(1024)}, u32[]{:S(2)}) copy-start(f32[1152]{0:T(1024)} %param.20) | copy-start | bytes 13828
  3.5 8.5 %copy-start.9 = (s32[16,1]{0,1:T(1,128)S(1)}, s32[16,1]{0,1:T(1,128)}, u32[]{:S(2)}) copy-start(s32[16,1]{0,1:T(1,128)} %param.26) | copy-start | bytes 196
  3.5 30.2 %copy-start.6 = (s32[16,1,48]{2,1,0:T(1,128)S(1)}, s32[16,1,48]{2,1,0:T(1,128)}, u32[]{:S(2)}) copy-start(s32[16,1,48]{2,1,0:T(1,128)} %param.27) | copy-start | bytes 9220
  3.5 39.4 %all-to-all-start = ((bf16[16,288,256]{2,1,0:T(8,128)(2,1)}), bf16[16,288,256]{2,1,0:T(8,128)(2,1)S(1)}, u32[]{:S(2)}, u32[]{:S(2)}) async-start(bf16[16,288,256]{2,1,0:T(8,128)(2,1)} %split.1), calls=%async_computation | async-start | bytes 4718592 | tf_op jit(solution)/shard_map/all_to_all | solution.py:348
  32.9 0.5 copy-start.10
  32.9 0.8 copy-start.12
  42.9 7.0 %copy-start.2 = (bf16[16,288,256]{2,1,0:T(8,128)(2,1)}, bf16[16,288,256]{2,1,0:T(8,128)(2,1)S(1)}, u32[]{:S(2)}) copy-start(bf16[16,288,256]{2,1,0:T(8,128)(2,1)S(1)} %all-to-all-done.r_ref.refs_0_.refs_1_) | copy-start | bytes 7077892
  49.9 12.2 %all-to-all-start.1 = ((bf16[16,48,144]{2,1,0:T(8,128)(2,1)}), bf16[16,48,144]{2,1,0:T(8,128)(2,1)}, u32[]{:S(2)}, u32[]{:S(2)}) async-start(bf16[16,48,144]{2,1,0:T(8,128)(2,1)} %bitcast.39), calls=%async_computation.1 | async-start | bytes 786432 | tf_op jit(solution)/shard_map/all_to_all | solution.py:397
  54.3 7.8 %copy-start = (bf16[1152,1152]{1,0:T(8,128)(2,1)S(1)}, bf16[1152,1152]{1,0:T(8,128)(2,1)}, u32[]{:S(2)}) copy-start(bf16[1152,1152]{1,0:T(8,128)(2,1)} %w_ref.3) | copy-start | bytes 7962628
  64.8 21.9 %all-to-all-start.2 = ((bf16[16,3,1152]{2,1,0:T(4,128)(2,1)}), bf16[16,3,1152]{2,1,0:T(4,128)(2,1)S(1)}, u32[]{:S(2)}, u32[]{:S(2)}) async-start(bf16[16,3,1152]{2,1,0:T(4,128)(2,1)} %normed.1), calls=%async_computation.2 | async-start | bytes 294912 | tf_op jit(solution)/shard_map/all_to_all | solution.py:403
  87.7 16.5 %all-to-all-start.3 = ((bf16[16,16,1152]{2,1,0:T(8,128)(2,1)}), bf16[16,16,1152]{2,1,0:T(8,128)(2,1)S(1)}, u32[]{:S(2)}, u32[]{:S(2)}) async-start(bf16[16,16,1152]{2,1,0:T(8,128)(2,1)} %compact.1), calls=%async_computation.3 | async-start | bytes 1179648 | tf_op jit(solution)/shard_map/all_to_all | solution.py:409
  92.4 11.7 %copy-start.3 = (bf16[1,1152,288]{1,2,0:T(8,128)(2,1)S(1)}, bf16[1,1152,288]{1,2,0:T(8,128)(2,1)}, u32[]{:S(2)}) copy-start(bf16[1,1152,288]{1,2,0:T(8,128)(2,1)} %param.22) | copy-start | bytes 1990660
  92.5 11.7 %copy-start.4 = (f32[1,288]{1,0:T(1,128)S(1)}, f32[1,288]{1,0:T(1,128)}, u32[]{:S(2)}) copy-start(f32[1,288]{1,0:T(1,128)} %be_ref.1) | copy-start | bytes 3460
  107.4 6.4 %copy-start.14 = (f32[1,1152]{1,0:T(1,128)S(1)}, f32[1,1152]{1,0:T(1,128)}, u32[]{:S(2)}) copy-start(f32[1,1152]{1,0:T(1,128)} %param.25) | copy-start | bytes 13828
  107.4 6.5 %copy-start.11 = (s32[16]{0:T(128)S(1)}, s32[16]{0:T(128)}, u32[]{:S(2)}) copy-start(s32[16]{0:T(128)} %copy-done.10) | copy-start | bytes 196
  107.4 6.5 %copy-start.13 = (s32[16]{0:T(128)S(1)}, s32[16]{0:T(128)}, u32[]{:S(2)}) copy-start(s32[16]{0:T(128)} %copy-done.12) | copy-start | bytes 196
  107.4 23.4 %all-to-all-start.4 = ((bf16[16,144,256]{2,1,0:T(8,128)(2,1)}), bf16[16,144,256]{2,1,0:T(8,128)(2,1)S(1)}, u32[]{:S(2)}, u32[]{:S(2)}) async-start(bf16[16,144,256]{2,1,0:T(8,128)(2,1)} %get-tuple-element.37), calls=%async_computation.4 | async-start | bytes 2359296 | tf_op jit(solution)/shard_map/all_to_all | solution.py:433
  113.8 26.6 %copy-start.7 = (s32[16,1,48]{2,1,0:T(1,128)S(1)}, s32[16,1,48]{2,1,0:T(1,128)}, u32[]{:S(2)}) copy-start(s32[16,1,48]{2,1,0:T(1,128)} %param.27) | copy-start | bytes 9220
  130.8 23.4 %copy-start.1 = (bf16[16,144,256]{2,1,0:T(8,128)(2,1)}, bf16[16,144,256]{2,1,0:T(8,128)(2,1)S(1)}, u32[]{:S(2)}) copy-start(bf16[16,144,256]{2,1,0:T(8,128)(2,1)S(1)} %all-to-all-done.4.x_ref.o_ref) | copy-start | bytes 3538948
  132.8 17.9 %all-to-all-start.5 = ((bf16[16,48,128]{2,1,0:T(8,128)(2,1)}), bf16[16,48,128]{2,1,0:T(8,128)(2,1)S(1)}, u32[]{:S(2)}, u32[]{:S(2)}) async-start(bf16[16,48,128]{2,1,0:T(8,128)(2,1)} %bitcast.34), calls=%async_computation.5 | async-start | bytes 393216 | tf_op jit(solution)/shard_map/all_to_all | solution.py:437
  154.2 16.1 %all-to-all-start.6 = ((bf16[16,72,256]{2,1,0:T(8,128)(2,1)}), bf16[16,72,256]{2,1,0:T(8,128)(2,1)S(1)}, u32[]{:S(2)}, u32[]{:S(2)}) async-start(bf16[16,72,256]{2,1,0:T(8,128)(2,1)} %scatter.1), calls=%async_computation.6 | async-start | bytes 1179648 | tf_op jit(solution)/shard_map/all_to_all | solution.py:450

commit v7 on v6

--- a/solution.py
+++ b/solution.py
@@ -75,9 +75,9 @@
 
 
 def score_part(q, k_ref, s_ref, j, top):
-    scores = nn(k_ref[j * 512 : (j + 1) * 512, :], q)
-    s_ref[j * 512 : (j + 1) * 512, :] = scores
-    for b in range(64):
+    scores = nn(k_ref[j * TL : (j + 1) * TL, :], q)
+    s_ref[j * TL : (j + 1) * TL, :] = scores
+    for b in range(TL // 8):
         part = scores[b * 8 : (b + 1) * 8]
         top = part if top is None else jnp.maximum(top, part)
     return top
@@ -96,8 +96,8 @@
 def interleave(q, top, k_ref, v_ref, next_ref, s_ref):
     new_top, total = None, None
     for j in range(16):
-        if q is not None and j % 2 == 0:
-            new_top = score_part(q, k_ref, next_ref, j // 2, new_top)
+        if q is not None:
+            new_top = score_part(q, k_ref, next_ref, j, new_top)
         if top is not None:
             total = value_part(top, v_ref, s_ref, j, total)
     if q is not None:

time: 173 us -> 173 us (level)
  transfers between devices with their start and end apart: 7 -> 7, of which waited for: 7 -> 7; matrix products, arithmetic and copies ran while one was open for 3% -> 3% of each run, Pallas kernels for 17% -> 16%
where the time goes in v7:
time: 173 us; the launch traced here: 172 us
  Pallas kernels  53.1 us (31%)
  starting transfers between devices  46.2 us (27%)
  waiting for transfers between devices  45.5 us (26%)
  blocking collectives  20.6 us (12%)
  local copies, waits for them, and re-layouts  4.16 us (2%)
  other arithmetic  1.8 us (1%)
    pallas_call x3, Pallas kernels, main_part(): pl.pallas_call(functools.partial(main_kernel, steps, aliased), grid=(step...  24.4 us
    all_gather x1, blocking collectives, per_device(): all_counts = lax.all_gather(own_counts, 'frame', axis=1)  20.6 us
    all_to_all x1, waiting for transfers between devices, per_device(): both = exchange(both, 'tok')  16.6 us
    all_to_all x1, starting transfers between devices, per_device(): normed = exchange(normed, 'frame')  12.5 us
    all_to_all x1, waiting for transfers between devices, per_device(): outs = exchange(outs.reshape(16, 48, 128), 'frame')  9.58 us
    all_to_all x1, waiting for transfers between devices, per_device(): mixed = exchange(mixed, 'tok')  8.6 us
    all_to_all x1, starting transfers between devices, per_device(): heads = exchange(sent, 'tok')  7.72 us
    all_to_all x1, starting transfers between devices, per_device(): outs = exchange(outs.reshape(16, 48, 128), 'frame')  7.32 us
  transfers between devices with their start and end apart: 7, of which 7 were waited for; matrix products, arithmetic and copies ran while one was open for 3% of the time, Pallas kernels for 16%

profile of v7, /device:TPU:1, one launch (start us, length us, event | category | flops | bytes accessed | tf_op | source)
XLA Modules:
  0.0 171.6 jit_solution(13287187911958594293)
XLA Ops:
  0.0 3.5 %split.1 = bf16[16,288,256]{2,1,0:T(8,128)(2,1)} custom-call(bf16[256,1152]{1,0:T(8,128)(2,1)} %bitcast.36, bf16[256,1152]{1,0:T(8,128)(2,1)} %bitcast.37, bf16[256,1152]{1,0:T(8,128)(2,1)} %bitcast.38, bf16[256,1152]{1,0:T(8,128)(2,1)} %bitcast.32), custom_call_target="tpu_custom_call" | custom-call | tf_op jit(solution)/shard_map/split/pallas_call | solution.py:332
  3.5 0.0 copy-start.5
  3.5 7.7 %all-to-all-start = ((bf16[16,288,256]{2,1,0:T(8,128)(2,1)}), bf16[16,288,256]{2,1,0:T(8,128)(2,1)S(1)}, u32[]{:S(2)}, u32[]{:S(2)}) async-start(bf16[16,288,256]{2,1,0:T(8,128)(2,1)} %split.1), calls=%async_computation | async-start | bytes 4718592 | tf_op jit(solution)/shard_map/all_to_all | solution.py:348
  11.3 0.1 select_reduce_fusion.1
  11.4 0.6 broadcast_in_dim.80.b_ref
  12.0 20.6 %all-gather = s32[16,1,16]{2,1,0:T(1,128)S(1)} all-gather(s32[1,1,16]{2,1,0:T(1,128)S(1)} %bitcast.46), channel_id=1, replica_groups=mesh['frame'=16,'tok'=16] {'frame'}, dimensions={0}, use_global_device_ids=true | all-gather | bytes 1088 | tf_op jit(solution)/shard_map/all_gather | solution.py:351
  32.6 0.1 copy.27
  32.7 0.1 multiply_reduce_fusion
  32.8 0.1 multiply_reduce_fusion.2
  32.9 0.5 copy-done.10
  33.4 0.1 fusion.1
  33.5 0.1 select_n.58.idx_ref
  33.6 0.1 broadcast_add_fusion
  33.7 1.0 select_reduce_fusion
  34.8 0.1 compare_select_fusion
  34.8 0.2 copy.28
  35.0 0.2 select_n.55.idx_ref
  35.2 1.5 copy.29
  36.7 6.2 %all-to-all-done.r_ref.refs_0_.refs_1_ = bf16[16,288,256]{2,1,0:T(8,128)(2,1)S(1)} async-done(((bf16[16,288,256]{2,1,0:T(8,128)(2,1)}), bf16[16,288,256]{2,1,0:T(8,128)(2,1)S(1)}, u32[]{:S(2)}, u32[]{:S(2)}) %all-to-all-start) | async-done | bytes 2359328 | tf_op jit(solution)/shard_map/all_to_all | solution.py:348
  42.9 7.1 %picked_attention.1 = (bf16[768,144]{1,0:T(8,128)(2,1)}, bf16[4096,128]{1,0:T(8,128)(2,1)}, bf16[80,4096]{1,0:T(8,128)(2,1)}) custom-call(s32[1,768]{1,0:T(1,128)S(1)} %select_n.55.idx_ref, bf16[16,288,256]{2,1,0:T(8,128)(2,1)S(1)} %all-to-all-done.r_ref.refs_0_.refs_1_), custom_call_target="tpu_custom_call" | custom-call | tf_op jit(solution)/shard_map/picked_attention/pallas_call | solution.py:380
  50.1 4.4 %all-to-all-start.1 = ((bf16[16,48,144]{2,1,0:T(8,128)(2,1)}), bf16[16,48,144]{2,1,0:T(8,128)(2,1)}, u32[]{:S(2)}, u32[]{:S(2)}) async-start(bf16[16,48,144]{2,1,0:T(8,128)(2,1)} %bitcast.39), calls=%async_computation.1 | async-start | bytes 786432 | tf_op jit(solution)/shard_map/all_to_all | solution.py:397
  54.5 6.8 %main_attention.3.refs_4_ = bf16[16,144,256]{2,1,0:T(8,128)(2,1)} custom-call(bf16[16,288,256]{2,1,0:T(8,128)(2,1)} %copy-done.2, bf16[16,288,256]{2,1,0:T(8,128)(2,1)} %copy-done.2, bf16[4096,128]{1,0:T(8,128)(2,1)} %get-tuple-element.27.refs_2_, bf16[80,4096]{1,0:T(8,128)(2,1)} %get-tuple-element.28.refs_3_), custom_call_target="tpu_custom_call" | custom-call | flops 4294967296 | bytes 2097152 | tf_op jit(solution)/shard_map/main_attention/pallas_call | solution.py:179
  61.3 1.0 all-to-all-done.1.x_ref
  62.3 2.6 %normed.1 = bf16[16,3,1152]{2,1,0:T(4,128)(2,1)} custom-call(bf16[16,48,144]{2,1,0:T(8,128)(2,1)} %all-to-all-done.1.x_ref, bf16[1152,1152]{1,0:T(8,128)(2,1)S(1)} %copy-done, f32[1,1152]{1,0:T(1,128)} %broadcast_in_dim.80.b_ref, f32[4,1152]{1,0:T(4,128)} %bitcast.40), custom_call_target="tpu_custom_call" | custom-call | tf_op jit(solution)/shard_map/normed/pallas_call | solution.py:400
  64.9 12.5 %all-to-all-start.2 = ((bf16[16,3,1152]{2,1,0:T(4,128)(2,1)}), bf16[16,3,1152]{2,1,0:T(4,128)(2,1)S(1)}, u32[]{:S(2)}, u32[]{:S(2)}) async-start(bf16[16,3,1152]{2,1,0:T(4,128)(2,1)} %normed.1), calls=%async_computation.2 | async-start | bytes 294912 | tf_op jit(solution)/shard_map/all_to_all | solution.py:403
  77.5 6.7 %main_attention.4.refs_4_ = bf16[16,144,256]{2,1,0:T(8,128)(2,1)} custom-call(bf16[16,288,256]{2,1,0:T(8,128)(2,1)} %copy-done.2, bf16[16,288,256]{2,1,0:T(8,128)(2,1)} %copy-done.2, bf16[4096,128]{1,0:T(8,128)(2,1)} %get-tuple-element.27.refs_2_, bf16[80,4096]{1,0:T(8,128)(2,1)} %get-tuple-element.28.refs_3_, ...), custom_call_target="tpu_custom_call", output_to_operand_aliasing={{}: (4, {})} | custom-call | flops 4294967296 | bytes 2097152 | tf_op jit(solution)/shard_map/main_attention/pallas_call | solution.py:179
  84.1 2.6 %all-to-all-done.2.x_ref = bf16[16,3,1152]{2,1,0:T(4,128)(2,1)S(1)} async-done(((bf16[16,3,1152]{2,1,0:T(4,128)(2,1)}), bf16[16,3,1152]{2,1,0:T(4,128)(2,1)S(1)}, u32[]{:S(2)}, u32[]{:S(2)}) %all-to-all-start.2) | async-done | bytes 110624 | tf_op jit(solution)/shard_map/all_to_all | solution.py:403
  86.8 1.0 compact.1
  87.8 4.5 %all-to-all-start.3 = ((bf16[16,16,1152]{2,1,0:T(8,128)(2,1)}), bf16[16,16,1152]{2,1,0:T(8,128)(2,1)S(1)}, u32[]{:S(2)}, u32[]{:S(2)}) async-start(bf16[16,16,1152]{2,1,0:T(8,128)(2,1)} %compact.1), calls=%async_computation.3 | async-start | bytes 1179648 | tf_op jit(solution)/shard_map/all_to_all | solution.py:409
  92.4 10.9 %main_attention.5._ = bf16[16,144,256]{2,1,0:T(8,128)(2,1)} custom-call(bf16[16,288,256]{2,1,0:T(8,128)(2,1)} %copy-done.2, bf16[16,288,256]{2,1,0:T(8,128)(2,1)} %copy-done.2, bf16[4096,128]{1,0:T(8,128)(2,1)} %get-tuple-element.27.refs_2_, bf16[80,4096]{1,0:T(8,128)(2,1)} %get-tuple-element.28.refs_3_, ...), custom_call_target="tpu_custom_call", output_to_operand_aliasing={{}: (4, {})} | custom-call | flops 8589934592 | bytes 2097152 | tf_op jit(solution)/shard_map/main_attention/pallas_call | solution.py:179
  103.2 0.8 all-to-all-done.3
  104.1 3.2 %expert.1 = (bf16[16,144,256]{2,1,0:T(8,128)(2,1)}, f32[8,256]{1,0:T(8,128)}) custom-call(bf16[256,1152]{1,0:T(8,128)(2,1)S(1)} %bitcast.28, f32[1,288]{1,0:T(1,128)S(1)} %copy-done.4, bf16[1,1152]{1,0:T(2,128)(2,1)S(1)} %broadcast_in_dim.79.router_ref, bf16[288,1152]{1,0:T(8,128)(2,1)S(1)} %bitcast.31, ...), custom_call_target="tpu_custom_call", output_to_operand_aliasing={{0}: (5, {})} | custom-call | tf_op jit(solution)/shard_map/expert/pallas_call | solution.py:412
  107.3 6.1 %all-to-all-start.4 = ((bf16[16,144,256]{2,1,0:T(8,128)(2,1)}), bf16[16,144,256]{2,1,0:T(8,128)(2,1)S(1)}, u32[]{:S(2)}, u32[]{:S(2)}) async-start(bf16[16,144,256]{2,1,0:T(8,128)(2,1)} %get-tuple-element.37), calls=%async_computation.4 | async-start | bytes 2359296 | tf_op jit(solution)/shard_map/all_to_all | solution.py:433
  113.4 0.1 reshape_squeeze.3
  113.5 0.1 add_select_fusion
  113.6 0.1 reshape.272.idx_ref
  113.7 0.1 copy.30.rb_ref
  113.8 16.6 %all-to-all-done.4.x_ref.o_ref = bf16[16,144,256]{2,1,0:T(8,128)(2,1)S(1)} async-done(((bf16[16,144,256]{2,1,0:T(8,128)(2,1)}), bf16[16,144,256]{2,1,0:T(8,128)(2,1)S(1)}, u32[]{:S(2)}, u32[]{:S(2)}) %all-to-all-start.4) | async-done | bytes 1179680 | tf_op jit(solution)/shard_map/all_to_all | solution.py:433
  130.4 2.0 %weighted.1 = bf16[768,128]{1,0:T(8,128)(2,1)} custom-call(bf16[16,144,256]{2,1,0:T(8,128)(2,1)S(1)} %all-to-all-done.4.x_ref.o_ref, f32[8,256]{1,0:T(8,128)} %get-tuple-element.39.gate_ref, f32[72,1]{1,0:T(8,128)S(1)} %copy.30.rb_ref, s32[1,768]{1,0:T(1,128)S(1)} %reshape.272.idx_ref), custom_call_target="tpu_custom_call" | custom-call | tf_op jit(solution)/shard_map/weighted/pallas_call | solution.py:434
  132.4 7.3 %all-to-all-start.5 = ((bf16[16,48,128]{2,1,0:T(8,128)(2,1)}), bf16[16,48,128]{2,1,0:T(8,128)(2,1)S(1)}, u32[]{:S(2)}, u32[]{:S(2)}) async-start(bf16[16,48,128]{2,1,0:T(8,128)(2,1)} %bitcast.34), calls=%async_computation.5 | async-start | bytes 393216 | tf_op jit(solution)/shard_map/all_to_all | solution.py:437
  139.8 0.1 fusion.3
  139.8 0.7 reshape.269.idx_ref
  140.5 9.6 %all-to-all-done.5 = bf16[16,48,128]{2,1,0:T(8,128)(2,1)S(1)} async-done(((bf16[16,48,128]{2,1,0:T(8,128)(2,1)}), bf16[16,48,128]{2,1,0:T(8,128)(2,1)S(1)}, u32[]{:S(2)}, u32[]{:S(2)}) %all-to-all-start.5) | async-done | bytes 196640 | tf_op jit(solution)/shard_map/all_to_all | solution.py:437
  150.1 3.5 %scatter.1 = bf16[16,72,256]{2,1,0:T(8,128)(2,1)} custom-call(bf16[768,128]{1,0:T(8,128)(2,1)S(1)} %bitcast.30, s32[1,768]{1,0:T(1,128)} %reshape.269.idx_ref), custom_call_target="tpu_custom_call" | custom-call | tf_op jit(solution)/shard_map/scatter/pallas_call | solution.py:441
  153.6 3.6 %all-to-all-start.6 = ((bf16[16,72,256]{2,1,0:T(8,128)(2,1)}), bf16[16,72,256]{2,1,0:T(8,128)(2,1)S(1)}, u32[]{:S(2)}, u32[]{:S(2)}) async-start(bf16[16,72,256]{2,1,0:T(8,128)(2,1)} %scatter.1), calls=%async_computation.6 | async-start | bytes 1179648 | tf_op jit(solution)/shard_map/all_to_all | solution.py:450
  157.2 3.9 %residual.1.res_ref = bf16[256,1152]{1,0:T(8,128)(2,1)S(1)} custom-call(bf16[16,144,256]{2,1,0:T(8,128)(2,1)} %copy-done.1, bf16[256,1152]{1,0:T(8,128)(2,1)} %bitcast.33, bf16[1152,1152]{1,0:T(8,128)(2,1)} %w_ref.3, f32[1,1152]{1,0:T(1,128)} %broadcast_in_dim.80.b_ref, f32[4,1152]{1,0:T(4,128)} %bitcast.41), custom_call_target="tpu_custom_call" | custom-call | tf_op jit(solution)/shard_map/residual/pallas_call | solution.py:438
  161.1 8.6 %all-to-all-done.6 = bf16[16,72,256]{2,1,0:T(8,128)(2,1)S(1)} async-done(((bf16[16,72,256]{2,1,0:T(8,128)(2,1)}), bf16[16,72,256]{2,1,0:T(8,128)(2,1)S(1)}, u32[]{:S(2)}, u32[]{:S(2)}) %all-to-all-start.6) | async-done | bytes 589856 | tf_op jit(solution)/shard_map/all_to_all | solution.py:450
  169.7 1.9 %final.1 = bf16[256,1152]{1,0:T(8,128)(2,1)} custom-call(bf16[1152,256]{1,0:T(8,128)(2,1)S(1)} %bitcast.29, bf16[256,1152]{1,0:T(8,128)(2,1)S(1)} %residual.1.res_ref, f32[4,1152]{1,0:T(4,128)} %bitcast.42), custom_call_target="tpu_custom_call" | custom-call | tf_op jit(solution)/shard_map/final/pallas_call | solution.py:451
  (37 shorter events, 0.1 us)
Async XLA Ops:
  3.5 7.8 %copy-start.5 = (bf16[1152,16]{0,1:T(8,128)(2,1)S(1)}, bf16[1152,16]{0,1:T(8,128)(2,1)}, u32[]{:S(2)}) copy-start(bf16[1152,16]{0,1:T(8,128)(2,1)} %param.21) | copy-start | bytes 110596
  3.5 7.9 %copy-start.8 = (f32[1152]{0:T(1024)S(1)}, f32[1152]{0:T(1024)}, u32[]{:S(2)}) copy-start(f32[1152]{0:T(1024)} %param.20) | copy-start | bytes 13828
  3.5 8.5 %copy-start.9 = (s32[16,1]{0,1:T(1,128)S(1)}, s32[16,1]{0,1:T(1,128)}, u32[]{:S(2)}) copy-start(s32[16,1]{0,1:T(1,128)} %param.26) | copy-start | bytes 196
  3.5 30.2 %copy-start.6 = (s32[16,1,48]{2,1,0:T(1,128)S(1)}, s32[16,1,48]{2,1,0:T(1,128)}, u32[]{:S(2)}) copy-start(s32[16,1,48]{2,1,0:T(1,128)} %param.27) | copy-start | bytes 9220
  3.5 39.4 %all-to-all-start = ((bf16[16,288,256]{2,1,0:T(8,128)(2,1)}), bf16[16,288,256]{2,1,0:T(8,128)(2,1)S(1)}, u32[]{:S(2)}, u32[]{:S(2)}) async-start(bf16[16,288,256]{2,1,0:T(8,128)(2,1)} %split.1), calls=%async_computation | async-start | bytes 4718592 | tf_op jit(solution)/shard_map/all_to_all | solution.py:348
  32.9 0.5 copy-start.10
  32.9 0.8 copy-start.12
  42.9 7.1 %copy-start.2 = (bf16[16,288,256]{2,1,0:T(8,128)(2,1)}, bf16[16,288,256]{2,1,0:T(8,128)(2,1)S(1)}, u32[]{:S(2)}) copy-start(bf16[16,288,256]{2,1,0:T(8,128)(2,1)S(1)} %all-to-all-done.r_ref.refs_0_.refs_1_) | copy-start | bytes 7077892
  50.1 12.3 %all-to-all-start.1 = ((bf16[16,48,144]{2,1,0:T(8,128)(2,1)}), bf16[16,48,144]{2,1,0:T(8,128)(2,1)}, u32[]{:S(2)}, u32[]{:S(2)}) async-start(bf16[16,48,144]{2,1,0:T(8,128)(2,1)} %bitcast.39), calls=%async_computation.1 | async-start | bytes 786432 | tf_op jit(solution)/shard_map/all_to_all | solution.py:397
  54.5 7.8 %copy-start = (bf16[1152,1152]{1,0:T(8,128)(2,1)S(1)}, bf16[1152,1152]{1,0:T(8,128)(2,1)}, u32[]{:S(2)}) copy-start(bf16[1152,1152]{1,0:T(8,128)(2,1)} %w_ref.3) | copy-start | bytes 7962628
  64.9 21.9 %all-to-all-start.2 = ((bf16[16,3,1152]{2,1,0:T(4,128)(2,1)}), bf16[16,3,1152]{2,1,0:T(4,128)(2,1)S(1)}, u32[]{:S(2)}, u32[]{:S(2)}) async-start(bf16[16,3,1152]{2,1,0:T(4,128)(2,1)} %normed.1), calls=%async_computation.2 | async-start | bytes 294912 | tf_op jit(solution)/shard_map/all_to_all | solution.py:403
  87.8 16.3 %all-to-all-start.3 = ((bf16[16,16,1152]{2,1,0:T(8,128)(2,1)}), bf16[16,16,1152]{2,1,0:T(8,128)(2,1)S(1)}, u32[]{:S(2)}, u32[]{:S(2)}) async-start(bf16[16,16,1152]{2,1,0:T(8,128)(2,1)} %compact.1), calls=%async_computation.3 | async-start | bytes 1179648 | tf_op jit(solution)/shard_map/all_to_all | solution.py:409
  92.3 11.7 %copy-start.3 = (bf16[1,1152,288]{1,2,0:T(8,128)(2,1)S(1)}, bf16[1,1152,288]{1,2,0:T(8,128)(2,1)}, u32[]{:S(2)}) copy-start(bf16[1,1152,288]{1,2,0:T(8,128)(2,1)} %param.22) | copy-start | bytes 1990660
  92.4 11.7 %copy-start.4 = (f32[1,288]{1,0:T(1,128)S(1)}, f32[1,288]{1,0:T(1,128)}, u32[]{:S(2)}) copy-start(f32[1,288]{1,0:T(1,128)} %be_ref.1) | copy-start | bytes 3460
  107.3 6.1 %copy-start.14 = (f32[1,1152]{1,0:T(1,128)S(1)}, f32[1,1152]{1,0:T(1,128)}, u32[]{:S(2)}) copy-start(f32[1,1152]{1,0:T(1,128)} %param.25) | copy-start | bytes 13828
  107.3 6.2 %copy-start.11 = (s32[16]{0:T(128)S(1)}, s32[16]{0:T(128)}, u32[]{:S(2)}) copy-start(s32[16]{0:T(128)} %copy-done.10) | copy-start | bytes 196
  107.3 6.2 %copy-start.13 = (s32[16]{0:T(128)S(1)}, s32[16]{0:T(128)}, u32[]{:S(2)}) copy-start(s32[16]{0:T(128)} %copy-done.12) | copy-start | bytes 196
  107.3 23.1 %all-to-all-start.4 = ((bf16[16,144,256]{2,1,0:T(8,128)(2,1)}), bf16[16,144,256]{2,1,0:T(8,128)(2,1)S(1)}, u32[]{:S(2)}, u32[]{:S(2)}) async-start(bf16[16,144,256]{2,1,0:T(8,128)(2,1)} %get-tuple-element.37), calls=%async_computation.4 | async-start | bytes 2359296 | tf_op jit(solution)/shard_map/all_to_all | solution.py:433
  113.4 26.4 %copy-start.7 = (s32[16,1,48]{2,1,0:T(1,128)S(1)}, s32[16,1,48]{2,1,0:T(1,128)}, u32[]{:S(2)}) copy-start(s32[16,1,48]{2,1,0:T(1,128)} %param.27) | copy-start | bytes 9220
  130.4 23.1 %copy-start.1 = (bf16[16,144,256]{2,1,0:T(8,128)(2,1)}, bf16[16,144,256]{2,1,0:T(8,128)(2,1)S(1)}, u32[]{:S(2)}) copy-start(bf16[16,144,256]{2,1,0:T(8,128)(2,1)S(1)} %all-to-all-done.4.x_ref.o_ref) | copy-start | bytes 3538948
  132.4 17.6 %all-to-all-start.5 = ((bf16[16,48,128]{2,1,0:T(8,128)(2,1)}), bf16[16,48,128]{2,1,0:T(8,128)(2,1)S(1)}, u32[]{:S(2)}, u32[]{:S(2)}) async-start(bf16[16,48,128]{2,1,0:T(8,128)(2,1)} %bitcast.34), calls=%async_computation.5 | async-start | bytes 393216 | tf_op jit(solution)/shard_map/all_to_all | solution.py:437
  153.6 16.1 %all-to-all-start.6 = ((bf16[16,72,256]{2,1,0:T(8,128)(2,1)}), bf16[16,72,256]{2,1,0:T(8,128)(2,1)S(1)}, u32[]{:S(2)}, u32[]{:S(2)}) async-start(bf16[16,72,256]{2,1,0:T(8,128)(2,1)} %scatter.1), calls=%async_computation.6 | async-start | bytes 1179648 | tf_op jit(solution)/shard_map/all_to_all | solution.py:450
